TPU v7x, 512 devices: a whole 4x4x16 slice. The times are simulated.
512 devices in a mesh: uly: 16 (over y, z_hi), blk: 32 (over z_lo, x, core).
Axes of the slice: x: 4, y: 4, z: 16 (z_hi: 4, z_lo: 4; z = z_hi * 4 + z_lo), core: 2. Of those that a mesh axis runs over, the one named last changes fastest.
Arguments:
- queries: bfloat16 [65536, 2048], P(('blk', 'uly')), may hold values from -6 to 6
- key_projection: bfloat16 [65536, 256], P(('blk', 'uly')), may hold values from -6 to 6
- value_projection: bfloat16 [65536, 256], P(('blk', 'uly')), may hold values from -6 to 6
- output_gradient: bfloat16 [65536, 2048], P(('blk', 'uly')), may hold values from -6 to 6
- doc_lengths: int32 [64], replicated, may hold values from 1 to 2048, 65536 in all
Outputs:
- context: bfloat16 [65536, 2048], P(('blk', 'uly'))
- grad_queries: bfloat16 [65536, 2048], P(('blk', 'uly'))
- keys_gradient: bfloat16 [65536, 256], P(('blk', 'uly'))
- values_gradient: bfloat16 [65536, 256], P(('blk', 'uly'))
Inputs may be any that keep to these rules, and one draw needn't show every extreme that they name: `doc_lengths`: the 64 lengths sum to 65536, and the longest is exactly 2048.
All inputs are finite; a program needn't handle non-finite values.
Results may differ from a plain program's by a relative error of at most 0.011.
Values may be sent and summed in bfloat16 or wider, within the bound.
No kernel may reach another device: no remote copies, remote signals or barrier semaphores. Data moves between devices by JAX's collectives and lax.ppermute only.
A program may use at most 64 MiB of HBM per device.

v0:
```python
import math

import jax
import jax.numpy as jnp
from jax import lax
from jax.sharding import PartitionSpec as P

QUERY_HEADS = 16
KEY_VALUE_HEADS = 2
HEAD_SIZE = 128


def from_behind(value, axis, steps):
    count = lax.axis_size(axis)
    first, last = (max(0, -steps), min(count, count - steps))
    return lax.ppermute(value, axis, [(source, source + steps) for source in range(first, last)])


def per_device(queries, key_projection, value_projection, output_gradient, doc_lengths):
    head_regroup = lax.axis_size("uly")
    local_heads = QUERY_HEADS // head_regroup
    group_width = head_regroup // KEY_VALUE_HEADS
    rows_per_part = queries.shape[0]
    span_rows = rows_per_part * head_regroup
    block_rows = min(512, span_rows)
    tile_count = span_rows // block_rows
    logit_scale = 1.0 / math.sqrt(HEAD_SIZE)
    span_start = lax.axis_index("blk") * span_rows
    buffer_anchor = span_start - span_rows
    stacked_keys = key_projection.reshape(rows_per_part, KEY_VALUE_HEADS, 1, HEAD_SIZE)
    stacked_values = value_projection.reshape(rows_per_part, KEY_VALUE_HEADS, 1, HEAD_SIZE)
    replica_count = stacked_keys.shape[2]
    key_send = jnp.repeat(stacked_keys, group_width, axis=1).reshape(
        rows_per_part, head_regroup * replica_count * HEAD_SIZE
    )
    value_send = jnp.repeat(stacked_values, group_width, axis=1).reshape(
        rows_per_part, head_regroup * replica_count * HEAD_SIZE
    )
    query_rows, grad_rows, key_rows, value_rows = (
        lax.all_to_all(queries, "uly", split_axis=1, concat_axis=0, tiled=True),
        lax.all_to_all(output_gradient, "uly", split_axis=1, concat_axis=0, tiled=True),
        lax.all_to_all(key_send, "uly", split_axis=1, concat_axis=0, tiled=True),
        lax.all_to_all(value_send, "uly", split_axis=1, concat_axis=0, tiled=True),
    )
    own_keys, own_values = (key_rows, value_rows)
    earlier_keys, earlier_values = from_behind((key_rows, value_rows), "blk", 1)
    key_buffer = jnp.concatenate([earlier_keys, own_keys], axis=0)
    value_buffer = jnp.concatenate([earlier_values, own_values], axis=0)
    query_heads = query_rows.reshape(span_rows, local_heads, HEAD_SIZE)
    grad_heads = grad_rows.reshape(span_rows, local_heads, HEAD_SIZE)
    doc_ends = jnp.cumsum(doc_lengths)
    doc_starts = doc_ends - doc_lengths
    positions = span_start + jnp.arange(span_rows, dtype=jnp.int32)
    doc_begin = jnp.max(
        jnp.where(doc_starts[None, :] <= positions[:, None], doc_starts[None, :], 0), axis=1
    )

    def key_block(key_index, query_block, query_pos, query_begin):
        start_shift = key_index * block_rows
        keys_here = lax.dynamic_slice_in_dim(key_buffer, start_shift, block_rows, 0)
        values_here = lax.dynamic_slice_in_dim(value_buffer, start_shift, block_rows, 0)
        key_pos = buffer_anchor + start_shift + jnp.arange(block_rows, dtype=jnp.int32)
        allowed = (key_pos[None, :] <= query_pos[:, None]) & (
            key_pos[None, :] >= query_begin[:, None]
        )
        scores = (
            jnp.einsum("qhd,kd->hqk", query_block, keys_here, preferred_element_type=jnp.float32)
            * logit_scale
        )
        return (scores, allowed[None], keys_here, values_here)

    def query_step(tile_index, carried):
        out_buffer, grad_query_buffer, grad_key_buffer, grad_value_buffer = carried
        row_offset = tile_index * block_rows
        query_block = lax.dynamic_slice_in_dim(query_heads, row_offset, block_rows, 0)
        gradient_block = lax.dynamic_slice_in_dim(grad_heads, row_offset, block_rows, 0)
        query_pos = span_start + row_offset + jnp.arange(block_rows, dtype=jnp.int32)
        query_begin = lax.dynamic_slice_in_dim(doc_begin, row_offset, block_rows, 0)
        first_tile = (query_begin[0] - buffer_anchor) // block_rows
        last_tile = tile_count + tile_index + 1

        def stats_step(key_index, running):
            row_top, row_total = running
            scores, allowed, _, _ = key_block(key_index, query_block, query_pos, query_begin)
            masked = jnp.where(allowed, scores, -1e30)
            new_top = jnp.maximum(row_top, jnp.max(masked, axis=2))
            kept = jnp.where(allowed, jnp.exp(masked - new_top[:, :, None]), 0.0)
            return (new_top, row_total * jnp.exp(row_top - new_top) + jnp.sum(kept, axis=2))

        start_top = jnp.full((local_heads, block_rows), -1e30, jnp.float32)
        start_total = jnp.zeros((local_heads, block_rows), jnp.float32)
        row_top, row_total = lax.fori_loop(
            first_tile, last_tile, stats_step, (start_top, start_total)
        )
        log_total = row_top + jnp.log(row_total)

        def output_step(key_index, accum_out):
            scores, allowed, _, values_here = key_block(
                key_index, query_block, query_pos, query_begin
            )
            weight_narrow = jnp.where(allowed, jnp.exp(scores - log_total[:, :, None]), 0.0).astype(
                jnp.bfloat16
            )
            return accum_out + jnp.einsum(
                "hqk,kd->qhd", weight_narrow, values_here, preferred_element_type=jnp.float32
            )

        attended = lax.fori_loop(
            first_tile,
            last_tile,
            output_step,
            jnp.zeros((block_rows, local_heads, HEAD_SIZE), jnp.float32),
        )
        row_delta = jnp.sum(gradient_block.astype(jnp.float32) * attended, axis=2).T

        def gradient_step(key_index, running):
            grad_query_acc, grad_key_all, grad_value_all = running
            scores, allowed, keys_here, values_here = key_block(
                key_index, query_block, query_pos, query_begin
            )
            weights = jnp.where(allowed, jnp.exp(scores - log_total[:, :, None]), 0.0)
            weight_narrow = weights.astype(jnp.bfloat16)
            grad_weights = jnp.einsum(
                "qhd,kd->hqk", gradient_block, values_here, preferred_element_type=jnp.float32
            )
            score_gradient_narrow = (weights * (grad_weights - row_delta[:, :, None])).astype(
                jnp.bfloat16
            )
            grad_query_acc = grad_query_acc + jnp.einsum(
                "hqk,kd->qhd", score_gradient_narrow, keys_here, preferred_element_type=jnp.float32
            )
            key_part = jnp.einsum(
                "hqk,qhd->kd",
                score_gradient_narrow,
                query_block,
                preferred_element_type=jnp.float32,
            )
            value_part = jnp.einsum(
                "hqk,qhd->kd", weight_narrow, gradient_block, preferred_element_type=jnp.float32
            )
            start_shift = key_index * block_rows
            grad_key_all = lax.dynamic_update_slice_in_dim(
                grad_key_all,
                lax.dynamic_slice_in_dim(grad_key_all, start_shift, block_rows, 0) + key_part,
                start_shift,
                0,
            )
            grad_value_all = lax.dynamic_update_slice_in_dim(
                grad_value_all,
                lax.dynamic_slice_in_dim(grad_value_all, start_shift, block_rows, 0) + value_part,
                start_shift,
                0,
            )
            return (grad_query_acc, grad_key_all, grad_value_all)

        start_query = jnp.zeros((block_rows, local_heads, HEAD_SIZE), jnp.float32)
        grad_query_acc, grad_key_buffer, grad_value_buffer = lax.fori_loop(
            first_tile, last_tile, gradient_step, (start_query, grad_key_buffer, grad_value_buffer)
        )
        out_buffer = lax.dynamic_update_slice_in_dim(out_buffer, attended, row_offset, 0)
        grad_query_buffer = lax.dynamic_update_slice_in_dim(
            grad_query_buffer, logit_scale * grad_query_acc, row_offset, 0
        )
        return (out_buffer, grad_query_buffer, grad_key_buffer, grad_value_buffer)

    head_zeros = jnp.zeros((span_rows, local_heads, HEAD_SIZE), jnp.float32)
    key_zeros = jnp.zeros((2 * span_rows, HEAD_SIZE), jnp.float32)
    out_buffer, grad_query_buffer, grad_key_buffer, grad_value_buffer = lax.fori_loop(
        0, tile_count, query_step, (head_zeros, head_zeros, key_zeros, key_zeros)
    )
    grad_key_buffer = grad_key_buffer * logit_scale
    earlier_grad_keys = grad_key_buffer[:span_rows]
    own_grad_keys = grad_key_buffer[span_rows:]
    earlier_grad_values = grad_value_buffer[:span_rows]
    own_grad_values = grad_value_buffer[span_rows:]
    moved_keys, moved_values = from_behind((earlier_grad_keys, earlier_grad_values), "blk", -1)
    key_grad_send = own_grad_keys + moved_keys
    value_grad_send = own_grad_values + moved_values
    returned_keys, returned_values = (
        lax.all_to_all(key_grad_send, "uly", split_axis=0, concat_axis=1, tiled=True),
        lax.all_to_all(value_grad_send, "uly", split_axis=0, concat_axis=1, tiled=True),
    )
    key_totals = jnp.sum(
        returned_keys.reshape(
            rows_per_part, KEY_VALUE_HEADS, group_width, replica_count, HEAD_SIZE
        ),
        axis=2,
    )
    value_totals = jnp.sum(
        returned_values.reshape(
            rows_per_part, KEY_VALUE_HEADS, group_width, replica_count, HEAD_SIZE
        ),
        axis=2,
    )
    keys_gradient = key_totals[:, :, 0].reshape(rows_per_part, KEY_VALUE_HEADS * HEAD_SIZE)
    values_gradient = value_totals[:, :, 0].reshape(rows_per_part, KEY_VALUE_HEADS * HEAD_SIZE)
    out_low = out_buffer.astype(jnp.bfloat16).reshape(span_rows, local_heads * HEAD_SIZE)
    grad_query_low = grad_query_buffer.astype(jnp.bfloat16).reshape(
        span_rows, local_heads * HEAD_SIZE
    )
    context, grad_queries = (
        lax.all_to_all(out_low, "uly", split_axis=0, concat_axis=1, tiled=True),
        lax.all_to_all(grad_query_low, "uly", split_axis=0, concat_axis=1, tiled=True),
    )
    return (
        context,
        grad_queries,
        keys_gradient.astype(jnp.bfloat16),
        values_gradient.astype(jnp.bfloat16),
    )


def solution(mesh):
    in_specs = (
        P(("blk", "uly"), None),
        P(("blk", "uly"), None),
        P(("blk", "uly"), None),
        P(("blk", "uly"), None),
        P(),
    )
    out_specs = (
        P(("blk", "uly"), None),
        P(("blk", "uly"), None),
        P(("blk", "uly"), None),
        P(("blk", "uly"), None),
    )
    return jax.shard_map(
        per_device, mesh=mesh, in_specs=in_specs, out_specs=out_specs, check_vma=False
    )
```

profile of v0, /device:TPU:32, one launch (start us, length us, event | category | flops | bytes accessed | tf_op | source)
XLA Modules:
  0.0 509.3 jit_solution(11933675454413650809)
XLA Ops:
  2.4 16.9 %all-to-all-start.2 = ((bf16[128,16,128]{2,0,1:T(8,128)(2,1)}), bf16[128,16,128]{2,0,1:T(8,128)(2,1)S(1)}, u32[]{:S(2)}, u32[]{:S(2)}) async-start(bf16[128,16,128]{2,0,1:T(8,128)(2,1)} %bitcast.9), calls=%async_computation.2 | async-start | bytes 1048576 | tf_op jit(solution)/shard_map/all_to_all | solution.py:43
  20.2 33.2 %all-to-all-done.2 = bf16[128,16,128]{2,0,1:T(8,128)(2,1)S(1)} async-done(((bf16[128,16,128]{2,0,1:T(8,128)(2,1)}), bf16[128,16,128]{2,0,1:T(8,128)(2,1)S(1)}, u32[]{:S(2)}, u32[]{:S(2)}) %all-to-all-start.2) | async-done | bytes 524320 | tf_op jit(solution)/shard_map/all_to_all | solution.py:43
  58.9 33.3 %all-to-all-done.1 = bf16[128,16,128]{2,0,1:T(8,128)(2,1)S(1)} async-done(((bf16[128,16,128]{2,0,1:T(8,128)(2,1)}), bf16[128,16,128]{2,0,1:T(8,128)(2,1)S(1)}, u32[]{:S(2)}, u32[]{:S(2)}) %all-to-all-start.1) | async-done | bytes 524320 | tf_op jit(solution)/shard_map/all_to_all | solution.py:42
  92.2 3.6 all-to-all-start
  96.8 31.8 %all-to-all-done = bf16[128,16,128]{0,2,1:T(8,128)(2,1)S(1)} async-done(((bf16[128,16,128]{0,2,1:T(8,128)(2,1)}), bf16[128,16,128]{0,2,1:T(8,128)(2,1)S(1)}, u32[]{:S(2)}, u32[]{:S(2)}) %all-to-all-start) | async-done | bytes 524320 | tf_op jit(solution)/shard_map/all_to_all | solution.py:40
  139.2 25.2 %all-to-all-done.3 = bf16[128,16,128]{0,2,1:T(8,128)(2,1)S(1)} async-done(((bf16[128,16,128]{0,2,1:T(8,128)(2,1)}), bf16[128,16,128]{0,2,1:T(8,128)(2,1)S(1)}, u32[]{:S(2)}, u32[]{:S(2)}) %all-to-all-start.3) | async-done | bytes 524320 | tf_op jit(solution)/shard_map/all_to_all | solution.py:41
  171.2 135.3 %while.137 = (s32[]{:T(128)}, bf16[2048,1,128]{0,2,1:T(8,128)(2,1)}, bf16[2048,1,128]{0,2,1:T(8,128)(2,1)}, f32[4096,128]{1,0:T(8,128)}, f32[4096,128]{1,0:T(8,1...) while((s32[]{:T(128)}, bf16[2048,1,128]{0,2,1:T(8,128)(2,1)}, ...), condition=%wide.region_12.13_spmd, body=%wide.region_2.12_spmd.sunk | while | flops 545001472 | bytes 13457978 | solution.py:168
  173.4 6.8 %while.138 = (s32[]{:T(128)}, f32[1,512]{1,0:T(1,128)S(1)}, f32[1,512]{1,0:T(1,128)S(1)}, s32[]{:T(128)}, s32[]{:T(128)}, /*index=5*/s32[512]{0:T(512)S(1)}, bf1...) while((s32[]{:T(128)}, f32[1,512]{1,0:T(1,128)S(1)}, ...), condition=%wide.region_6.6_spmd.clone, body=%wide.region_3.5_spmd.clone.sunk | while | flops 70256648 | bytes 2402499 | solution.py:92
  180.3 6.6 %while.139 = (s32[]{:T(128)}, f32[512,1,128]{0,2,1:T(8,128)S(1)}, s32[]{:T(128)}, bf16[4096,128]{1,0:T(8,128)(2,1)}, s32[]{:T(128)}, /*index=5*/s32[512]{0:T(512...) while((s32[]{:T(128)}, f32[512,1,128]{0,2,1:T(8,128)S(1)}, ...), condition=%wide.region_8.8_spmd.clone, body=%wide.region_7.7_spmd.clone.sunk | while | flops 136119296 | bytes 931015 | solution.py:108
  187.2 24.1 %while.140 = (s32[]{:T(128)}, f32[512,1,128]{0,2,1:T(8,128)S(1)}, f32[4096,128]{1,0:T(8,128)}, f32[4096,128]{1,0:T(8,128)S(1)}, s32[]{:T(128)}, /*index=5*/bf16[...) while((s32[]{:T(128)}, f32[512,1,128]{0,2,1:T(8,128)S(1)}, ...), condition=%wide.region_11.11_spmd.clone, body=%wide.region_10.10_spmd.clone.sunk | while | flops 338363392 | bytes 7223547 | solution.py:157
  214.3 8.5 %while.138 = (s32[]{:T(128)}, f32[1,512]{1,0:T(1,128)S(1)}, f32[1,512]{1,0:T(1,128)S(1)}, s32[]{:T(128)}, s32[]{:T(128)}, /*index=5*/s32[512]{0:T(512)S(1)}, bf1...) while((s32[]{:T(128)}, f32[1,512]{1,0:T(1,128)S(1)}, ...), condition=%wide.region_6.6_spmd.clone, body=%wide.region_3.5_spmd.clone.sunk | while | flops 70256648 | bytes 2402499 | solution.py:92
  222.8 8.2 %while.139 = (s32[]{:T(128)}, f32[512,1,128]{0,2,1:T(8,128)S(1)}, s32[]{:T(128)}, bf16[4096,128]{1,0:T(8,128)(2,1)}, s32[]{:T(128)}, /*index=5*/s32[512]{0:T(512...) while((s32[]{:T(128)}, f32[512,1,128]{0,2,1:T(8,128)S(1)}, ...), condition=%wide.region_8.8_spmd.clone, body=%wide.region_7.7_spmd.clone.sunk | while | flops 136119296 | bytes 931015 | solution.py:108
  231.4 30.1 %while.140 = (s32[]{:T(128)}, f32[512,1,128]{0,2,1:T(8,128)S(1)}, f32[4096,128]{1,0:T(8,128)}, f32[4096,128]{1,0:T(8,128)S(1)}, s32[]{:T(128)}, /*index=5*/bf16[...) while((s32[]{:T(128)}, f32[512,1,128]{0,2,1:T(8,128)S(1)}, ...), condition=%wide.region_11.11_spmd.clone, body=%wide.region_10.10_spmd.clone.sunk | while | flops 338363392 | bytes 7223547 | solution.py:157
  271.5 12.1 %while.140 = (s32[]{:T(128)}, f32[512,1,128]{0,2,1:T(8,128)S(1)}, f32[4096,128]{1,0:T(8,128)}, f32[4096,128]{1,0:T(8,128)S(1)}, s32[]{:T(128)}, /*index=5*/bf16[...) while((s32[]{:T(128)}, f32[512,1,128]{0,2,1:T(8,128)S(1)}, ...), condition=%wide.region_11.11_spmd.clone, body=%wide.region_10.10_spmd.clone.sunk | while | flops 338363392 | bytes 7223547 | solution.py:157
  293.6 12.1 %while.140 = (s32[]{:T(128)}, f32[512,1,128]{0,2,1:T(8,128)S(1)}, f32[4096,128]{1,0:T(8,128)}, f32[4096,128]{1,0:T(8,128)S(1)}, s32[]{:T(128)}, /*index=5*/bf16[...) while((s32[]{:T(128)}, f32[512,1,128]{0,2,1:T(8,128)S(1)}, ...), condition=%wide.region_11.11_spmd.clone, body=%wide.region_10.10_spmd.clone.sunk | while | flops 338363392 | bytes 7223547 | solution.py:157
  308.6 7.7 %all-to-all-start.4 = ((bf16[16,128,128]{2,1,0:T(8,128)(2,1)}), bf16[16,128,128]{2,1,0:T(8,128)(2,1)S(1)}, u32[]{:S(2)}, u32[]{:S(2)}) async-start(bf16[16,128,128]{2,1,0:T(8,128)(2,1)} %bitcast.221), calls=%async_computation.4 | async-start | bytes 1048576 | tf_op jit(solution)/shard_map/all_to_all | solution.py:202
  317.3 29.0 %all-to-all-done.4 = bf16[16,128,128]{2,1,0:T(8,128)(2,1)S(1)} async-done(((bf16[16,128,128]{2,1,0:T(8,128)(2,1)}), bf16[16,128,128]{2,1,0:T(8,128)(2,1)S(1)}, u32[]{:S(2)}, u32[]{:S(2)}) %all-to-all-start.4) | async-done | bytes 524320 | tf_op jit(solution)/shard_map/all_to_all | solution.py:202
  346.3 6.3 %all-to-all-start.5 = ((bf16[16,128,128]{2,1,0:T(8,128)(2,1)}), bf16[16,128,128]{2,1,0:T(8,128)(2,1)S(1)}, u32[]{:S(2)}, u32[]{:S(2)}) async-start(bf16[16,128,128]{2,1,0:T(8,128)(2,1)} %bitcast.220), calls=%async_computation.5 | async-start | bytes 1048576 | tf_op jit(solution)/shard_map/all_to_all | solution.py:203
  354.6 44.6 %collective-permute-done.3 = f32[2048,128]{1,0:T(8,128)S(1)} collective-permute-done((f32[2048,128]{1,0:T(8,128)S(1)}, f32[2048,128]{1,0:T(8,128)S(1)}, u32[]{:S(2)}, u32[]{:S(2)}) %collective-permute-start.3) | collective-permute-done | bytes 1048608 | tf_op jit(solution)/shard_map/ppermute | solution.py:16
  400.3 20.1 %all-to-all-start.7 = ((f32[16,128,128]{2,1,0:T(8,128)}), f32[16,128,128]{2,1,0:T(8,128)S(1)}, u32[]{:S(2)}, u32[]{:S(2)}) async-start(f32[16,128,128]{2,1,0:T(8,128)} %bitcast.25), calls=%async_computation.7 | async-start | bytes 2097152 | tf_op jit(solution)/shard_map/all_to_all | solution.py:181
  422.2 5.8 %collective-permute-start.2 = (f32[2048,128]{1,0:T(8,128)S(1)}, f32[2048,128]{1,0:T(8,128)S(1)}, u32[]{:S(2)}, u32[]{:S(2)}) collective-permute-start(f32[2048,128]{1,0:T(8,128)S(1)} %slice.27), channel_id=1, source_target_pairs={{1,0},{2,1},{3,2},{4,3},{5,4},{6,5},{7,6},{8,7},{9,8},{10,9},{11,1... | collective-permute-start | bytes 3145736 | tf_op jit(solution)/shard_map/ppermute | solution.py:16
  428.0 39.2 %collective-permute-done.2 = f32[2048,128]{1,0:T(8,128)S(1)} collective-permute-done((f32[2048,128]{1,0:T(8,128)S(1)}, f32[2048,128]{1,0:T(8,128)S(1)}, u32[]{:S(2)}, u32[]{:S(2)}) %collective-permute-start.2) | collective-permute-done | bytes 1048608 | tf_op jit(solution)/shard_map/ppermute | solution.py:16
  468.3 14.2 %all-to-all-start.6 = ((f32[16,128,128]{2,1,0:T(8,128)}), f32[16,128,128]{2,1,0:T(8,128)S(1)}, u32[]{:S(2)}, u32[]{:S(2)}) async-start(f32[16,128,128]{2,1,0:T(8,128)} %bitcast.21), calls=%async_computation.6 | async-start | bytes 2097152 | tf_op jit(solution)/shard_map/all_to_all | solution.py:180
  487.8 20.6 %all-to-all-done.6 = f32[16,128,128]{2,1,0:T(8,128)S(1)} async-done(((f32[16,128,128]{2,1,0:T(8,128)}), f32[16,128,128]{2,1,0:T(8,128)S(1)}, u32[]{:S(2)}, u32[]{:S(2)}) %all-to-all-start.6) | async-done | bytes 1048608 | tf_op jit(solution)/shard_map/all_to_all | solution.py:180
  (286 shorter events, 185.6 us)
Async XLA Ops:
  0.6 0.8 copy-start
  0.6 57.3 %copy-start.2 = (bf16[128,2048]{1,0:T(8,128)(2,1)S(1)}, bf16[128,2048]{1,0:T(8,128)(2,1)}, u32[]{:S(2)}) copy-start(bf16[128,2048]{1,0:T(8,128)(2,1)} %param.13) | copy-start | bytes 1572868
  2.4 51.1 %all-to-all-start.2 = ((bf16[128,16,128]{2,0,1:T(8,128)(2,1)}), bf16[128,16,128]{2,0,1:T(8,128)(2,1)S(1)}, u32[]{:S(2)}, u32[]{:S(2)}) async-start(bf16[128,16,128]{2,0,1:T(8,128)(2,1)} %bitcast.9), calls=%async_computation.2 | async-start | bytes 1048576 | tf_op jit(solution)/shard_map/all_to_all | solution.py:43
  19.3 76.5 %copy-start.3 = (bf16[128,2048]{1,0:T(8,128)(2,1)S(1)}, bf16[128,2048]{1,0:T(8,128)(2,1)}, u32[]{:S(2)}) copy-start(bf16[128,2048]{1,0:T(8,128)(2,1)} %param.16) | copy-start | bytes 1572868
  54.3 37.9 %all-to-all-start.1 = ((bf16[128,16,128]{2,0,1:T(8,128)(2,1)}), bf16[128,16,128]{2,0,1:T(8,128)(2,1)S(1)}, u32[]{:S(2)}, u32[]{:S(2)}) async-start(bf16[128,16,128]{2,0,1:T(8,128)(2,1)} %bitcast.6), calls=%async_computation.1 | async-start | bytes 1048576 | tf_op jit(solution)/shard_map/all_to_all | solution.py:42
  57.9 76.2 %copy-start.4 = (s32[64]{0:T(128)S(1)}, s32[64]{0:T(128)}, u32[]{:S(2)}) copy-start(s32[64]{0:T(128)} %param.17) | copy-start | bytes 772
  92.2 36.4 %all-to-all-start = ((bf16[128,16,128]{0,2,1:T(8,128)(2,1)}), bf16[128,16,128]{0,2,1:T(8,128)(2,1)S(1)}, u32[]{:S(2)}, u32[]{:S(2)}) async-start(bf16[128,16,128]{0,2,1:T(8,128)(2,1)} %bitcast.3), calls=%async_computation | async-start | bytes 1048576 | tf_op jit(solution)/shard_map/all_to_all | solution.py:40
  128.6 35.8 %all-to-all-start.3 = ((bf16[128,16,128]{0,2,1:T(8,128)(2,1)}), bf16[128,16,128]{0,2,1:T(8,128)(2,1)S(1)}, u32[]{:S(2)}, u32[]{:S(2)}) async-start(bf16[128,16,128]{0,2,1:T(8,128)(2,1)} %bitcast.12), calls=%async_computation.3 | async-start | bytes 1048576 | tf_op jit(solution)/shard_map/all_to_all | solution.py:41
  132.2 32.5 %collective-permute-start = (bf16[2048,128]{1,0:T(8,128)(2,1)S(1)}, bf16[2048,128]{1,0:T(8,128)(2,1)S(1)}, u32[]{:S(2)}, u32[]{:S(2)}) collective-permute-start(bf16[2048,128]{1,0:T(8,128)(2,1)S(1)} %bitcast.226), channel_id=1, source_target_pairs={{0,1},{1,2},{2,3},{3,4},{4,5},{5,6},{6,7},{7,8},{8,9},{9,10},{10,1... | collective-permute-start | bytes 1572872 | tf_op jit(solution)/shard_map/ppermute | solution.py:16
  134.5 31.3 %collective-permute-start.1 = (bf16[2048,128]{1,0:T(8,128)(2,1)S(1)}, bf16[2048,128]{1,0:T(8,128)(2,1)}, u32[]{:S(2)}, u32[]{:S(2)}) collective-permute-start(bf16[2048,128]{1,0:T(8,128)(2,1)S(1)} %bitcast.224), channel_id=1, source_target_pairs={{0,1},{1,2},{2,3},{3,4},{4,5},{5,6},{6,7},{7,8},{8,9},{9,10},{10,1... | collective-permute-start | bytes 1572872 | tf_op jit(solution)/shard_map/ppermute | solution.py:16
  306.5 9.9 %copy-start.1 = (bf16[2048,1,128]{0,2,1:T(8,128)(2,1)S(1)}, bf16[2048,1,128]{0,2,1:T(8,128)(2,1)}, u32[]{:S(2)}) copy-start(bf16[2048,1,128]{0,2,1:T(8,128)(2,1)} %get-tuple-element.483) | copy-start | bytes 1572868
  308.6 37.7 %all-to-all-start.4 = ((bf16[16,128,128]{2,1,0:T(8,128)(2,1)}), bf16[16,128,128]{2,1,0:T(8,128)(2,1)S(1)}, u32[]{:S(2)}, u32[]{:S(2)}) async-start(bf16[16,128,128]{2,1,0:T(8,128)(2,1)} %bitcast.221), calls=%async_computation.4 | async-start | bytes 1048576 | tf_op jit(solution)/shard_map/all_to_all | solution.py:202
  346.3 54.0 %all-to-all-start.5 = ((bf16[16,128,128]{2,1,0:T(8,128)(2,1)}), bf16[16,128,128]{2,1,0:T(8,128)(2,1)S(1)}, u32[]{:S(2)}, u32[]{:S(2)}) async-start(bf16[16,128,128]{2,1,0:T(8,128)(2,1)} %bitcast.220), calls=%async_computation.5 | async-start | bytes 1048576 | tf_op jit(solution)/shard_map/all_to_all | solution.py:203
  352.7 46.5 %collective-permute-start.3 = (f32[2048,128]{1,0:T(8,128)S(1)}, f32[2048,128]{1,0:T(8,128)S(1)}, u32[]{:S(2)}, u32[]{:S(2)}) collective-permute-start(f32[2048,128]{1,0:T(8,128)S(1)} %slice.25), channel_id=1, source_target_pairs={{1,0},{2,1},{3,2},{4,3},{5,4},{6,5},{7,6},{8,7},{9,8},{10,9},{11,1... | collective-permute-start | bytes 3145736 | tf_op jit(solution)/shard_map/ppermute | solution.py:16
  400.3 68.0 %all-to-all-start.7 = ((f32[16,128,128]{2,1,0:T(8,128)}), f32[16,128,128]{2,1,0:T(8,128)S(1)}, u32[]{:S(2)}, u32[]{:S(2)}) async-start(f32[16,128,128]{2,1,0:T(8,128)} %bitcast.25), calls=%async_computation.7 | async-start | bytes 2097152 | tf_op jit(solution)/shard_map/all_to_all | solution.py:181
  422.2 45.0 %collective-permute-start.2 = (f32[2048,128]{1,0:T(8,128)S(1)}, f32[2048,128]{1,0:T(8,128)S(1)}, u32[]{:S(2)}, u32[]{:S(2)}) collective-permute-start(f32[2048,128]{1,0:T(8,128)S(1)} %slice.27), channel_id=1, source_target_pairs={{1,0},{2,1},{3,2},{4,3},{5,4},{6,5},{7,6},{8,7},{9,8},{10,9},{11,1... | collective-permute-start | bytes 3145736 | tf_op jit(solution)/shard_map/ppermute | solution.py:16
  468.3 40.1 %all-to-all-start.6 = ((f32[16,128,128]{2,1,0:T(8,128)}), f32[16,128,128]{2,1,0:T(8,128)S(1)}, u32[]{:S(2)}, u32[]{:S(2)}) async-start(f32[16,128,128]{2,1,0:T(8,128)} %bitcast.21), calls=%async_computation.6 | async-start | bytes 2097152 | tf_op jit(solution)/shard_map/all_to_all | solution.py:180
where the time goes:
time: 512 us; the launch traced here: 509 us
  waiting for transfers between devices  257 us (50%)
  matrix products  115 us (22%)
  starting transfers between devices  89.1 us (17%)
  local copies, waits for them, and re-layouts  26.5 us (5%)
  other arithmetic  15.8 us (3%)
    ppermute x4, waiting for transfers between devices, from_behind(): lax.ppermute(value, axis, [(source, source + steps) for source in range(f...  83.7 us
    dot_general x26, matrix products, key_block(): jnp.einsum('qhd,kd->hqk', query_block, keys_here, preferred_element_type=...  34.3 us
    all_to_all x1, waiting for transfers between devices, per_device(): lax.all_to_all(key_send, 'uly', split_axis=1, concat_axis=0, tiled=True)  33.3 us
    all_to_all x1, waiting for transfers between devices, per_device(): lax.all_to_all(value_send, 'uly', split_axis=1, concat_axis=0, tiled=True)  33.2 us
    all_to_all x1, waiting for transfers between devices, per_device(): lax.all_to_all(queries, 'uly', split_axis=1, concat_axis=0, tiled=True)  31.8 us
    all_to_all x1, waiting for transfers between devices, per_device(): lax.all_to_all(out_low, 'uly', split_axis=0, concat_axis=1, tiled=True)  29 us
    dot_general x13, matrix products, gradient_step(): jnp.einsum('hqk,qhd->kd', score_gradient_narrow, query_block, preferred_e...  25.4 us
    all_to_all x1, waiting for transfers between devices, per_device(): lax.all_to_all(output_gradient, 'uly', split_axis=1, concat_axis=0, tiled...  25.2 us
  transfers between devices with their start and end apart: 12, of which 8 were waited for; matrix products, arithmetic and copies ran while one was open for 3% of the time, Pallas kernels for 0%

commit v1 on v0

v1 whole, which is shorter than its diff:
```python
import math

import jax
import jax.numpy as jnp
import numpy as np
from jax import lax
from jax.experimental import pallas as pl
from jax.experimental.pallas import tpu as pltpu
from jax.sharding import Mesh
from jax.sharding import PartitionSpec as P

HEAD_SIZE = 128
SPAN = 2048
CHUNK = 128
TILE = 256
TILES = 2 * SPAN // TILE
OWN = SPAN // TILE
HEADS = 4
ROWS = HEADS * CHUNK
BLOCK_AXES = ("z_lo", "x", "core")
TOKEN_AXES = ("z_lo", "x", "core", "y", "z_hi")
SCALE = 1.0 / math.sqrt(HEAD_SIZE)
LOG2_SCALE = SCALE * math.log2(math.e)


def attention_kernel(
    scalars, begin_ref, qd_ref, kv_before_ref, kv_own_ref,
    out_ref, grad_before_ref, grad_own_ref,
    keys, values, keys_t, values_t, probs, grad_keys, grad_values, out_t, grad_query_t, top, total,
):
    first = scalars[0]
    z_hi = scalars[4]

    def load(source, shift):
        def body(tile, _):
            both = source[tile - shift]
            k, v = both[:, :HEAD_SIZE], both[:, HEAD_SIZE:]
            keys[tile] = k
            values[tile] = v
            keys_t[tile] = k.T
            values_t[tile] = v.T
            return 0

        return body

    lax.fori_loop(first, OWN, load(kv_before_ref, 0), 0)
    lax.fori_loop(jnp.maximum(first, OWN), TILES, load(kv_own_ref, OWN), 0)

    def clear(tile, _):
        grad_keys[tile] = jnp.zeros((TILE, HEAD_SIZE), jnp.float32)
        grad_values[tile] = jnp.zeros((TILE, HEAD_SIZE), jnp.float32)
        return 0

    lax.fori_loop(0, TILES, clear, 0)

    def chunk_step(chunk, _):
        start = SPAN + (4 * chunk + z_hi) * CHUNK
        low = scalars[chunk]
        high = (start + CHUNK - 1) // TILE + 1
        block = qd_ref[chunk]
        rows_q = jnp.concatenate(
            [block[:CHUNK, h * HEAD_SIZE : (h + 1) * HEAD_SIZE] for h in range(HEADS)], axis=0
        )
        rows_d = jnp.concatenate(
            [block[CHUNK:, h * HEAD_SIZE : (h + 1) * HEAD_SIZE] for h in range(HEADS)], axis=0
        )
        query_pos = start + (lax.broadcasted_iota(jnp.int32, (1, ROWS), 1) & (CHUNK - 1))
        begin = begin_ref[chunk]
        top[...] = jnp.full((8, ROWS), -1e30, jnp.float32)
        total[...] = jnp.zeros((8, ROWS), jnp.float32)
        out_t[...] = jnp.zeros((HEAD_SIZE, ROWS), jnp.float32)
        grad_query_t[...] = jnp.zeros((HEAD_SIZE, ROWS), jnp.float32)

        def scores_step(tile, _):
            s = lax.dot_general(
                keys[tile], rows_q, (((1,), (1,)), ((), ())), preferred_element_type=jnp.float32
            )
            key_pos = tile * TILE + lax.broadcasted_iota(jnp.int32, (TILE, ROWS), 0)
            allowed = (key_pos >= begin) & (key_pos <= query_pos)
            s = jnp.where(allowed, s * LOG2_SCALE, -1e30)
            probs[tile] = s
            top[...] = jnp.maximum(top[...], jnp.max(s.reshape(TILE // 8, 8, ROWS), axis=0))
            return 0

        lax.fori_loop(low, high, scores_step, 0)
        row_top = jnp.max(top[...], axis=0, keepdims=True)

        def output_step(tile, _):
            p = jnp.exp2(probs[tile] - row_top)
            probs[tile] = p
            total[...] += jnp.sum(p.reshape(TILE // 8, 8, ROWS), axis=0)
            out_t[...] += lax.dot_general(
                values_t[tile], p.astype(jnp.bfloat16), (((1,), (0,)), ((), ())),
                preferred_element_type=jnp.float32,
            )
            return 0

        lax.fori_loop(low, high, output_step, 0)
        inverse = 1.0 / jnp.sum(total[...], axis=0, keepdims=True)
        attended = out_t[...] * inverse
        context = attended.T
        delta = jnp.sum(rows_d.astype(jnp.float32).T * attended, axis=0, keepdims=True)

        def gradient_step(tile, _):
            w = probs[tile] * inverse
            grad_weights = lax.dot_general(
                values[tile], rows_d, (((1,), (1,)), ((), ())), preferred_element_type=jnp.float32
            )
            grad_scores = (w * (grad_weights - delta)).astype(jnp.bfloat16)
            grad_values[tile] += lax.dot_general(
                w.astype(jnp.bfloat16), rows_d, (((1,), (0,)), ((), ())),
                preferred_element_type=jnp.float32,
            )
            grad_keys[tile] += lax.dot_general(
                grad_scores, rows_q, (((1,), (0,)), ((), ())), preferred_element_type=jnp.float32
            )
            grad_query_t[...] += lax.dot_general(
                keys_t[tile], grad_scores, (((1,), (0,)), ((), ())),
                preferred_element_type=jnp.float32,
            )
            return 0

        lax.fori_loop(low, high, gradient_step, 0)
        grad_query = (grad_query_t[...] * SCALE).T
        for h in range(HEADS):
            span = slice(h * HEAD_SIZE, (h + 1) * HEAD_SIZE)
            out_ref[chunk, :CHUNK, span] = context[h * CHUNK : (h + 1) * CHUNK].astype(jnp.bfloat16)
            out_ref[chunk, CHUNK:, span] = grad_query[h * CHUNK : (h + 1) * CHUNK].astype(jnp.bfloat16)
        return 0

    lax.fori_loop(0, 4, chunk_step, 0)

    def store(target, shift):
        def body(tile, _):
            target[tile - shift, :, :HEAD_SIZE] = (grad_keys[tile] * SCALE).astype(jnp.bfloat16)
            target[tile - shift, :, HEAD_SIZE:] = grad_values[tile].astype(jnp.bfloat16)
            return 0

        return body

    lax.fori_loop(0, OWN, store(grad_before_ref, 0), 0)
    lax.fori_loop(OWN, TILES, store(grad_own_ref, OWN), 0)


def attention(scalars, begin, qd, kv_before, kv_own):
    vmem = pl.BlockSpec(memory_space=pltpu.VMEM)
    tiles = jax.ShapeDtypeStruct((OWN, TILE, 2 * HEAD_SIZE), jnp.bfloat16)
    f32, bf16 = jnp.float32, jnp.bfloat16
    return pl.pallas_call(
        attention_kernel,
        out_shape=(jax.ShapeDtypeStruct((4, 2 * CHUNK, ROWS), bf16), tiles, tiles),
        in_specs=[pl.BlockSpec(memory_space=pltpu.SMEM)] + [vmem] * 4,
        out_specs=(vmem, vmem, vmem),
        scratch_shapes=[
            pltpu.VMEM((TILES, TILE, HEAD_SIZE), bf16),
            pltpu.VMEM((TILES, TILE, HEAD_SIZE), bf16),
            pltpu.VMEM((TILES, HEAD_SIZE, TILE), bf16),
            pltpu.VMEM((TILES, HEAD_SIZE, TILE), bf16),
            pltpu.VMEM((TILES, TILE, ROWS), f32),
            pltpu.VMEM((TILES, TILE, HEAD_SIZE), f32),
            pltpu.VMEM((TILES, TILE, HEAD_SIZE), f32),
            pltpu.VMEM((HEAD_SIZE, ROWS), f32),
            pltpu.VMEM((HEAD_SIZE, ROWS), f32),
            pltpu.VMEM((8, ROWS), f32),
            pltpu.VMEM((8, ROWS), f32),
        ],
        compiler_params=pltpu.CompilerParams(vmem_limit_bytes=48 << 20),
        cost_estimate=pl.CostEstimate(
            flops=4 * 10**9, bytes_accessed=6 << 20, transcendentals=3 * 10**6
        ),
        name="attention",
    )(scalars, begin, qd, kv_before, kv_own)


def per_device(queries, key_projection, value_projection, output_gradient, doc_lengths):
    z_hi = lax.axis_index("z_hi").astype(jnp.int32)
    block = lax.axis_index(BLOCK_AXES).astype(jnp.int32)
    anchor = (block - 1) * SPAN
    qd = lax.all_to_all(
        jnp.concatenate([queries, output_gradient], axis=0), "y", split_axis=1, concat_axis=0, tiled=True
    ).reshape(4, 2 * CHUNK, ROWS)
    kv = jnp.concatenate(
        [
            key_projection[:, :HEAD_SIZE], value_projection[:, :HEAD_SIZE],
            key_projection[:, HEAD_SIZE:], value_projection[:, HEAD_SIZE:],
        ],
        axis=1,
    )
    kv = lax.all_gather(kv, "z_hi", axis=0, tiled=True)
    first, second = kv[:, : 2 * HEAD_SIZE], kv[:, 2 * HEAD_SIZE :]
    kv_own = lax.all_to_all(
        jnp.stack([first, first, second, second]), "y", split_axis=0, concat_axis=0, tiled=True
    )
    blocks = lax.axis_size(BLOCK_AXES)
    kv_before = lax.ppermute(kv_own, BLOCK_AXES, [(i, i + 1) for i in range(blocks - 1)])
    docs = doc_lengths.shape[0]
    order = jnp.arange(docs)
    starts = jnp.sum(jnp.where(order[None, :] < order[:, None], doc_lengths[None, :], 0), axis=1)
    chunk_start = (4 * jnp.arange(4, dtype=jnp.int32) + z_hi) * CHUNK + anchor + SPAN
    position = (chunk_start[:, None] + jnp.arange(CHUNK, dtype=jnp.int32)[None, :])[..., None]
    begin = jnp.max(jnp.where(starts <= position, starts, 0), axis=2).astype(jnp.int32) - anchor
    scalars = jnp.concatenate([begin[:, 0] // TILE, z_hi[None]])
    begin = jnp.tile(begin, (1, HEADS)).reshape(4, 1, ROWS)

    shape = (OWN, TILE, 2 * HEAD_SIZE)
    out, grad_before, grad_own = attention(
        scalars, begin, qd, kv_before.reshape(shape), kv_own.reshape(shape)
    )
    returned = lax.ppermute(grad_before, BLOCK_AXES, [(i + 1, i) for i in range(blocks - 1)])
    grad_own = (grad_own.astype(jnp.float32) + returned.astype(jnp.float32)).astype(jnp.bfloat16)
    grad = lax.all_to_all(
        grad_own.reshape(4, 4, CHUNK, 2 * HEAD_SIZE), "y", split_axis=0, concat_axis=0, tiled=True
    ).astype(jnp.float32)
    grad = jnp.stack([grad[0] + grad[1], grad[2] + grad[3]], axis=1).astype(jnp.bfloat16)
    grad = lax.all_to_all(grad, "z_hi", split_axis=0, concat_axis=0, tiled=True)
    grad = jnp.sum(grad.astype(jnp.float32), axis=0).astype(jnp.bfloat16)
    keys_gradient = jnp.concatenate([grad[0, :, :HEAD_SIZE], grad[1, :, :HEAD_SIZE]], axis=1)
    values_gradient = jnp.concatenate([grad[0, :, HEAD_SIZE:], grad[1, :, HEAD_SIZE:]], axis=1)
    out = lax.all_to_all(
        out.reshape(4 * 2 * CHUNK, ROWS), "y", split_axis=0, concat_axis=1, tiled=True
    )
    return out[:CHUNK], out[CHUNK:], keys_gradient, values_gradient


def solution(mesh):
    order = [mesh.axis_names.index(name) for name in ("uly", "blk")]
    devices = np.transpose(mesh.devices, order).reshape(4, 4, 4, 4, 2)
    fine = Mesh(devices, ("y", "z_hi", "z_lo", "x", "core"))
    rows = P(TOKEN_AXES, None)
    return jax.shard_map(
        per_device, mesh=fine, in_specs=(rows, rows, rows, rows, P()),
        out_specs=(rows, rows, rows, rows), check_vma=False,
    )
```

time: 512 us -> 183 us (0.36)
  the two profiles are of different devices: /device:TPU:32 before, /device:TPU:6 now
where the time goes in v1:
time: 183 us; the launch traced here: 182 us
  waiting for transfers between devices  75.2 us (41%)
  blocking collectives  53.3 us (29%)
  starting transfers between devices  22.8 us (12%)
  Pallas kernels  19.6 us (11%)
  local copies, waits for them, and re-layouts  5.52 us (3%)
  other arithmetic  4.49 us (2%)
    all_gather x1, blocking collectives, per_device(): kv = lax.all_gather(kv, 'z_hi', axis=0, tiled=True)  32.8 us
    all_to_all x1, waiting for transfers between devices, per_device(): grad = lax.all_to_all(grad, 'z_hi', split_axis=0, concat_axis=0, tiled=True)  24 us
    all_to_all x1, blocking collectives, per_device(): lax.all_to_all(grad_own.reshape(4, 4, CHUNK, 2 * HEAD_SIZE), 'y', split_a...  20.5 us
    pallas_call x1, Pallas kernels, attention(): pl.pallas_call(attention_kernel, out_shape=(jax.ShapeDtypeStruct((4, 2 *...  19.6 us
    all_to_all x1, waiting for transfers between devices, per_device(): lax.all_to_all(out.reshape(4 * 2 * CHUNK, ROWS), 'y', split_axis=0, conca...  14.7 us
    ppermute x1, waiting for transfers between devices, per_device(): lax.ppermute(grad_before, BLOCK_AXES, [(i + 1, i) for i in range(blocks -...  12.3 us
    all_to_all x1, waiting for transfers between devices, per_device(): lax.all_to_all(jnp.stack([first, first, second, second]), 'y', split_axis...  10.5 us
    all_to_all x1, waiting for transfers between devices, per_device(): lax.all_to_all(jnp.concatenate([queries, output_gradient], axis=0), 'y',...  9.08 us
  transfers between devices with their start and end apart: 6, of which 6 were waited for; matrix products, arithmetic and copies ran while one was open for 3% of the time, Pallas kernels for 0%

profile of v1, /device:TPU:6, one launch (start us, length us, event | category | flops | bytes accessed | tf_op | source)
XLA Modules:
  0.0 181.8 jit_solution(9367110280046796738)
XLA Ops:
  0.6 0.8 fusion.5
  1.5 32.8 %all_gather.3 = bf16[512,512]{1,0:T(8,128)(2,1)S(1)} all-gather(bf16[128,512]{1,0:T(8,128)(2,1)S(1)} %pad_maximum_fusion.3), channel_id=1, replica_groups=mesh['y'=4,'z_hi'=4,'z_lo'=4,'x'=4,'core'=2] {'z_hi'}, dimensions={0}, use_global_device_ids=true | all-gather | bytes 655360 | tf_op jit(solution)/shard_map/all_gather | solution.py:189
  34.3 1.1 pad_maximum_fusion.1
  35.5 4.5 %all-to-all-start.1 = ((bf16[4,512,256]{2,1,0:T(8,128)(2,1)}), bf16[4,512,256]{2,1,0:T(8,128)(2,1)S(1)}, u32[]{:S(2)}, u32[]{:S(2)}) async-start(bf16[4,512,256]{2,1,0:T(8,128)(2,1)} %pad_maximum_fusion.1), calls=%async_computation.1 | async-start | bytes 2097152 | tf_op jit(solution)/shard_map/all_to_all | solution.py:191
  40.6 1.3 copy.37
  42.1 10.5 %all-to-all-done.1 = bf16[4,512,256]{2,1,0:T(8,128)(2,1)S(1)} async-done(((bf16[4,512,256]{2,1,0:T(8,128)(2,1)}), bf16[4,512,256]{2,1,0:T(8,128)(2,1)S(1)}, u32[]{:S(2)}, u32[]{:S(2)}) %all-to-all-start.1) | async-done | bytes 1048608 | tf_op jit(solution)/shard_map/all_to_all | solution.py:191
  52.6 3.5 %all-to-all-start = ((bf16[256,4,512]{2,0,1:T(8,128)(2,1)}), bf16[256,4,512]{2,0,1:T(8,128)(2,1)S(1)}, u32[]{:S(2)}, u32[]{:S(2)}) async-start(bf16[256,4,512]{2,0,1:T(8,128)(2,1)} %copy.37), calls=%async_computation | async-start | bytes 2097152 | tf_op jit(solution)/shard_map/all_to_all | solution.py:179
  56.1 1.9 %collective-permute-start = (bf16[4,512,256]{2,1,0:T(8,128)(2,1)S(1)}, bf16[4,512,256]{2,1,0:T(8,128)(2,1)S(1)}, u32[]{:S(2)}, u32[]{:S(2)}) collective-permute-start(bf16[4,512,256]{2,1,0:T(8,128)(2,1)S(1)} %all-to-all-done.1), channel_id=1, source_target_pairs={{0,1},{1,2},{2,3},{3,4},{4,5},{5,6},{6,7},{7,8},{8,9},{9,10},{10,1... | collective-permute-start | bytes 3145736 | tf_op jit(solution)/shard_map/ppermute | solution.py:195
  58.5 9.1 %all-to-all-done = bf16[256,4,512]{2,0,1:T(8,128)(2,1)S(1)} async-done(((bf16[256,4,512]{2,0,1:T(8,128)(2,1)}), bf16[256,4,512]{2,0,1:T(8,128)(2,1)S(1)}, u32[]{:S(2)}, u32[]{:S(2)}) %all-to-all-start) | async-done | bytes 1048608 | tf_op jit(solution)/shard_map/all_to_all | solution.py:179
  67.6 4.7 %collective-permute-done = bf16[4,512,256]{2,1,0:T(8,128)(2,1)S(1)} collective-permute-done((bf16[4,512,256]{2,1,0:T(8,128)(2,1)S(1)}, bf16[4,512,256]{2,1,0:T(8,128)(2,1)S(1)}, u32[]{:S(2)}, u32[]{:S(2)}) %collective-permute-start) | collective-permute-done | bytes 1048608 | tf_op jit(solution)/shard_map/ppermute | solution.py:195
  72.3 19.6 %attention.1 = (bf16[4,256,512]{2,1,0:T(8,128)(2,1)}, bf16[8,256,256]{2,1,0:T(8,128)(2,1)S(1)}, bf16[8,256,256]{2,1,0:T(8,128)(2,1)S(1)}) custom-call(s32[5]{0:T(128)S(1)} %pad_add_fusion.scalars, s32[4,1,512]{2,1,0:T(1,128)S(1)} %bitcast.29, bf16[4,256,512]{2,1,0:T(8,128)(2,1)S(1)} %bitcast.28, bf16[8,256,256]{2,1,0:T(8,128)(2,1)S(1)} %bitcast.30, ...), custom_call_target="tpu_custom_call" | custom-call | flops 4000000000 | bytes 6291456 | tf_op jit(solution)/shard_map/attention/pallas_call | solution.py:149
  91.9 5.9 %collective-permute-start.1 = (bf16[8,256,256]{2,1,0:T(8,128)(2,1)S(1)}, bf16[8,256,256]{2,1,0:T(8,128)(2,1)S(1)}, u32[]{:S(2)}, u32[]{:S(2)}) collective-permute-start(bf16[8,256,256]{2,1,0:T(8,128)(2,1)S(1)} %get-tuple-element.9), channel_id=1, source_target_pairs={{1,0},{2,1},{3,2},{4,3},{5,4},{6,5},{7,6},{8,7},{9,8},{10,9},{11,1... | collective-permute-start | bytes 3145736 | tf_op jit(solution)/shard_map/ppermute | solution.py:209
  97.8 12.3 %collective-permute-done.1 = bf16[8,256,256]{2,1,0:T(8,128)(2,1)S(1)} collective-permute-done((bf16[8,256,256]{2,1,0:T(8,128)(2,1)S(1)}, bf16[8,256,256]{2,1,0:T(8,128)(2,1)S(1)}, u32[]{:S(2)}, u32[]{:S(2)}) %collective-permute-start.1) | collective-permute-done | bytes 1048608 | tf_op jit(solution)/shard_map/ppermute | solution.py:209
  110.1 0.3 add_convert_fusion
  110.4 20.5 %all_to_all.44 = bf16[4,4,128,256]{3,2,1,0:T(8,128)(2,1)S(1)} all-to-all(bf16[4,4,128,256]{3,2,1,0:T(8,128)(2,1)S(1)} %bitcast.31), channel_id=1, replica_groups=mesh['y'=4,'z_hi'=4,'z_lo'=4,'x'=4,'core'=2] {'y'}, dimensions={0} | all-to-all | bytes 2097152 | tf_op jit(solution)/shard_map/all_to_all | solution.py:211
  130.9 3.5 %all-to-all-start.2 = ((bf16[4,256,512]{2,1,0:T(8,128)(2,1)}), bf16[4,256,512]{2,1,0:T(8,128)(2,1)S(1)}, u32[]{:S(2)}, u32[]{:S(2)}) async-start(bf16[4,256,512]{2,1,0:T(8,128)(2,1)} %get-tuple-element.7), calls=%async_computation.2 | async-start | bytes 2097152 | tf_op jit(solution)/shard_map/all_to_all | solution.py:219
  134.8 0.9 pad_maximum_fusion.2
  135.6 14.7 %all-to-all-done.2 = bf16[4,256,512]{2,1,0:T(8,128)(2,1)S(1)} async-done(((bf16[4,256,512]{2,1,0:T(8,128)(2,1)}), bf16[4,256,512]{2,1,0:T(8,128)(2,1)S(1)}, u32[]{:S(2)}, u32[]{:S(2)}) %all-to-all-start.2) | async-done | bytes 1048608 | tf_op jit(solution)/shard_map/all_to_all | solution.py:219
  150.3 3.5 %all-to-all-start.4 = ((bf16[4,2,128,256]{3,2,1,0:T(8,128)(2,1)}), bf16[4,2,128,256]{3,2,1,0:T(8,128)(2,1)S(1)}, u32[]{:S(2)}, u32[]{:S(2)}) async-start(bf16[4,2,128,256]{3,2,1,0:T(8,128)(2,1)} %pad_maximum_fusion.2), calls=%async_computation.4 | async-start | bytes 1048576 | tf_op jit(solution)/shard_map/all_to_all | solution.py:215
  154.1 1.0 copy.42
  155.4 1.0 copy.41
  156.4 24.0 %all-to-all-done.4 = bf16[4,2,128,256]{3,2,1,0:T(8,128)(2,1)S(1)} async-done(((bf16[4,2,128,256]{3,2,1,0:T(8,128)(2,1)}), bf16[4,2,128,256]{3,2,1,0:T(8,128)(2,1)S(1)}, u32[]{:S(2)}, u32[]{:S(2)}) %all-to-all-start.4) | async-done | bytes 524320 | tf_op jit(solution)/shard_map/all_to_all | solution.py:215
  180.5 0.6 pad_maximum_fusion.5
  181.1 0.6 pad_maximum_fusion.4
  (29 shorter events, 2.3 us)
Async XLA Ops:
  34.3 5.6 %copy-start.1 = (bf16[128,2048]{1,0:T(8,128)(2,1)S(1)}, bf16[128,2048]{1,0:T(8,128)(2,1)}, u32[]{:S(2)}) copy-start(bf16[128,2048]{1,0:T(8,128)(2,1)} %param.5) | copy-start | bytes 1572868
  34.3 5.9 %copy-start.2 = (bf16[128,2048]{1,0:T(8,128)(2,1)S(1)}, bf16[128,2048]{1,0:T(8,128)(2,1)}, u32[]{:S(2)}) copy-start(bf16[128,2048]{1,0:T(8,128)(2,1)} %param.8) | copy-start | bytes 1572868
  35.5 17.1 %all-to-all-start.1 = ((bf16[4,512,256]{2,1,0:T(8,128)(2,1)}), bf16[4,512,256]{2,1,0:T(8,128)(2,1)S(1)}, u32[]{:S(2)}, u32[]{:S(2)}) async-start(bf16[4,512,256]{2,1,0:T(8,128)(2,1)} %pad_maximum_fusion.1), calls=%async_computation.1 | async-start | bytes 2097152 | tf_op jit(solution)/shard_map/all_to_all | solution.py:191
  40.5 1.5 copy-start.3
  52.6 19.6 %copy-start = (bf16[4,512,256]{2,1,0:T(8,128)(2,1)}, bf16[4,512,256]{2,1,0:T(8,128)(2,1)S(1)}, u32[]{:S(2)}) copy-start(bf16[4,512,256]{2,1,0:T(8,128)(2,1)S(1)} %all-to-all-done.1) | copy-start | bytes 3145732
  52.6 14.9 %all-to-all-start = ((bf16[256,4,512]{2,0,1:T(8,128)(2,1)}), bf16[256,4,512]{2,0,1:T(8,128)(2,1)S(1)}, u32[]{:S(2)}, u32[]{:S(2)}) async-start(bf16[256,4,512]{2,0,1:T(8,128)(2,1)} %copy.37), calls=%async_computation | async-start | bytes 2097152 | tf_op jit(solution)/shard_map/all_to_all | solution.py:179
  56.1 16.1 %collective-permute-start = (bf16[4,512,256]{2,1,0:T(8,128)(2,1)S(1)}, bf16[4,512,256]{2,1,0:T(8,128)(2,1)S(1)}, u32[]{:S(2)}, u32[]{:S(2)}) collective-permute-start(bf16[4,512,256]{2,1,0:T(8,128)(2,1)S(1)} %all-to-all-done.1), channel_id=1, source_target_pairs={{0,1},{1,2},{2,3},{3,4},{4,5},{5,6},{6,7},{7,8},{8,9},{9,10},{10,1... | collective-permute-start | bytes 3145736 | tf_op jit(solution)/shard_map/ppermute | solution.py:195
  91.9 18.2 %collective-permute-start.1 = (bf16[8,256,256]{2,1,0:T(8,128)(2,1)S(1)}, bf16[8,256,256]{2,1,0:T(8,128)(2,1)S(1)}, u32[]{:S(2)}, u32[]{:S(2)}) collective-permute-start(bf16[8,256,256]{2,1,0:T(8,128)(2,1)S(1)} %get-tuple-element.9), channel_id=1, source_target_pairs={{1,0},{2,1},{3,2},{4,3},{5,4},{6,5},{7,6},{8,7},{9,8},{10,9},{11,1... | collective-permute-start | bytes 3145736 | tf_op jit(solution)/shard_map/ppermute | solution.py:209
  130.9 19.4 %all-to-all-start.2 = ((bf16[4,256,512]{2,1,0:T(8,128)(2,1)}), bf16[4,256,512]{2,1,0:T(8,128)(2,1)S(1)}, u32[]{:S(2)}, u32[]{:S(2)}) async-start(bf16[4,256,512]{2,1,0:T(8,128)(2,1)} %get-tuple-element.7), calls=%async_computation.2 | async-start | bytes 2097152 | tf_op jit(solution)/shard_map/all_to_all | solution.py:219
  150.3 30.1 %all-to-all-start.4 = ((bf16[4,2,128,256]{3,2,1,0:T(8,128)(2,1)}), bf16[4,2,128,256]{3,2,1,0:T(8,128)(2,1)S(1)}, u32[]{:S(2)}, u32[]{:S(2)}) async-start(bf16[4,2,128,256]{3,2,1,0:T(8,128)(2,1)} %pad_maximum_fusion.2), calls=%async_computation.4 | async-start | bytes 1048576 | tf_op jit(solution)/shard_map/all_to_all | solution.py:215

commit v2 on v1

--- a/solution.py
+++ b/solution.py
@@ -15,6 +15,7 @@
 TILE = 256
 TILES = 2 * SPAN // TILE
 OWN = SPAN // TILE
+GROUP = 4
 HEADS = 4
 ROWS = HEADS * CHUNK
 BLOCK_AXES = ("z_lo", "x", "core")
@@ -28,17 +29,20 @@
     out_ref, grad_before_ref, grad_own_ref,
     keys, values, keys_t, values_t, probs, grad_keys, grad_values, out_t, grad_query_t, top, total,
 ):
+    z_hi = scalars[8]
     first = scalars[0]
-    z_hi = scalars[4]
 
     def load(source, shift):
         def body(tile, _):
+            here = pl.ds(pl.multiple_of(tile * TILE, TILE), TILE)
             both = source[tile - shift]
             k, v = both[:, :HEAD_SIZE], both[:, HEAD_SIZE:]
-            keys[tile] = k
-            values[tile] = v
-            keys_t[tile] = k.T
-            values_t[tile] = v.T
+            keys[here] = k
+            values[here] = v
+            keys_t[:, here] = k.T
+            values_t[:, here] = v.T
+            grad_keys[here] = jnp.zeros((TILE, HEAD_SIZE), jnp.float32)
+            grad_values[here] = jnp.zeros((TILE, HEAD_SIZE), jnp.float32)
             return 0
 
         return body
@@ -46,17 +50,18 @@
     lax.fori_loop(first, OWN, load(kv_before_ref, 0), 0)
     lax.fori_loop(jnp.maximum(first, OWN), TILES, load(kv_own_ref, OWN), 0)
 
-    def clear(tile, _):
-        grad_keys[tile] = jnp.zeros((TILE, HEAD_SIZE), jnp.float32)
-        grad_values[tile] = jnp.zeros((TILE, HEAD_SIZE), jnp.float32)
-        return 0
-
-    lax.fori_loop(0, TILES, clear, 0)
+    def sweep(low, high, step):
+        groups = (high - low) // GROUP
+        lax.fori_loop(0, groups, lambda i, _: step(low + i * GROUP, GROUP), 0)
+        if GROUP > 1:
+            lax.fori_loop(low + groups * GROUP, high, lambda i, _: step(i, 1), 0)
 
     def chunk_step(chunk, _):
         start = SPAN + (4 * chunk + z_hi) * CHUNK
         low = scalars[chunk]
         high = (start + CHUNK - 1) // TILE + 1
+        full_low = jnp.minimum((scalars[4 + chunk] + TILE - 1) // TILE, high)
+        full_high = jnp.clip((start + 1) // TILE, full_low, high)
         block = qd_ref[chunk]
         rows_q = jnp.concatenate(
             [block[:CHUNK, h * HEAD_SIZE : (h + 1) * HEAD_SIZE] for h in range(HEADS)], axis=0
@@ -71,56 +76,68 @@
         out_t[...] = jnp.zeros((HEAD_SIZE, ROWS), jnp.float32)
         grad_query_t[...] = jnp.zeros((HEAD_SIZE, ROWS), jnp.float32)
 
-        def scores_step(tile, _):
-            s = lax.dot_general(
-                keys[tile], rows_q, (((1,), (1,)), ((), ())), preferred_element_type=jnp.float32
-            )
-            key_pos = tile * TILE + lax.broadcasted_iota(jnp.int32, (TILE, ROWS), 0)
-            allowed = (key_pos >= begin) & (key_pos <= query_pos)
-            s = jnp.where(allowed, s * LOG2_SCALE, -1e30)
-            probs[tile] = s
-            top[...] = jnp.maximum(top[...], jnp.max(s.reshape(TILE // 8, 8, ROWS), axis=0))
-            return 0
-
-        lax.fori_loop(low, high, scores_step, 0)
+        def scores_step(masked):
+            def step(tile, count):
+                size = count * TILE
+                here = pl.ds(pl.multiple_of(tile * TILE, TILE), size)
+                s = LOG2_SCALE * lax.dot_general(
+                    keys[here], rows_q, (((1,), (1,)), ((), ())), preferred_element_type=jnp.float32
+                )
+                if masked:
+                    key_pos = tile * TILE + lax.broadcasted_iota(jnp.int32, (size, ROWS), 0)
+                    allowed = (key_pos >= begin) & (key_pos <= query_pos)
+                    s = jnp.where(allowed, s, -1e30)
+                probs[here] = s
+                top[...] = jnp.maximum(top[...], jnp.max(s.reshape(size // 8, 8, ROWS), axis=0))
+                return 0
+
+            return step
+
+        sweep(low, full_low, scores_step(True))
+        sweep(full_low, full_high, scores_step(False))
+        sweep(full_high, high, scores_step(True))
         row_top = jnp.max(top[...], axis=0, keepdims=True)
 
-        def output_step(tile, _):
-            p = jnp.exp2(probs[tile] - row_top)
-            probs[tile] = p
-            total[...] += jnp.sum(p.reshape(TILE // 8, 8, ROWS), axis=0)
+        def output_step(tile, count):
+            size = count * TILE
+            here = pl.ds(pl.multiple_of(tile * TILE, TILE), size)
+            p = jnp.exp2(probs[here] - row_top)
+            probs[here] = p
+            total[...] += jnp.sum(p.reshape(size // 8, 8, ROWS), axis=0)
             out_t[...] += lax.dot_general(
-                values_t[tile], p.astype(jnp.bfloat16), (((1,), (0,)), ((), ())),
+                values_t[:, here], p.astype(jnp.bfloat16), (((1,), (0,)), ((), ())),
                 preferred_element_type=jnp.float32,
             )
             return 0
 
-        lax.fori_loop(low, high, output_step, 0)
+        sweep(low, high, output_step)
         inverse = 1.0 / jnp.sum(total[...], axis=0, keepdims=True)
         attended = out_t[...] * inverse
         context = attended.T
         delta = jnp.sum(rows_d.astype(jnp.float32).T * attended, axis=0, keepdims=True)
 
-        def gradient_step(tile, _):
-            w = probs[tile] * inverse
+        def gradient_step(tile, count):
+            size = count * TILE
+            here = pl.ds(pl.multiple_of(tile * TILE, TILE), size)
+            w = probs[here] * inverse
             grad_weights = lax.dot_general(
-                values[tile], rows_d, (((1,), (1,)), ((), ())), preferred_element_type=jnp.float32
+                values[here], rows_d, (((1,), (1,)), ((), ())), preferred_element_type=jnp.float32
             )
             grad_scores = (w * (grad_weights - delta)).astype(jnp.bfloat16)
-            grad_values[tile] += lax.dot_general(
+            grad_values[here] += lax.dot_general(
                 w.astype(jnp.bfloat16), rows_d, (((1,), (0,)), ((), ())),
                 preferred_element_type=jnp.float32,
             )
-            grad_keys[tile] += lax.dot_general(
+            grad_keys[here] += lax.dot_general(
                 grad_scores, rows_q, (((1,), (0,)), ((), ())), preferred_element_type=jnp.float32
             )
             grad_query_t[...] += lax.dot_general(
-                keys_t[tile], grad_scores, (((1,), (0,)), ((), ())),
+                keys_t[:, here], grad_scores, (((1,), (0,)), ((), ())),
                 preferred_element_type=jnp.float32,
             )
             return 0
 
-        lax.fori_loop(low, high, gradient_step, 0)
+        sweep(low, high, gradient_step)
         grad_query = (grad_query_t[...] * SCALE).T
         for h in range(HEADS):
             span = slice(h * HEAD_SIZE, (h + 1) * HEAD_SIZE)
@@ -132,14 +149,24 @@
 
     def store(target, shift):
         def body(tile, _):
-            target[tile - shift, :, :HEAD_SIZE] = (grad_keys[tile] * SCALE).astype(jnp.bfloat16)
-            target[tile - shift, :, HEAD_SIZE:] = grad_values[tile].astype(jnp.bfloat16)
+            here = pl.ds(pl.multiple_of(tile * TILE, TILE), TILE)
+            target[tile - shift, :, :HEAD_SIZE] = (grad_keys[here] * SCALE).astype(jnp.bfloat16)
+            target[tile - shift, :, HEAD_SIZE:] = grad_values[here].astype(jnp.bfloat16)
             return 0
 
         return body
 
-    lax.fori_loop(0, OWN, store(grad_before_ref, 0), 0)
-    lax.fori_loop(OWN, TILES, store(grad_own_ref, OWN), 0)
+    def blank(target, shift):
+        def body(tile, _):
+            target[tile - shift] = jnp.zeros((TILE, 2 * HEAD_SIZE), jnp.bfloat16)
+            return 0
+
+        return body
+
+    lax.fori_loop(0, jnp.minimum(first, OWN), blank(grad_before_ref, 0), 0)
+    lax.fori_loop(OWN, first, blank(grad_own_ref, OWN), 0)
+    lax.fori_loop(first, OWN, store(grad_before_ref, 0), 0)
+    lax.fori_loop(jnp.maximum(first, OWN), TILES, store(grad_own_ref, OWN), 0)
 
 
 def attention(scalars, begin, qd, kv_before, kv_own):
@@ -152,13 +179,13 @@
         in_specs=[pl.BlockSpec(memory_space=pltpu.SMEM)] + [vmem] * 4,
         out_specs=(vmem, vmem, vmem),
         scratch_shapes=[
-            pltpu.VMEM((TILES, TILE, HEAD_SIZE), bf16),
-            pltpu.VMEM((TILES, TILE, HEAD_SIZE), bf16),
-            pltpu.VMEM((TILES, HEAD_SIZE, TILE), bf16),
-            pltpu.VMEM((TILES, HEAD_SIZE, TILE), bf16),
-            pltpu.VMEM((TILES, TILE, ROWS), f32),
-            pltpu.VMEM((TILES, TILE, HEAD_SIZE), f32),
-            pltpu.VMEM((TILES, TILE, HEAD_SIZE), f32),
+            pltpu.VMEM((2 * SPAN, HEAD_SIZE), bf16),
+            pltpu.VMEM((2 * SPAN, HEAD_SIZE), bf16),
+            pltpu.VMEM((HEAD_SIZE, 2 * SPAN), bf16),
+            pltpu.VMEM((HEAD_SIZE, 2 * SPAN), bf16),
+            pltpu.VMEM((2 * SPAN, ROWS), f32),
+            pltpu.VMEM((2 * SPAN, HEAD_SIZE), f32),
+            pltpu.VMEM((2 * SPAN, HEAD_SIZE), f32),
             pltpu.VMEM((HEAD_SIZE, ROWS), f32),
             pltpu.VMEM((HEAD_SIZE, ROWS), f32),
             pltpu.VMEM((8, ROWS), f32),
@@ -187,6 +214,7 @@
         axis=1,
     )
     kv = lax.all_gather(kv, "z_hi", axis=0, tiled=True)
+    qd, kv = lax.optimization_barrier((qd, kv))
     first, second = kv[:, : 2 * HEAD_SIZE], kv[:, 2 * HEAD_SIZE :]
     kv_own = lax.all_to_all(
         jnp.stack([first, first, second, second]), "y", split_axis=0, concat_axis=0, tiled=True
@@ -199,7 +227,7 @@
     chunk_start = (4 * jnp.arange(4, dtype=jnp.int32) + z_hi) * CHUNK + anchor + SPAN
     position = (chunk_start[:, None] + jnp.arange(CHUNK, dtype=jnp.int32)[None, :])[..., None]
     begin = jnp.max(jnp.where(starts <= position, starts, 0), axis=2).astype(jnp.int32) - anchor
-    scalars = jnp.concatenate([begin[:, 0] // TILE, z_hi[None]])
+    scalars = jnp.concatenate([begin[:, 0] // TILE, begin[:, -1], z_hi[None]])
     begin = jnp.tile(begin, (1, HEADS)).reshape(4, 1, ROWS)
 
     shape = (OWN, TILE, 2 * HEAD_SIZE)
@@ -207,6 +235,10 @@
         scalars, begin, qd, kv_before.reshape(shape), kv_own.reshape(shape)
     )
     returned = lax.ppermute(grad_before, BLOCK_AXES, [(i + 1, i) for i in range(blocks - 1)])
+    out = lax.all_to_all(
+        out.reshape(4 * 2 * CHUNK, ROWS), "y", split_axis=0, concat_axis=1, tiled=True
+    )
+    out, returned = lax.optimization_barrier((out, returned))
     grad_own = (grad_own.astype(jnp.float32) + returned.astype(jnp.float32)).astype(jnp.bfloat16)
     grad = lax.all_to_all(
         grad_own.reshape(4, 4, CHUNK, 2 * HEAD_SIZE), "y", split_axis=0, concat_axis=0, tiled=True
@@ -216,9 +248,6 @@
     grad = jnp.sum(grad.astype(jnp.float32), axis=0).astype(jnp.bfloat16)
     keys_gradient = jnp.concatenate([grad[0, :, :HEAD_SIZE], grad[1, :, :HEAD_SIZE]], axis=1)
     values_gradient = jnp.concatenate([grad[0, :, HEAD_SIZE:], grad[1, :, HEAD_SIZE:]], axis=1)
-    out = lax.all_to_all(
-        out.reshape(4 * 2 * CHUNK, ROWS), "y", split_axis=0, concat_axis=1, tiled=True
-    )
     return out[:CHUNK], out[CHUNK:], keys_gradient, values_gradient
 
 

time: 183 us -> 174 us (0.951)
  waiting for transfers between devices: 75.2 us -> 51.1 us
  blocking collectives: 53.3 us -> 71 us
  starting transfers between devices: 22.8 us -> 15.3 us
  local copies, waits for them, and re-layouts: 5.52 us -> 7.79 us
  Pallas kernels: 19.6 us -> 21.6 us
    all_to_all x0 -> x1, blocking collectives: none -> 19.2 us  [per_device(): lax.all_to_all(out.reshape(4 * 2 * CHUNK, ROWS), 'y', split_axis=0, conca...]
    all_to_all x1 -> x0, waiting for transfers between devices: 14.7 us -> none  [per_device(): lax.all_to_all(out.reshape(4 * 2 * CHUNK, ROWS), 'y', split_axis=0, conca...]
    ppermute x1, waiting for transfers between devices: 12.3 us -> 0.01 us  [per_device(): lax.ppermute(grad_before, BLOCK_AXES, [(i + 1, i) for i in range(blocks -...]
    all_to_all x1, waiting for transfers between devices: 9.08 us -> 0.01 us  [per_device(): lax.all_to_all(jnp.concatenate([queries, output_gradient], axis=0), 'y',...]
    ppermute x1, waiting for transfers between devices: 4.7 us -> 13.7 us  [per_device(): lax.ppermute(kv_own, BLOCK_AXES, [(i, i + 1) for i in range(blocks - 1)])]
    ppermute x1, starting transfers between devices: 5.92 us -> 1.92 us  [per_device(): lax.ppermute(grad_before, BLOCK_AXES, [(i + 1, i) for i in range(blocks -...]
    all_to_all x1 -> x0, starting transfers between devices: 3.52 us -> none  [per_device(): lax.all_to_all(out.reshape(4 * 2 * CHUNK, ROWS), 'y', split_axis=0, conca...]
    all_to_all x1, blocking collectives: 20.5 us -> 17.4 us  [per_device(): lax.all_to_all(grad_own.reshape(4, 4, CHUNK, 2 * HEAD_SIZE), 'y', split_a...]
  transfers between devices with their start and end apart: 6 -> 5, of which waited for: 6 -> 3; matrix products, arithmetic and copies ran while one was open for 3% -> 2% of each run, Pallas kernels for 0% -> 0%
where the time goes in v2:
time: 174 us; the launch traced here: 173 us
  blocking collectives  71 us (41%)
  waiting for transfers between devices  51.1 us (29%)
  Pallas kernels  21.6 us (12%)
  starting transfers between devices  15.3 us (9%)
  local copies, waits for them, and re-layouts  7.79 us (4%)
  other arithmetic  5.6 us (3%)
    all_gather x1, blocking collectives, per_device(): kv = lax.all_gather(kv, 'z_hi', axis=0, tiled=True)  34.5 us
    all_to_all x1, waiting for transfers between devices, per_device(): grad = lax.all_to_all(grad, 'z_hi', split_axis=0, concat_axis=0, tiled=True)  26.1 us
    pallas_call x1, Pallas kernels, attention(): pl.pallas_call(attention_kernel, out_shape=(jax.ShapeDtypeStruct((4, 2 *...  21.6 us
    all_to_all x1, blocking collectives, per_device(): lax.all_to_all(out.reshape(4 * 2 * CHUNK, ROWS), 'y', split_axis=0, conca...  19.2 us
    all_to_all x1, blocking collectives, per_device(): lax.all_to_all(grad_own.reshape(4, 4, CHUNK, 2 * HEAD_SIZE), 'y', split_a...  17.4 us
    ppermute x1, waiting for transfers between devices, per_device(): lax.ppermute(kv_own, BLOCK_AXES, [(i, i + 1) for i in range(blocks - 1)])  13.7 us
    all_to_all x1, waiting for transfers between devices, per_device(): lax.all_to_all(jnp.stack([first, first, second, second]), 'y', split_axis...  11.3 us
    unnamed x12, local copies, waits for them, and re-layouts  4.66 us
  transfers between devices with their start and end apart: 5, of which 3 were waited for; matrix products, arithmetic and copies ran while one was open for 2% of the time, Pallas kernels for 0%

profile of v2, /device:TPU:6, one launch (start us, length us, event | category | flops | bytes accessed | tf_op | source)
XLA Modules:
  0.0 173.3 jit_solution(10686124224991033735)
XLA Ops:
  0.6 1.3 copy.32
  1.9 1.3 copy.33
  3.4 1.3 copy.34
  4.7 4.5 %all-to-all-start = ((bf16[256,4,512]{2,0,1:T(8,128)(2,1)}), bf16[256,4,512]{2,0,1:T(8,128)(2,1)S(1)}, u32[]{:S(2)}, u32[]{:S(2)}) async-start(bf16[256,4,512]{2,0,1:T(8,128)(2,1)} %copy.34), calls=%async_computation | async-start | bytes 2097152 | tf_op jit(solution)/shard_map/all_to_all | solution.py:206
  9.3 34.5 %all_gather.3 = bf16[512,512]{1,0:T(8,128)(2,1)S(1)} all-gather(bf16[128,512]{1,0:T(8,128)(2,1)S(1)} %pad_maximum_fusion.3), channel_id=1, replica_groups=mesh['y'=4,'z_hi'=4,'z_lo'=4,'x'=4,'core'=2] {'z_hi'}, dimensions={0}, use_global_device_ids=true | all-gather | bytes 655360 | tf_op jit(solution)/shard_map/all_gather | solution.py:216
  43.8 1.1 pad_maximum_fusion.1
  44.9 3.5 %all-to-all-start.1 = ((bf16[4,512,256]{2,1,0:T(8,128)(2,1)}), bf16[4,512,256]{2,1,0:T(8,128)(2,1)S(1)}, u32[]{:S(2)}, u32[]{:S(2)}) async-start(bf16[4,512,256]{2,1,0:T(8,128)(2,1)} %pad_maximum_fusion.1), calls=%async_computation.1 | async-start | bytes 2097152 | tf_op jit(solution)/shard_map/all_to_all | solution.py:219
  48.5 11.3 %all-to-all-done.1 = bf16[4,512,256]{2,1,0:T(8,128)(2,1)S(1)} async-done(((bf16[4,512,256]{2,1,0:T(8,128)(2,1)}), bf16[4,512,256]{2,1,0:T(8,128)(2,1)S(1)}, u32[]{:S(2)}, u32[]{:S(2)}) %all-to-all-start.1) | async-done | bytes 1048608 | tf_op jit(solution)/shard_map/all_to_all | solution.py:219
  59.8 1.9 %collective-permute-start = (bf16[4,512,256]{2,1,0:T(8,128)(2,1)S(1)}, bf16[4,512,256]{2,1,0:T(8,128)(2,1)S(1)}, u32[]{:S(2)}, u32[]{:S(2)}) collective-permute-start(bf16[4,512,256]{2,1,0:T(8,128)(2,1)S(1)} %all-to-all-done.1), channel_id=1, source_target_pairs={{0,1},{1,2},{2,3},{3,4},{4,5},{5,6},{6,7},{7,8},{8,9},{9,10},{10,1... | collective-permute-start | bytes 3145736 | tf_op jit(solution)/shard_map/ppermute | solution.py:223
  62.2 13.7 %collective-permute-done = bf16[4,512,256]{2,1,0:T(8,128)(2,1)S(1)} collective-permute-done((bf16[4,512,256]{2,1,0:T(8,128)(2,1)S(1)}, bf16[4,512,256]{2,1,0:T(8,128)(2,1)S(1)}, u32[]{:S(2)}, u32[]{:S(2)}) %collective-permute-start) | collective-permute-done | bytes 1048608 | tf_op jit(solution)/shard_map/ppermute | solution.py:223
  76.0 21.6 %attention.1 = (bf16[4,256,512]{2,1,0:T(8,128)(2,1)S(1)}, bf16[8,256,256]{2,1,0:T(8,128)(2,1)S(1)}, bf16[8,256,256]{2,1,0:T(8,128)(2,1)S(1)}) custom-call(s32[9]{0:T(128)S(1)} %pad_add_fusion.scalars, s32[4,1,512]{2,1,0:T(1,128)S(1)} %bitcast.28, bf16[4,256,512]{2,1,0:T(8,128)(2,1)S(1)} %bitcast.27, bf16[8,256,256]{2,1,0:T(8,128)(2,1)S(1)} %bitcast.29, ...), custom_call_target="tpu_custom_call" | custom-call | flops 4000000000 | bytes 6291456 | tf_op jit(solution)/shard_map/attention/pallas_call | solution.py:176
  97.6 1.9 %collective-permute-start.1 = (bf16[8,256,256]{2,1,0:T(8,128)(2,1)S(1)}, bf16[8,256,256]{2,1,0:T(8,128)(2,1)}, u32[]{:S(2)}, u32[]{:S(2)}) collective-permute-start(bf16[8,256,256]{2,1,0:T(8,128)(2,1)S(1)} %get-tuple-element.14), channel_id=1, source_target_pairs={{1,0},{2,1},{3,2},{4,3},{5,4},{6,5},{7,6},{8,7},{9,8},{10,9},{11,1... | collective-permute-start | bytes 3145736 | tf_op jit(solution)/shard_map/ppermute | solution.py:237
  99.5 19.2 %all_to_all.47 = bf16[4,256,512]{2,1,0:T(8,128)(2,1)} all-to-all(bf16[4,256,512]{2,1,0:T(8,128)(2,1)S(1)} %get-tuple-element.13), channel_id=1, replica_groups=mesh['y'=4,'z_hi'=4,'z_lo'=4,'x'=4,'core'=2] {'y'}, dimensions={0} | all-to-all | bytes 2097152 | tf_op jit(solution)/shard_map/all_to_all | solution.py:238
  118.7 1.5 copy.35
  120.2 1.5 add_convert_fusion
  121.6 17.4 %all_to_all.48 = bf16[4,4,128,256]{3,2,1,0:T(8,128)(2,1)S(1)} all-to-all(bf16[4,4,128,256]{3,2,1,0:T(8,128)(2,1)S(1)} %bitcast.30), channel_id=1, replica_groups=mesh['y'=4,'z_hi'=4,'z_lo'=4,'x'=4,'core'=2] {'y'}, dimensions={0} | all-to-all | bytes 2097152 | tf_op jit(solution)/shard_map/all_to_all | solution.py:243
  139.0 0.2 convert_element_type.18
  139.4 0.8 pad_maximum_fusion.2
  140.2 3.5 %all-to-all-start.4 = ((bf16[4,2,128,256]{3,2,1,0:T(8,128)(2,1)}), bf16[4,2,128,256]{3,2,1,0:T(8,128)(2,1)S(1)}, u32[]{:S(2)}, u32[]{:S(2)}) async-start(bf16[4,2,128,256]{3,2,1,0:T(8,128)(2,1)} %pad_maximum_fusion.2), calls=%async_computation.4 | async-start | bytes 1048576 | tf_op jit(solution)/shard_map/all_to_all | solution.py:247
  143.8 1.0 copy.38
  144.8 1.0 copy.37
  145.8 26.1 %all-to-all-done.4 = bf16[4,2,128,256]{3,2,1,0:T(8,128)(2,1)S(1)} async-done(((bf16[4,2,128,256]{3,2,1,0:T(8,128)(2,1)}), bf16[4,2,128,256]{3,2,1,0:T(8,128)(2,1)S(1)}, u32[]{:S(2)}, u32[]{:S(2)}) %all-to-all-start.4) | async-done | bytes 524320 | tf_op jit(solution)/shard_map/all_to_all | solution.py:247
  172.0 0.6 pad_maximum_fusion.5
  172.6 0.6 pad_maximum_fusion.4
  (27 shorter events, 1.1 us)
Async XLA Ops:
  3.4 5.8 %copy-start.1 = (bf16[128,256]{1,0:T(8,128)(2,1)S(1)}, bf16[128,256]{1,0:T(8,128)(2,1)}, u32[]{:S(2)}) copy-start(bf16[128,256]{1,0:T(8,128)(2,1)} %param.6) | copy-start | bytes 196612
  3.4 5.8 %copy-start.2 = (bf16[128,256]{1,0:T(8,128)(2,1)S(1)}, bf16[128,256]{1,0:T(8,128)(2,1)}, u32[]{:S(2)}) copy-start(bf16[128,256]{1,0:T(8,128)(2,1)} %param.7) | copy-start | bytes 196612
  4.7 39.0 %all-to-all-start = ((bf16[256,4,512]{2,0,1:T(8,128)(2,1)}), bf16[256,4,512]{2,0,1:T(8,128)(2,1)S(1)}, u32[]{:S(2)}, u32[]{:S(2)}) async-start(bf16[256,4,512]{2,0,1:T(8,128)(2,1)} %copy.34), calls=%async_computation | async-start | bytes 2097152 | tf_op jit(solution)/shard_map/all_to_all | solution.py:206
  43.8 4.6 %copy-start.3 = (s32[64]{0:T(128)S(1)}, s32[64]{0:T(128)}, u32[]{:S(2)}) copy-start(s32[64]{0:T(128)} %param.9) | copy-start | bytes 772
  44.9 15.0 %all-to-all-start.1 = ((bf16[4,512,256]{2,1,0:T(8,128)(2,1)}), bf16[4,512,256]{2,1,0:T(8,128)(2,1)S(1)}, u32[]{:S(2)}, u32[]{:S(2)}) async-start(bf16[4,512,256]{2,1,0:T(8,128)(2,1)} %pad_maximum_fusion.1), calls=%async_computation.1 | async-start | bytes 2097152 | tf_op jit(solution)/shard_map/all_to_all | solution.py:219
  59.8 16.1 %copy-start = (bf16[4,512,256]{2,1,0:T(8,128)(2,1)}, bf16[4,512,256]{2,1,0:T(8,128)(2,1)S(1)}, u32[]{:S(2)}) copy-start(bf16[4,512,256]{2,1,0:T(8,128)(2,1)S(1)} %all-to-all-done.1) | copy-start | bytes 3145732
  59.8 16.1 %collective-permute-start = (bf16[4,512,256]{2,1,0:T(8,128)(2,1)S(1)}, bf16[4,512,256]{2,1,0:T(8,128)(2,1)S(1)}, u32[]{:S(2)}, u32[]{:S(2)}) collective-permute-start(bf16[4,512,256]{2,1,0:T(8,128)(2,1)S(1)} %all-to-all-done.1), channel_id=1, source_target_pairs={{0,1},{1,2},{2,3},{3,4},{4,5},{5,6},{6,7},{7,8},{8,9},{9,10},{10,1... | collective-permute-start | bytes 3145736 | tf_op jit(solution)/shard_map/ppermute | solution.py:223
  97.6 22.6 %collective-permute-start.1 = (bf16[8,256,256]{2,1,0:T(8,128)(2,1)S(1)}, bf16[8,256,256]{2,1,0:T(8,128)(2,1)}, u32[]{:S(2)}, u32[]{:S(2)}) collective-permute-start(bf16[8,256,256]{2,1,0:T(8,128)(2,1)S(1)} %get-tuple-element.14), channel_id=1, source_target_pairs={{1,0},{2,1},{3,2},{4,3},{5,4},{6,5},{7,6},{8,7},{9,8},{10,9},{11,1... | collective-permute-start | bytes 3145736 | tf_op jit(solution)/shard_map/ppermute | solution.py:237
  140.2 31.7 %all-to-all-start.4 = ((bf16[4,2,128,256]{3,2,1,0:T(8,128)(2,1)}), bf16[4,2,128,256]{3,2,1,0:T(8,128)(2,1)S(1)}, u32[]{:S(2)}, u32[]{:S(2)}) async-start(bf16[4,2,128,256]{3,2,1,0:T(8,128)(2,1)} %pad_maximum_fusion.2), calls=%async_computation.4 | async-start | bytes 1048576 | tf_op jit(solution)/shard_map/all_to_all | solution.py:247

commit v3 on v1

v3 whole, which is shorter than its diff:
```python
import math

import jax
import jax.numpy as jnp
import numpy as np
from jax import lax
from jax.experimental import pallas as pl
from jax.experimental.pallas import tpu as pltpu
from jax.sharding import Mesh
from jax.sharding import PartitionSpec as P

HEAD_SIZE = 128
SPAN = 2048
CHUNK = 128
TILE = 256
TILES = SPAN // TILE
GROUP = 4
BACK_GROUP = 2
HEADS = 4
ROWS = HEADS * CHUNK
BLOCK_AXES = ("z_lo", "x", "core")
TOKEN_AXES = ("z_lo", "x", "core", "y", "z_hi")
SCALE = 1.0 / math.sqrt(HEAD_SIZE)
LOG2_SCALE = SCALE * math.log2(math.e)
F32, BF16 = jnp.float32, jnp.bfloat16


def dot(a, b, contract):
    return lax.dot_general(a, b, (contract, ((), ())), preferred_element_type=F32)


def rows_of(ref, chunk, part):
    block = ref[chunk, part * CHUNK : (part + 1) * CHUNK]
    return jnp.concatenate(
        [block[:, h * HEAD_SIZE : (h + 1) * HEAD_SIZE] for h in range(HEADS)], axis=0
    )


def store_rows(ref, chunk, value):
    for h in range(HEADS):
        ref[chunk, :, h * HEAD_SIZE : (h + 1) * HEAD_SIZE] = value[
            h * CHUNK : (h + 1) * CHUNK
        ].astype(BF16)


def at(tile, count=1):
    return pl.ds(pl.multiple_of(tile * TILE, TILE), count * TILE)


def sweep(low, high, step, group):
    groups = (high - low) // group

    def many(i, _):
        step(low + i * group, group)
        return 0

    def one(i, _):
        step(i, 1)
        return 0

    lax.fori_loop(0, groups, many, 0)
    if group > 1:
        lax.fori_loop(low + groups * group, high, one, 0)


def own_range(scalars, chunk):
    start = (4 * chunk + scalars[8]) * CHUNK
    low = jnp.maximum(scalars[chunk], 0) // TILE
    high = (start + CHUNK - 1) // TILE + 1
    full_low = jnp.minimum((jnp.maximum(scalars[4 + chunk], 0) + TILE - 1) // TILE, high)
    full_high = jnp.clip((start + 1) // TILE, full_low, high)
    return start, low, high, full_low, full_high


def before_range(scalars, chunk):
    low = jnp.minimum(scalars[chunk] + SPAN, SPAN) // TILE
    full_low = jnp.minimum((scalars[4 + chunk] + SPAN + TILE - 1) // TILE, TILES)
    return low, full_low


def position_in_rows(start):
    return start + (lax.broadcasted_iota(jnp.int32, (1, ROWS), 1) & (CHUNK - 1))


def scores(keys, rows_q, tile, count, limits):
    s = LOG2_SCALE * dot(keys, rows_q, ((1,), (1,)))
    if limits is not None:
        begin, last = limits
        key_pos = tile * TILE + lax.broadcasted_iota(jnp.int32, (count * TILE, ROWS), 0)
        allowed = key_pos >= begin
        if last is not None:
            allowed &= key_pos <= last
        s = jnp.where(allowed, s, -1e30)
    return s


def fold(value, how):
    return how(value.reshape(value.shape[0] // 8, 8, ROWS), axis=0)


def own_forward(scalars, begin_ref, qd_ref, kv_ref, stats_ref, out_ref, values_t, probs, top, total):
    first = jnp.maximum(scalars[0], 0) // TILE

    def load(tile, _):
        values_t[:, at(tile)] = kv_ref[at(tile), HEAD_SIZE:].T
        return 0

    lax.fori_loop(first, TILES, load, 0)

    def chunk_step(chunk, _):
        start, low, high, full_low, full_high = own_range(scalars, chunk)
        rows_q = rows_of(qd_ref, chunk, 0)
        limits = (begin_ref[chunk], position_in_rows(start))
        top[...] = jnp.full((8, ROWS), -1e30, F32)
        total[...] = jnp.zeros((8, ROWS), F32)
        out_ref[chunk] = jnp.zeros((HEAD_SIZE, ROWS), F32)

        def scores_step(limits):
            def step(tile, count):
                here = at(tile, count)
                s = scores(kv_ref[here, :HEAD_SIZE], rows_q, tile, count, limits)
                probs[here] = s
                top[...] = jnp.maximum(top[...], fold(s, jnp.max))

            return step

        sweep(low, full_low, scores_step(limits), GROUP)
        sweep(full_low, full_high, scores_step(None), GROUP)
        sweep(full_high, high, scores_step(limits), GROUP)
        row_top = jnp.max(top[...], axis=0, keepdims=True)

        def output_step(tile, count):
            here = at(tile, count)
            p = jnp.exp2(probs[here] - row_top)
            total[...] += fold(p, jnp.sum)
            out_ref[chunk] += dot(values_t[:, here], p.astype(BF16), ((1,), (0,)))

        sweep(low, high, output_step, GROUP)
        stats_ref[chunk, 0:1] = row_top
        stats_ref[chunk, 1:2] = jnp.sum(total[...], axis=0, keepdims=True)
        return 0

    lax.fori_loop(0, 4, chunk_step, 0)


def before_part(
    scalars, begin_ref, qd_ref, kv_ref, stats_in, out_in,
    context_ref, grad_ref, stats_ref, grad_query_ref,
    keys_t, values_t, probs, grad_keys, grad_values, out_t, top, total,
):
    first = jnp.minimum(scalars[0] + SPAN, SPAN) // TILE

    def load(tile, _):
        keys_t[:, at(tile)] = kv_ref[at(tile), :HEAD_SIZE].T
        values_t[:, at(tile)] = kv_ref[at(tile), HEAD_SIZE:].T
        grad_keys[at(tile)] = jnp.zeros((TILE, HEAD_SIZE), F32)
        grad_values[at(tile)] = jnp.zeros((TILE, HEAD_SIZE), F32)
        return 0

    lax.fori_loop(first, TILES, load, 0)

    def blank(tile, _):
        grad_ref[at(tile)] = jnp.zeros((TILE, 2 * HEAD_SIZE), BF16)
        return 0

    lax.fori_loop(0, first, blank, 0)

    def chunk_step(chunk, _):
        low, full_low = before_range(scalars, chunk)
        rows_q = rows_of(qd_ref, chunk, 0)
        rows_d = rows_of(qd_ref, chunk, 1)
        limits = (begin_ref[chunk] + SPAN, None)
        own_top, own_total = stats_in[chunk, 0:1], stats_in[chunk, 1:2]
        top[...] = jnp.broadcast_to(own_top, (8, ROWS))
        total[...] = jnp.zeros((8, ROWS), F32)
        grad_query_ref[chunk] = jnp.zeros((HEAD_SIZE, ROWS), F32)

        def scores_step(limits):
            def step(tile, count):
                here = at(tile, count)
                s = scores(kv_ref[here, :HEAD_SIZE], rows_q, tile, count, limits)
                probs[here] = s
                top[...] = jnp.maximum(top[...], fold(s, jnp.max))

            return step

        sweep(low, full_low, scores_step(limits), GROUP)
        sweep(full_low, TILES, scores_step(None), GROUP)
        row_top = jnp.max(top[...], axis=0, keepdims=True)
        rescale = jnp.exp2(own_top - row_top)
        out_t[...] = out_in[chunk] * rescale

        def output_step(tile, count):
            here = at(tile, count)
            p = jnp.exp2(probs[here] - row_top)
            probs[here] = p
            total[...] += fold(p, jnp.sum)
            out_t[...] += dot(values_t[:, here], p.astype(BF16), ((1,), (0,)))

        sweep(low, TILES, output_step, GROUP)
        row_total = jnp.sum(total[...], axis=0, keepdims=True) + own_total * rescale
        inverse = 1.0 / row_total
        attended = out_t[...] * inverse
        delta = jnp.sum(rows_d.astype(F32).T * attended, axis=0, keepdims=True)
        store_rows(context_ref, chunk, attended.T)
        stats_ref[chunk, 0:1] = row_top + jnp.log2(row_total)
        stats_ref[chunk, 1:2] = delta

        def gradient_step(tile, count):
            here = at(tile, count)
            w = probs[here] * inverse
            grad_weights = dot(kv_ref[here, HEAD_SIZE:], rows_d, ((1,), (1,)))
            grad_scores = (w * (grad_weights - delta)).astype(BF16)
            grad_values[here] += dot(w.astype(BF16), rows_d, ((1,), (0,)))
            grad_keys[here] += dot(grad_scores, rows_q, ((1,), (0,)))
            grad_query_ref[chunk] += dot(keys_t[:, here], grad_scores, ((1,), (0,)))

        sweep(low, TILES, gradient_step, GROUP)
        return 0

    lax.fori_loop(0, 4, chunk_step, 0)

    def store(tile, _):
        grad_ref[at(tile), :HEAD_SIZE] = (grad_keys[at(tile)] * SCALE).astype(BF16)
        grad_ref[at(tile), HEAD_SIZE:] = grad_values[at(tile)].astype(BF16)
        return 0

    lax.fori_loop(first, TILES, store, 0)


def own_backward(
    scalars, begin_ref, qd_ref, kv_ref, stats_in, grad_query_in,
    grad_query_ref, grad_ref, keys_t, grad_keys, grad_values, grad_query_t,
):
    first = jnp.maximum(scalars[0], 0) // TILE

    def load(tile, _):
        keys_t[:, at(tile)] = kv_ref[at(tile), :HEAD_SIZE].T
        grad_keys[at(tile)] = jnp.zeros((TILE, HEAD_SIZE), F32)
        grad_values[at(tile)] = jnp.zeros((TILE, HEAD_SIZE), F32)
        return 0

    lax.fori_loop(first, TILES, load, 0)

    def blank(tile, _):
        grad_ref[at(tile)] = jnp.zeros((TILE, 2 * HEAD_SIZE), BF16)
        return 0

    lax.fori_loop(0, first, blank, 0)

    def chunk_step(chunk, _):
        start, low, high, full_low, full_high = own_range(scalars, chunk)
        rows_q = rows_of(qd_ref, chunk, 0)
        rows_d = rows_of(qd_ref, chunk, 1)
        limits = (begin_ref[chunk], position_in_rows(start))
        log_total, delta = stats_in[chunk, 0:1], stats_in[chunk, 1:2]
        grad_query_t[...] = grad_query_in[chunk]

        def gradient_step(limits):
            def step(tile, count):
                here = at(tile, count)
                s = scores(kv_ref[here, :HEAD_SIZE], rows_q, tile, count, limits)
                w = jnp.exp2(s - log_total)
                grad_weights = dot(kv_ref[here, HEAD_SIZE:], rows_d, ((1,), (1,)))
                grad_scores = (w * (grad_weights - delta)).astype(BF16)
                grad_values[here] += dot(w.astype(BF16), rows_d, ((1,), (0,)))
                grad_keys[here] += dot(grad_scores, rows_q, ((1,), (0,)))
                grad_query_t[...] += dot(keys_t[:, here], grad_scores, ((1,), (0,)))

            return step

        sweep(low, full_low, gradient_step(limits), BACK_GROUP)
        sweep(full_low, full_high, gradient_step(None), BACK_GROUP)
        sweep(full_high, high, gradient_step(limits), BACK_GROUP)
        store_rows(grad_query_ref, chunk, (grad_query_t[...] * SCALE).T)
        return 0

    lax.fori_loop(0, 4, chunk_step, 0)

    def store(tile, _):
        grad_ref[at(tile), :HEAD_SIZE] = (grad_keys[at(tile)] * SCALE).astype(BF16)
        grad_ref[at(tile), HEAD_SIZE:] = grad_values[at(tile)].astype(BF16)
        return 0

    lax.fori_loop(first, TILES, store, 0)


def call(kernel, name, gflops, outs, scratch, *args):
    vmem = pl.BlockSpec(memory_space=pltpu.VMEM)
    return pl.pallas_call(
        kernel,
        out_shape=tuple(jax.ShapeDtypeStruct(shape, dtype) for shape, dtype in outs),
        in_specs=[pl.BlockSpec(memory_space=pltpu.SMEM)] + [vmem] * (len(args) - 1),
        out_specs=tuple(vmem for _ in outs),
        scratch_shapes=[pltpu.VMEM(shape, dtype) for shape, dtype in scratch],
        compiler_params=pltpu.CompilerParams(vmem_limit_bytes=36 << 20),
        cost_estimate=pl.CostEstimate(
            flops=gflops * 10**9, bytes_accessed=4 << 20, transcendentals=2 * 10**6
        ),
        name=name,
    )(*args)


STATS = ((4, 2, ROWS), F32)
ACROSS = ((4, HEAD_SIZE, ROWS), F32)
RESULT = ((4, CHUNK, ROWS), BF16)
GRADS = ((SPAN, 2 * HEAD_SIZE), BF16)
TURNED = ((HEAD_SIZE, SPAN), BF16)
SQUARE = ((SPAN, ROWS), F32)
SUMS = ((SPAN, HEAD_SIZE), F32)
FLAT = ((HEAD_SIZE, ROWS), F32)
EIGHT = ((8, ROWS), F32)


def run_own_forward(scalars, begin, qd, kv):
    return call(
        own_forward, "own_forward", 2, (STATS, ACROSS), (TURNED, SQUARE, EIGHT, EIGHT),
        scalars, begin, qd, kv,
    )


def run_before_part(scalars, begin, qd, kv, stats, out):
    return call(
        before_part, "before_part", 2, (RESULT, GRADS, STATS, ACROSS),
        (TURNED, TURNED, SQUARE, SUMS, SUMS, FLAT, EIGHT, EIGHT),
        scalars, begin, qd, kv, stats, out,
    )


def run_own_backward(scalars, begin, qd, kv, stats, grad_query):
    return call(
        own_backward, "own_backward", 3, (RESULT, GRADS), (TURNED, SUMS, SUMS, FLAT),
        scalars, begin, qd, kv, stats, grad_query,
    )


def columns(value, index, count):
    width = value.shape[1] // count
    return value[:, index * width : (index + 1) * width]


def per_device(queries, key_projection, value_projection, output_gradient, doc_lengths):
    z_hi = lax.axis_index("z_hi").astype(jnp.int32)
    block = lax.axis_index(BLOCK_AXES).astype(jnp.int32)
    blocks = lax.axis_size(BLOCK_AXES)
    own_start = block * SPAN
    qd = jnp.stack(
        [
            jnp.concatenate([columns(queries, d, 4), columns(output_gradient, d, 4)], axis=0)
            for d in range(4)
        ]
    )
    qd = lax.all_to_all(qd, "y", split_axis=0, concat_axis=0, tiled=True)
    kv = jnp.concatenate(
        [
            columns(part, head, 2)
            for head in range(2)
            for part in (key_projection, value_projection)
        ],
        axis=1,
    )
    kv = lax.all_gather(kv, "z_hi", axis=0, tiled=True)
    qd, kv = lax.optimization_barrier((qd, kv))
    first, second = columns(kv, 0, 2), columns(kv, 1, 2)
    kv_own = lax.all_to_all(
        jnp.stack([first, first, second, second]), "y", split_axis=0, concat_axis=0, tiled=True
    ).reshape(SPAN, 2 * HEAD_SIZE)
    kv_before = lax.ppermute(kv_own, BLOCK_AXES, [(i, i + 1) for i in range(blocks - 1)])
    docs = doc_lengths.shape[0]
    order = jnp.arange(docs)
    starts = jnp.sum(jnp.where(order[None, :] < order[:, None], doc_lengths[None, :], 0), axis=1)
    chunk_start = (4 * jnp.arange(4, dtype=jnp.int32) + z_hi) * CHUNK + own_start
    position = (chunk_start[:, None] + jnp.arange(CHUNK, dtype=jnp.int32)[None, :])[..., None]
    begin = jnp.max(jnp.where(starts <= position, starts, 0), axis=2).astype(jnp.int32) - own_start
    scalars = jnp.concatenate([begin[:, 0], begin[:, -1], z_hi[None]])
    begin = jnp.tile(begin, (1, HEADS)).reshape(4, 1, ROWS)

    stats, out = run_own_forward(scalars, begin, qd, kv_own)
    kv_before, stats, out = lax.optimization_barrier((kv_before, stats, out))
    context, grad_before, stats, grad_query = run_before_part(
        scalars, begin, qd, kv_before, stats, out
    )
    returned = lax.ppermute(grad_before, BLOCK_AXES, [(i + 1, i) for i in range(blocks - 1)])
    context = lax.all_to_all(context, "y", split_axis=0, concat_axis=0, tiled=True)
    grad_query, grad_own = run_own_backward(scalars, begin, qd, kv_own, stats, grad_query)
    context, returned, grad_own = lax.optimization_barrier((context, returned, grad_own))
    grad_own = (grad_own.astype(F32) + returned.astype(F32)).astype(BF16)
    grad = lax.all_to_all(
        grad_own.reshape(4, 4, CHUNK, 2 * HEAD_SIZE), "y", split_axis=0, concat_axis=0, tiled=True
    )

    def part(step):
        mine = lax.dynamic_index_in_dim(grad, (z_hi + step) % 4, axis=1, keepdims=False).astype(F32)
        return jnp.stack([mine[0] + mine[1], mine[2] + mine[3]])

    arrived = [
        lax.ppermute(part(step).astype(BF16), "z_hi", [(i, (i + step) % 4) for i in range(4)])
        for step in (2, 1, 3)
    ]
    grad_query = lax.all_to_all(grad_query, "y", split_axis=0, concat_axis=0, tiled=True)
    grad_query, *arrived = lax.optimization_barrier((grad_query, *arrived))
    grad = part(0)
    for piece in arrived:
        grad += piece.astype(F32)
    grad = grad.astype(BF16)
    keys_gradient = jnp.concatenate([grad[0, :, :HEAD_SIZE], grad[1, :, :HEAD_SIZE]], axis=1)
    values_gradient = jnp.concatenate([grad[0, :, HEAD_SIZE:], grad[1, :, HEAD_SIZE:]], axis=1)
    return (
        jnp.concatenate([context[i] for i in range(4)], axis=1),
        jnp.concatenate([grad_query[i] for i in range(4)], axis=1),
        keys_gradient,
        values_gradient,
    )


def solution(mesh):
    order = [mesh.axis_names.index(name) for name in ("uly", "blk")]
    devices = np.transpose(mesh.devices, order).reshape(4, 4, 4, 4, 2)
    fine = Mesh(devices, ("y", "z_hi", "z_lo", "x", "core"))
    rows = P(TOKEN_AXES, None)
    return jax.shard_map(
        per_device, mesh=fine, in_specs=(rows, rows, rows, rows, P()),
        out_specs=(rows, rows, rows, rows), check_vma=False,
    )
```

time: 183 us -> 166 us (0.907)
  the two profiles are of different devices: /device:TPU:6 before, /device:TPU:12 now
where the time goes in v3:
time: 166 us; the launch traced here: 165 us
  starting transfers between devices  47.3 us (28%)
  waiting for transfers between devices  44.7 us (27%)
  blocking collectives  32.3 us (19%)
  Pallas kernels  26.5 us (16%)
  other arithmetic  8.66 us (5%)
  local copies, waits for them, and re-layouts  4.98 us (3%)
    all_gather x1, blocking collectives, per_device(): kv = lax.all_gather(kv, 'z_hi', axis=0, tiled=True)  32.3 us
    pallas_call x3, Pallas kernels, call(): pl.pallas_call(kernel, out_shape=tuple((jax.ShapeDtypeStruct(shape, dtype...  26.5 us
    ppermute x3, waiting for transfers between devices, per_device(): lax.ppermute(part(step).astype(BF16), 'z_hi', [(i, (i + step) % 4) for i...  19.3 us
    ppermute x3, starting transfers between devices, per_device(): lax.ppermute(part(step).astype(BF16), 'z_hi', [(i, (i + step) % 4) for i...  17.3 us
    all_to_all x1, waiting for transfers between devices, per_device(): lax.all_to_all(jnp.stack([first, first, second, second]), 'y', split_axis...  9.91 us
    all_to_all x1, waiting for transfers between devices, per_device(): lax.all_to_all(grad_own.reshape(4, 4, CHUNK, 2 * HEAD_SIZE), 'y', split_a...  9.52 us
    ppermute x1, waiting for transfers between devices, per_device(): lax.ppermute(kv_own, BLOCK_AXES, [(i, i + 1) for i in range(blocks - 1)])  5.92 us
    all_to_all x1, starting transfers between devices, per_device(): lax.all_to_all(jnp.stack([first, first, second, second]), 'y', split_axis...  5.83 us
  transfers between devices with their start and end apart: 10, of which 6 were waited for; matrix products, arithmetic and copies ran while one was open for 2% of the time, Pallas kernels for 11%

profile of v3, /device:TPU:12, one launch (start us, length us, event | category | flops | bytes accessed | tf_op | source)
XLA Modules:
  0.0 165.2 jit_solution(9780810442376059201)
XLA Ops:
  0.6 1.2 fusion.17
  2.1 1.1 pad_maximum_fusion
  3.2 5.0 %all-to-all-start = ((bf16[4,256,512]{2,1,0:T(8,128)(2,1)}), bf16[4,256,512]{2,1,0:T(8,128)(2,1)S(1)}, u32[]{:S(2)}, u32[]{:S(2)}) async-start(bf16[4,256,512]{2,1,0:T(8,128)(2,1)} %pad_maximum_fusion), calls=%async_computation | async-start | bytes 2097152 | tf_op jit(solution)/shard_map/all_to_all | solution.py:353
  8.3 32.3 %all_gather.3 = bf16[512,512]{1,0:T(8,128)(2,1)S(1)} all-gather(bf16[128,512]{1,0:T(8,128)(2,1)S(1)} %pad_maximum_fusion.4), channel_id=1, replica_groups=mesh['y'=4,'z_hi'=4,'z_lo'=4,'x'=4,'core'=2] {'z_hi'}, dimensions={0}, use_global_device_ids=true | all-gather | bytes 655360 | tf_op jit(solution)/shard_map/all_gather | solution.py:362
  40.6 1.1 pad_maximum_fusion.1
  41.7 5.8 %all-to-all-start.1 = ((bf16[4,512,256]{2,1,0:T(8,128)(2,1)}), bf16[4,512,256]{2,1,0:T(8,128)(2,1)S(1)}, u32[]{:S(2)}, u32[]{:S(2)}) async-start(bf16[4,512,256]{2,1,0:T(8,128)(2,1)} %pad_maximum_fusion.1), calls=%async_computation.1 | async-start | bytes 2097152 | tf_op jit(solution)/shard_map/all_to_all | solution.py:365
  47.7 9.9 %all-to-all-done.1 = bf16[4,512,256]{2,1,0:T(8,128)(2,1)S(1)} async-done(((bf16[4,512,256]{2,1,0:T(8,128)(2,1)}), bf16[4,512,256]{2,1,0:T(8,128)(2,1)S(1)}, u32[]{:S(2)}, u32[]{:S(2)}) %all-to-all-start.1) | async-done | bytes 1048608 | tf_op jit(solution)/shard_map/all_to_all | solution.py:365
  57.6 1.9 %collective-permute-start = (bf16[2048,256]{1,0:T(8,128)(2,1)S(1)}, bf16[2048,256]{1,0:T(8,128)(2,1)S(1)}, u32[]{:S(2)}, u32[]{:S(2)}) collective-permute-start(bf16[2048,256]{1,0:T(8,128)(2,1)S(1)} %bitcast.56), channel_id=1, source_target_pairs={{0,1},{1,2},{2,3},{3,4},{4,5},{5,6},{6,7},{7,8},{8,9},{9,10},{10,1... | collective-permute-start | bytes 3145736 | tf_op jit(solution)/shard_map/ppermute | solution.py:368
  60.0 7.8 %own_forward.1 = (f32[4,2,512]{2,1,0:T(2,128)S(1)}, f32[4,128,512]{2,1,0:T(8,128)S(1)}) custom-call(s32[9]{0:T(128)S(1)} %pad_add_fusion.scalars, s32[4,1,512]{2,1,0:T(1,128)S(1)} %bitcast.59, bf16[4,256,512]{2,1,0:T(8,128)(2,1)S(1)} %all-to-all-done.qd_ref, bf16[2048,256]{1,0:T(8,128)(2,1)S(1)} %bitcast.57), custom_call_target="tpu_custom_call" | custom-call | flops 2000000000 | bytes 4194304 | tf_op jit(solution)/shard_map/own_forward/pallas_call | solution.py:290
  67.8 5.9 %collective-permute-done.kv_ref = bf16[2048,256]{1,0:T(8,128)(2,1)S(1)} collective-permute-done((bf16[2048,256]{1,0:T(8,128)(2,1)S(1)}, bf16[2048,256]{1,0:T(8,128)(2,1)S(1)}, u32[]{:S(2)}, u32[]{:S(2)}) %collective-permute-start) | collective-permute-done | bytes 1048608 | tf_op jit(solution)/shard_map/ppermute | solution.py:368
  73.7 8.3 %before_part.1 = (bf16[4,128,512]{2,1,0:T(8,128)(2,1)}, bf16[2048,256]{1,0:T(8,128)(2,1)}, f32[4,2,512]{2,1,0:T(2,128)S(1)}, f32[4,128,512]{2,1,0:T(8,128)S(1)}) custom-call(s32[9]{0:T(128)S(1)} %pad_add_fusion.scalars, s32[4,1,512]{2,1,0:T(1,128)S(1)} %bitcast.60, bf16[4,256,512]{2,1,0:T(8,128)(2,1)S(1)} %all-to-all-done.qd_ref, ...), custom_call_target="tpu_custom_call" | custom-call | flops 2000000000 | bytes 4194304 | tf_op jit(solution)/shard_map/before_part/pallas_call | solution.py:290
  83.0 1.9 %collective-permute-start.1 = (bf16[2048,256]{1,0:T(8,128)(2,1)}, bf16[2048,256]{1,0:T(8,128)(2,1)}, u32[]{:S(2)}, u32[]{:S(2)}) collective-permute-start(bf16[2048,256]{1,0:T(8,128)(2,1)} %get-tuple-element.32), channel_id=1, source_target_pairs={{1,0},{2,1},{3,2},{4,3},{5,4},{6,5},{7,6},{8,7},{9,8},{10,9},{11,1... | collective-permute-start | bytes 3145736 | tf_op jit(solution)/shard_map/ppermute | solution.py:383
  84.9 5.6 %all-to-all-start.2 = ((bf16[4,128,512]{2,1,0:T(8,128)(2,1)}), bf16[4,128,512]{2,1,0:T(8,128)(2,1)}, u32[]{:S(2)}, u32[]{:S(2)}) async-start(bf16[4,128,512]{2,1,0:T(8,128)(2,1)} %get-tuple-element.31), calls=%async_computation.2 | async-start | bytes 1048576 | tf_op jit(solution)/shard_map/all_to_all | solution.py:384
  90.5 1.2 copy-done.1
  91.7 10.4 %own_backward.1 = (bf16[4,128,512]{2,1,0:T(8,128)(2,1)}, bf16[2048,256]{1,0:T(8,128)(2,1)S(1)}) custom-call(s32[9]{0:T(128)S(1)} %pad_add_fusion.scalars, s32[4,1,512]{2,1,0:T(1,128)S(1)} %bitcast.61, bf16[4,256,512]{2,1,0:T(8,128)(2,1)S(1)} %all-to-all-done.qd_ref, bf16[2048,256]{1,0:T(8,128)(2,1)S(1)} %bitcast.58, ...), custom_call_target="tpu_custom_call" | custom-call | flops 3000000000 | bytes 4194304 | tf_op jit(solution)/shard_map/own_backward/pallas_call | solution.py:290
  102.1 2.5 %add_convert_fusion = bf16[2048,256]{1,0:T(8,128)(2,1)} fusion(bf16[2048,256]{1,0:T(8,128)(2,1)} %collective-permute-done.1, bf16[2048,256]{1,0:T(8,128)(2,1)S(1)} %get-tuple-element.38), kind=kLoop, calls=%fused_computation | loop fusion | flops 2097152 | bytes 3145728 | tf_op jit(solution)/shard_map/convert_element_type | solution.py:387
  104.6 4.8 %all-to-all-start.4 = ((bf16[4,4,128,256]{3,2,1,0:T(8,128)(2,1)}), bf16[4,4,128,256]{3,2,1,0:T(8,128)(2,1)S(1)}, u32[]{:S(2)}, u32[]{:S(2)}) async-start(bf16[4,4,128,256]{3,2,1,0:T(8,128)(2,1)} %bitcast.13), calls=%async_computation.4 | async-start | bytes 2097152 | tf_op jit(solution)/shard_map/all_to_all | solution.py:388
  111.4 9.5 %all-to-all-done.4 = bf16[4,4,128,256]{3,2,1,0:T(8,128)(2,1)S(1)} async-done(((bf16[4,4,128,256]{3,2,1,0:T(8,128)(2,1)}), bf16[4,4,128,256]{3,2,1,0:T(8,128)(2,1)S(1)}, u32[]{:S(2)}, u32[]{:S(2)}) %all-to-all-start.4) | async-done | bytes 1048608 | tf_op jit(solution)/shard_map/all_to_all | solution.py:388
  120.9 4.9 %all-to-all-start.3 = ((bf16[4,128,512]{2,1,0:T(8,128)(2,1)}), bf16[4,128,512]{2,1,0:T(8,128)(2,1)S(1)}, u32[]{:S(2)}, u32[]{:S(2)}) async-start(bf16[4,128,512]{2,1,0:T(8,128)(2,1)} %get-tuple-element.37), calls=%async_computation.3 | async-start | bytes 1048576 | tf_op jit(solution)/shard_map/all_to_all | solution.py:400
  126.1 4.1 %collective-permute-start.4 = (bf16[2,128,256]{2,1,0:T(8,128)(2,1)S(1)}, bf16[2,128,256]{2,1,0:T(8,128)(2,1)S(1)}, u32[]{:S(2)}, u32[]{:S(2)}) collective-permute-start(bf16[2,128,256]{2,1,0:T(8,128)(2,1)S(1)} %pad_maximum_fusion.7), channel_id=1, source_target_pairs={{0,96},{32,0},{64,32},{96,64},{1,97},{33,1},{65,33},{97,65},{2,98}... | collective-permute-start | bytes 393224 | tf_op jit(solution)/shard_map/ppermute | solution.py:397
  130.3 5.7 %collective-permute-start.3 = (bf16[2,128,256]{2,1,0:T(8,128)(2,1)S(1)}, bf16[2,128,256]{2,1,0:T(8,128)(2,1)S(1)}, u32[]{:S(2)}, u32[]{:S(2)}) collective-permute-start(bf16[2,128,256]{2,1,0:T(8,128)(2,1)S(1)} %pad_maximum_fusion.6), channel_id=1, source_target_pairs={{0,32},{32,64},{64,96},{96,0},{1,33},{33,65},{65,97},{97,1},{2,34}... | collective-permute-start | bytes 393224 | tf_op jit(solution)/shard_map/ppermute | solution.py:397
  136.0 7.6 %collective-permute-start.2 = (bf16[2,128,256]{2,1,0:T(8,128)(2,1)S(1)}, bf16[2,128,256]{2,1,0:T(8,128)(2,1)S(1)}, u32[]{:S(2)}, u32[]{:S(2)}) collective-permute-start(bf16[2,128,256]{2,1,0:T(8,128)(2,1)S(1)} %pad_maximum_fusion.5), channel_id=1, source_target_pairs={{0,64},{32,96},{64,0},{96,32},{1,65},{33,97},{65,1},{97,33},{2,66}... | collective-permute-start | bytes 393224 | tf_op jit(solution)/shard_map/ppermute | solution.py:397
  144.3 9.9 %collective-permute-done.3 = bf16[2,128,256]{2,1,0:T(8,128)(2,1)S(1)} collective-permute-done((bf16[2,128,256]{2,1,0:T(8,128)(2,1)S(1)}, bf16[2,128,256]{2,1,0:T(8,128)(2,1)S(1)}, u32[]{:S(2)}, u32[]{:S(2)}) %collective-permute-start.3) | collective-permute-done | bytes 131104 | tf_op jit(solution)/shard_map/ppermute | solution.py:397
  154.2 8.7 %collective-permute-done.2 = bf16[2,128,256]{2,1,0:T(8,128)(2,1)S(1)} collective-permute-done((bf16[2,128,256]{2,1,0:T(8,128)(2,1)S(1)}, bf16[2,128,256]{2,1,0:T(8,128)(2,1)S(1)}, u32[]{:S(2)}, u32[]{:S(2)}) %collective-permute-start.2) | collective-permute-done | bytes 131104 | tf_op jit(solution)/shard_map/ppermute | solution.py:397
  (46 shorter events, 7.1 us)
Async XLA Ops:
  0.6 1.3 copy-start.2
  3.2 5.0 %copy-start.3 = (bf16[128,256]{1,0:T(8,128)(2,1)S(1)}, bf16[128,256]{1,0:T(8,128)(2,1)}, u32[]{:S(2)}) copy-start(bf16[128,256]{1,0:T(8,128)(2,1)} %param.6) | copy-start | bytes 196612
  3.2 5.0 %copy-start.4 = (bf16[128,256]{1,0:T(8,128)(2,1)S(1)}, bf16[128,256]{1,0:T(8,128)(2,1)}, u32[]{:S(2)}) copy-start(bf16[128,256]{1,0:T(8,128)(2,1)} %param.7) | copy-start | bytes 196612
  3.2 37.4 %all-to-all-start = ((bf16[4,256,512]{2,1,0:T(8,128)(2,1)}), bf16[4,256,512]{2,1,0:T(8,128)(2,1)S(1)}, u32[]{:S(2)}, u32[]{:S(2)}) async-start(bf16[4,256,512]{2,1,0:T(8,128)(2,1)} %pad_maximum_fusion), calls=%async_computation | async-start | bytes 2097152 | tf_op jit(solution)/shard_map/all_to_all | solution.py:353
  41.7 5.8 %copy-start.5 = (s32[64]{0:T(128)S(1)}, s32[64]{0:T(128)}, u32[]{:S(2)}) copy-start(s32[64]{0:T(128)} %param.9) | copy-start | bytes 772
  41.7 15.9 %all-to-all-start.1 = ((bf16[4,512,256]{2,1,0:T(8,128)(2,1)}), bf16[4,512,256]{2,1,0:T(8,128)(2,1)S(1)}, u32[]{:S(2)}, u32[]{:S(2)}) async-start(bf16[4,512,256]{2,1,0:T(8,128)(2,1)} %pad_maximum_fusion.1), calls=%async_computation.1 | async-start | bytes 2097152 | tf_op jit(solution)/shard_map/all_to_all | solution.py:365
  57.6 16.1 %collective-permute-start = (bf16[2048,256]{1,0:T(8,128)(2,1)S(1)}, bf16[2048,256]{1,0:T(8,128)(2,1)S(1)}, u32[]{:S(2)}, u32[]{:S(2)}) collective-permute-start(bf16[2048,256]{1,0:T(8,128)(2,1)S(1)} %bitcast.56), channel_id=1, source_target_pairs={{0,1},{1,2},{2,3},{3,4},{4,5},{5,6},{6,7},{7,8},{8,9},{9,10},{10,1... | collective-permute-start | bytes 3145736 | tf_op jit(solution)/shard_map/ppermute | solution.py:368
  82.0 1.0 copy-start
  83.0 19.1 %collective-permute-start.1 = (bf16[2048,256]{1,0:T(8,128)(2,1)}, bf16[2048,256]{1,0:T(8,128)(2,1)}, u32[]{:S(2)}, u32[]{:S(2)}) collective-permute-start(bf16[2048,256]{1,0:T(8,128)(2,1)} %get-tuple-element.32), channel_id=1, source_target_pairs={{1,0},{2,1},{3,2},{4,3},{5,4},{6,5},{7,6},{8,7},{9,8},{10,9},{11,1... | collective-permute-start | bytes 3145736 | tf_op jit(solution)/shard_map/ppermute | solution.py:383
  84.9 17.2 %all-to-all-start.2 = ((bf16[4,128,512]{2,1,0:T(8,128)(2,1)}), bf16[4,128,512]{2,1,0:T(8,128)(2,1)}, u32[]{:S(2)}, u32[]{:S(2)}) async-start(bf16[4,128,512]{2,1,0:T(8,128)(2,1)} %get-tuple-element.31), calls=%async_computation.2 | async-start | bytes 1048576 | tf_op jit(solution)/shard_map/all_to_all | solution.py:384
  90.5 1.2 copy-start.1
  104.6 16.3 %all-to-all-start.4 = ((bf16[4,4,128,256]{3,2,1,0:T(8,128)(2,1)}), bf16[4,4,128,256]{3,2,1,0:T(8,128)(2,1)S(1)}, u32[]{:S(2)}, u32[]{:S(2)}) async-start(bf16[4,4,128,256]{3,2,1,0:T(8,128)(2,1)} %bitcast.13), calls=%async_computation.4 | async-start | bytes 2097152 | tf_op jit(solution)/shard_map/all_to_all | solution.py:388
  120.9 22.7 %all-to-all-start.3 = ((bf16[4,128,512]{2,1,0:T(8,128)(2,1)}), bf16[4,128,512]{2,1,0:T(8,128)(2,1)S(1)}, u32[]{:S(2)}, u32[]{:S(2)}) async-start(bf16[4,128,512]{2,1,0:T(8,128)(2,1)} %get-tuple-element.37), calls=%async_computation.3 | async-start | bytes 1048576 | tf_op jit(solution)/shard_map/all_to_all | solution.py:400
  126.1 18.2 %collective-permute-start.4 = (bf16[2,128,256]{2,1,0:T(8,128)(2,1)S(1)}, bf16[2,128,256]{2,1,0:T(8,128)(2,1)S(1)}, u32[]{:S(2)}, u32[]{:S(2)}) collective-permute-start(bf16[2,128,256]{2,1,0:T(8,128)(2,1)S(1)} %pad_maximum_fusion.7), channel_id=1, source_target_pairs={{0,96},{32,0},{64,32},{96,64},{1,97},{33,1},{65,33},{97,65},{2,98}... | collective-permute-start | bytes 393224 | tf_op jit(solution)/shard_map/ppermute | solution.py:397
  130.3 23.9 %collective-permute-start.3 = (bf16[2,128,256]{2,1,0:T(8,128)(2,1)S(1)}, bf16[2,128,256]{2,1,0:T(8,128)(2,1)S(1)}, u32[]{:S(2)}, u32[]{:S(2)}) collective-permute-start(bf16[2,128,256]{2,1,0:T(8,128)(2,1)S(1)} %pad_maximum_fusion.6), channel_id=1, source_target_pairs={{0,32},{32,64},{64,96},{96,0},{1,33},{33,65},{65,97},{97,1},{2,34}... | collective-permute-start | bytes 393224 | tf_op jit(solution)/shard_map/ppermute | solution.py:397
  136.0 27.0 %collective-permute-start.2 = (bf16[2,128,256]{2,1,0:T(8,128)(2,1)S(1)}, bf16[2,128,256]{2,1,0:T(8,128)(2,1)S(1)}, u32[]{:S(2)}, u32[]{:S(2)}) collective-permute-start(bf16[2,128,256]{2,1,0:T(8,128)(2,1)S(1)} %pad_maximum_fusion.5), channel_id=1, source_target_pairs={{0,64},{32,96},{64,0},{96,32},{1,65},{33,97},{65,1},{97,33},{2,66}... | collective-permute-start | bytes 393224 | tf_op jit(solution)/shard_map/ppermute | solution.py:397

commit v4 on v3

--- a/solution.py
+++ b/solution.py
@@ -272,7 +272,7 @@
         sweep(low, full_low, gradient_step(limits), BACK_GROUP)
         sweep(full_low, full_high, gradient_step(None), BACK_GROUP)
         sweep(full_high, high, gradient_step(limits), BACK_GROUP)
-        store_rows(grad_query_ref, chunk, (grad_query_t[...] * SCALE).T)
+        store_rows(grad_query_ref, (chunk - scalars[9]) & 3, (grad_query_t[...] * SCALE).T)
         return 0
 
     lax.fori_loop(0, 4, chunk_step, 0)
@@ -285,7 +285,7 @@
     lax.fori_loop(first, TILES, store, 0)
 
 
-def call(kernel, name, gflops, outs, scratch, *args):
+def call(kernel, name, gflops, megabytes, outs, scratch, *args):
     vmem = pl.BlockSpec(memory_space=pltpu.VMEM)
     return pl.pallas_call(
         kernel,
@@ -293,7 +293,7 @@
         in_specs=[pl.BlockSpec(memory_space=pltpu.SMEM)] + [vmem] * (len(args) - 1),
         out_specs=tuple(vmem for _ in outs),
         scratch_shapes=[pltpu.VMEM(shape, dtype) for shape, dtype in scratch],
-        compiler_params=pltpu.CompilerParams(vmem_limit_bytes=36 << 20),
+        compiler_params=pltpu.CompilerParams(vmem_limit_bytes=megabytes << 20),
         cost_estimate=pl.CostEstimate(
             flops=gflops * 10**9, bytes_accessed=4 << 20, transcendentals=2 * 10**6
         ),
@@ -314,14 +314,14 @@
 
 def run_own_forward(scalars, begin, qd, kv):
     return call(
-        own_forward, "own_forward", 2, (STATS, ACROSS), (TURNED, SQUARE, EIGHT, EIGHT),
+        own_forward, "own_forward", 2, 12, (STATS, ACROSS), (TURNED, SQUARE, EIGHT, EIGHT),
         scalars, begin, qd, kv,
     )
 
 
 def run_before_part(scalars, begin, qd, kv, stats, out):
     return call(
-        before_part, "before_part", 2, (RESULT, GRADS, STATS, ACROSS),
+        before_part, "before_part", 2, 18, (RESULT, GRADS, STATS, ACROSS),
         (TURNED, TURNED, SQUARE, SUMS, SUMS, FLAT, EIGHT, EIGHT),
         scalars, begin, qd, kv, stats, out,
     )
@@ -329,9 +329,60 @@
 
 def run_own_backward(scalars, begin, qd, kv, stats, grad_query):
     return call(
-        own_backward, "own_backward", 3, (RESULT, GRADS), (TURNED, SUMS, SUMS, FLAT),
+        own_backward, "own_backward", 3, 14, (RESULT, GRADS), (TURNED, SUMS, SUMS, FLAT),
         scalars, begin, qd, kv, stats, grad_query,
     )
+
+
+def small(kernel, name, outs, scalar, *args):
+    vmem = pl.BlockSpec(memory_space=pltpu.VMEM)
+    smem = [pl.BlockSpec(memory_space=pltpu.SMEM)] if scalar is not None else []
+    return pl.pallas_call(
+        kernel,
+        out_shape=tuple(jax.ShapeDtypeStruct(shape, dtype) for shape, dtype in outs),
+        in_specs=smem + [vmem] * len(args),
+        out_specs=tuple(vmem for _ in outs),
+        compiler_params=pltpu.CompilerParams(vmem_limit_bytes=8 << 20),
+        cost_estimate=pl.CostEstimate(flops=10**6, bytes_accessed=2 << 20, transcendentals=0),
+        name=name,
+    )(*([scalar] if scalar is not None else []), *args)
+
+
+def pack(queries, output_gradient, keys, values):
+    def kernel(q_ref, d_ref, k_ref, v_ref, qd_ref, kv_ref):
+        for d in range(4):
+            span = slice(d * ROWS, (d + 1) * ROWS)
+            qd_ref[d, :CHUNK] = q_ref[:, span]
+            qd_ref[d, CHUNK:] = d_ref[:, span]
+        for head in range(2):
+            here = slice(head * HEAD_SIZE, (head + 1) * HEAD_SIZE)
+            kv_ref[:, 2 * head * HEAD_SIZE : (2 * head + 1) * HEAD_SIZE] = k_ref[:, here]
+            kv_ref[:, (2 * head + 1) * HEAD_SIZE : (2 * head + 2) * HEAD_SIZE] = v_ref[:, here]
+
+    outs = (((4, 2 * CHUNK, ROWS), BF16), ((CHUNK, 4 * HEAD_SIZE), BF16))
+    return small(kernel, "pack", outs, None, queries, output_gradient, keys, values)
+
+
+def join(y, *pieces):
+    def kernel(y_ref, *refs):
+        out = refs[-1]
+        for step in range(4):
+            group = (y_ref[0] - step) & 3
+            out[:, pl.ds(pl.multiple_of(group * ROWS, ROWS), ROWS)] = refs[step][...]
+
+    return small(kernel, "join", (((CHUNK, 4 * ROWS), BF16),), y, *pieces)[0]
+
+
+def last_sum(grad):
+    def kernel(grad_ref, keys_ref, values_ref):
+        for head in range(2):
+            total = sum(grad_ref[i, head].astype(F32) for i in range(4)).astype(BF16)
+            here = slice(head * HEAD_SIZE, (head + 1) * HEAD_SIZE)
+            keys_ref[:, here] = total[:, :HEAD_SIZE]
+            values_ref[:, here] = total[:, HEAD_SIZE:]
+
+    outs = (((CHUNK, 2 * HEAD_SIZE), BF16),) * 2
+    return small(kernel, "last_sum", outs, None, grad)
 
 
 def columns(value, index, count):
@@ -341,24 +392,12 @@
 
 def per_device(queries, key_projection, value_projection, output_gradient, doc_lengths):
     z_hi = lax.axis_index("z_hi").astype(jnp.int32)
+    y = lax.axis_index("y").astype(jnp.int32)
     block = lax.axis_index(BLOCK_AXES).astype(jnp.int32)
     blocks = lax.axis_size(BLOCK_AXES)
     own_start = block * SPAN
-    qd = jnp.stack(
-        [
-            jnp.concatenate([columns(queries, d, 4), columns(output_gradient, d, 4)], axis=0)
-            for d in range(4)
-        ]
-    )
+    qd, kv = pack(queries, output_gradient, key_projection, value_projection)
     qd = lax.all_to_all(qd, "y", split_axis=0, concat_axis=0, tiled=True)
-    kv = jnp.concatenate(
-        [
-            columns(part, head, 2)
-            for head in range(2)
-            for part in (key_projection, value_projection)
-        ],
-        axis=1,
-    )
     kv = lax.all_gather(kv, "z_hi", axis=0, tiled=True)
     qd, kv = lax.optimization_barrier((qd, kv))
     first, second = columns(kv, 0, 2), columns(kv, 1, 2)
@@ -372,7 +411,7 @@
     chunk_start = (4 * jnp.arange(4, dtype=jnp.int32) + z_hi) * CHUNK + own_start
     position = (chunk_start[:, None] + jnp.arange(CHUNK, dtype=jnp.int32)[None, :])[..., None]
     begin = jnp.max(jnp.where(starts <= position, starts, 0), axis=2).astype(jnp.int32) - own_start
-    scalars = jnp.concatenate([begin[:, 0], begin[:, -1], z_hi[None]])
+    scalars = jnp.concatenate([begin[:, 0], begin[:, -1], z_hi[None], y[None]])
     begin = jnp.tile(begin, (1, HEADS)).reshape(4, 1, ROWS)
 
     stats, out = run_own_forward(scalars, begin, qd, kv_own)
@@ -389,25 +428,19 @@
         grad_own.reshape(4, 4, CHUNK, 2 * HEAD_SIZE), "y", split_axis=0, concat_axis=0, tiled=True
     )
 
-    def part(step):
-        mine = lax.dynamic_index_in_dim(grad, (z_hi + step) % 4, axis=1, keepdims=False).astype(F32)
-        return jnp.stack([mine[0] + mine[1], mine[2] + mine[3]])
-
-    arrived = [
-        lax.ppermute(part(step).astype(BF16), "z_hi", [(i, (i + step) % 4) for i in range(4)])
-        for step in (2, 1, 3)
+    grad = grad.astype(F32)
+    grad = jnp.stack([grad[0] + grad[1], grad[2] + grad[3]], axis=1).astype(BF16)
+    grad, grad_query = lax.optimization_barrier((grad, grad_query))
+    grad = lax.all_to_all(grad, "z_hi", split_axis=0, concat_axis=0, tiled=True)
+    pieces = [grad_query[0]] + [
+        lax.ppermute(grad_query[step], "y", [(i, (i + step) % 4) for i in range(4)])
+        for step in (1, 2, 3)
     ]
-    grad_query = lax.all_to_all(grad_query, "y", split_axis=0, concat_axis=0, tiled=True)
-    grad_query, *arrived = lax.optimization_barrier((grad_query, *arrived))
-    grad = part(0)
-    for piece in arrived:
-        grad += piece.astype(F32)
-    grad = grad.astype(BF16)
-    keys_gradient = jnp.concatenate([grad[0, :, :HEAD_SIZE], grad[1, :, :HEAD_SIZE]], axis=1)
-    values_gradient = jnp.concatenate([grad[0, :, HEAD_SIZE:], grad[1, :, HEAD_SIZE:]], axis=1)
+    grad_queries = join(y[None], *pieces)
+    keys_gradient, values_gradient = last_sum(grad)
     return (
         jnp.concatenate([context[i] for i in range(4)], axis=1),
-        jnp.concatenate([grad_query[i] for i in range(4)], axis=1),
+        grad_queries,
         keys_gradient,
         values_gradient,
     )

time: 166 us -> 162 us (0.976)
  the two profiles are of different devices: /device:TPU:12 before, /device:TPU:3 now
where the time goes in v4:
time: 162 us; the launch traced here: 161 us
  blocking collectives  49.4 us (30%)
  starting transfers between devices  36.3 us (22%)
  waiting for transfers between devices  33.7 us (21%)
  Pallas kernels  27.5 us (17%)
  local copies, waits for them, and re-layouts  8.13 us (5%)
  other arithmetic  4.99 us (3%)
    all_gather x1, blocking collectives, per_device(): kv = lax.all_gather(kv, 'z_hi', axis=0, tiled=True)  30.8 us
    pallas_call x3, Pallas kernels, call(): pl.pallas_call(kernel, out_shape=tuple((jax.ShapeDtypeStruct(shape, dtype...  24.9 us
    all_to_all x1, blocking collectives, per_device(): lax.all_to_all(grad_own.reshape(4, 4, CHUNK, 2 * HEAD_SIZE), 'y', split_a...  18.6 us
    all_to_all x1, waiting for transfers between devices, per_device(): grad = lax.all_to_all(grad, 'z_hi', split_axis=0, concat_axis=0, tiled=True)  13.1 us
    all_to_all x1, waiting for transfers between devices, per_device(): lax.all_to_all(jnp.stack([first, first, second, second]), 'y', split_axis...  10.1 us
    ppermute x1, starting transfers between devices, per_device(): lax.ppermute(kv_own, BLOCK_AXES, [(i, i + 1) for i in range(blocks - 1)])  8.78 us
    ppermute x3, starting transfers between devices, per_device(): lax.ppermute(grad_query[step], 'y', [(i, (i + step) % 4) for i in range(4)])  7.81 us
    unnamed x18, local copies, waits for them, and re-layouts  6.75 us
  transfers between devices with their start and end apart: 9, of which 6 were waited for; matrix products, arithmetic and copies ran while one was open for 2% of the time, Pallas kernels for 9%

profile of v4, /device:TPU:3, one launch (start us, length us, event | category | flops | bytes accessed | tf_op | source)
XLA Modules:
  0.0 160.9 jit_solution(2063664264741820946)
XLA Ops:
  4.4 1.1 pack.1
  5.5 4.2 %all-to-all-start = ((bf16[4,256,512]{2,1,0:T(8,128)(2,1)}), bf16[4,256,512]{2,1,0:T(8,128)(2,1)S(1)}, u32[]{:S(2)}, u32[]{:S(2)}) async-start(bf16[4,256,512]{2,1,0:T(8,128)(2,1)} %get-tuple-element.26), calls=%async_computation | async-start | bytes 2097152 | tf_op jit(solution)/shard_map/all_to_all | solution.py:400
  9.7 30.8 %all_gather.3 = bf16[512,512]{1,0:T(8,128)(2,1)S(1)} all-gather(bf16[128,512]{1,0:T(8,128)(2,1)S(1)} %get-tuple-element.27), channel_id=1, replica_groups=mesh['y'=4,'z_hi'=4,'z_lo'=4,'x'=4,'core'=2] {'z_hi'}, dimensions={0}, use_global_device_ids=true | all-gather | bytes 655360 | tf_op jit(solution)/shard_map/all_gather | solution.py:401
  40.6 1.1 pad_maximum_fusion
  41.7 3.5 %all-to-all-start.1 = ((bf16[4,512,256]{2,1,0:T(8,128)(2,1)}), bf16[4,512,256]{2,1,0:T(8,128)(2,1)S(1)}, u32[]{:S(2)}, u32[]{:S(2)}) async-start(bf16[4,512,256]{2,1,0:T(8,128)(2,1)} %pad_maximum_fusion), calls=%async_computation.1 | async-start | bytes 2097152 | tf_op jit(solution)/shard_map/all_to_all | solution.py:404
  45.3 10.1 %all-to-all-done.1 = bf16[4,512,256]{2,1,0:T(8,128)(2,1)S(1)} async-done(((bf16[4,512,256]{2,1,0:T(8,128)(2,1)}), bf16[4,512,256]{2,1,0:T(8,128)(2,1)S(1)}, u32[]{:S(2)}, u32[]{:S(2)}) %all-to-all-start.1) | async-done | bytes 1048608 | tf_op jit(solution)/shard_map/all_to_all | solution.py:404
  55.4 8.8 %collective-permute-start = (bf16[2048,256]{1,0:T(8,128)(2,1)S(1)}, bf16[2048,256]{1,0:T(8,128)(2,1)S(1)}, u32[]{:S(2)}, u32[]{:S(2)}) collective-permute-start(bf16[2048,256]{1,0:T(8,128)(2,1)S(1)} %bitcast.31), channel_id=1, source_target_pairs={{0,1},{1,2},{2,3},{3,4},{4,5},{5,6},{6,7},{7,8},{8,9},{9,10},{10,1... | collective-permute-start | bytes 3145736 | tf_op jit(solution)/shard_map/ppermute | solution.py:407
  64.7 6.3 %own_forward.1 = (f32[4,2,512]{2,1,0:T(2,128)S(1)}, f32[4,128,512]{2,1,0:T(8,128)S(1)}) custom-call(s32[10]{0:T(128)S(1)} %pad_add_fusion.scalars, s32[4,1,512]{2,1,0:T(1,128)S(1)} %bitcast.34, bf16[4,256,512]{2,1,0:T(8,128)(2,1)S(1)} %all-to-all-done.qd_ref, bf16[2048,256]{1,0:T(8,128)(2,1)S(1)} %bitcast.32), custom_call_target="tpu_custom_call" | custom-call | flops 2000000000 | bytes 4194304 | tf_op jit(solution)/shard_map/own_forward/pallas_call | solution.py:290
  71.0 4.9 %collective-permute-done.kv_ref = bf16[2048,256]{1,0:T(8,128)(2,1)S(1)} collective-permute-done((bf16[2048,256]{1,0:T(8,128)(2,1)S(1)}, bf16[2048,256]{1,0:T(8,128)(2,1)S(1)}, u32[]{:S(2)}, u32[]{:S(2)}) %collective-permute-start) | collective-permute-done | bytes 1048608 | tf_op jit(solution)/shard_map/ppermute | solution.py:407
  75.9 10.9 %before_part.1 = (bf16[4,128,512]{2,1,0:T(8,128)(2,1)}, bf16[2048,256]{1,0:T(8,128)(2,1)}, f32[4,2,512]{2,1,0:T(2,128)S(1)}, f32[4,128,512]{2,1,0:T(8,128)S(1)}) custom-call(s32[10]{0:T(128)S(1)} %pad_add_fusion.scalars, s32[4,1,512]{2,1,0:T(1,128)S(1)} %bitcast.35, bf16[4,256,512]{2,1,0:T(8,128)(2,1)S(1)} %all-to-all-done.qd_ref, ...), custom_call_target="tpu_custom_call" | custom-call | flops 2000000000 | bytes 4194304 | tf_op jit(solution)/shard_map/before_part/pallas_call | solution.py:290
  87.8 3.3 %collective-permute-start.1 = (bf16[2048,256]{1,0:T(8,128)(2,1)}, bf16[2048,256]{1,0:T(8,128)(2,1)}, u32[]{:S(2)}, u32[]{:S(2)}) collective-permute-start(bf16[2048,256]{1,0:T(8,128)(2,1)} %get-tuple-element.36), channel_id=1, source_target_pairs={{1,0},{2,1},{3,2},{4,3},{5,4},{6,5},{7,6},{8,7},{9,8},{10,9},{11,1... | collective-permute-start | bytes 3145736 | tf_op jit(solution)/shard_map/ppermute | solution.py:422
  91.2 4.2 %all-to-all-start.2 = ((bf16[4,128,512]{2,1,0:T(8,128)(2,1)}), bf16[4,128,512]{2,1,0:T(8,128)(2,1)}, u32[]{:S(2)}, u32[]{:S(2)}) async-start(bf16[4,128,512]{2,1,0:T(8,128)(2,1)} %get-tuple-element.35), calls=%async_computation.2 | async-start | bytes 1048576 | tf_op jit(solution)/shard_map/all_to_all | solution.py:423
  95.4 1.2 copy-done.7
  96.6 7.6 %own_backward.1 = (bf16[4,128,512]{2,1,0:T(8,128)(2,1)S(1)}, bf16[2048,256]{1,0:T(8,128)(2,1)S(1)}) custom-call(s32[10]{0:T(128)S(1)} %pad_add_fusion.scalars, s32[4,1,512]{2,1,0:T(1,128)S(1)} %bitcast.36, bf16[4,256,512]{2,1,0:T(8,128)(2,1)S(1)} %all-to-all-done.qd_ref, bf16[2048,256]{1,0:T(8,128)(2,1)S(1)} %bitcast.33, ...), custom_call_target="tpu_custom_call" | custom-call | flops 3000000000 | bytes 4194304 | tf_op jit(solution)/shard_map/own_backward/pallas_call | solution.py:290
  105.3 1.5 add_convert_fusion
  106.8 18.6 %all_to_all.25 = bf16[4,4,128,256]{3,2,1,0:T(8,128)(2,1)S(1)} all-to-all(bf16[4,4,128,256]{3,2,1,0:T(8,128)(2,1)S(1)} %bitcast.37), channel_id=1, replica_groups=mesh['y'=4,'z_hi'=4,'z_lo'=4,'x'=4,'core'=2] {'y'}, dimensions={0} | all-to-all | bytes 2097152 | tf_op jit(solution)/shard_map/all_to_all | solution.py:427
  126.6 4.5 %all-to-all-start.4 = ((bf16[4,2,128,256]{3,2,1,0:T(8,128)(2,1)}), bf16[4,2,128,256]{3,2,1,0:T(8,128)(2,1)S(1)}, u32[]{:S(2)}, u32[]{:S(2)}) async-start(bf16[4,2,128,256]{3,2,1,0:T(8,128)(2,1)} %pad_maximum_fusion.2), calls=%async_computation.4 | async-start | bytes 1048576 | tf_op jit(solution)/shard_map/all_to_all | solution.py:434
  131.1 1.1 slice_bitcast_fusion.9
  132.3 2.8 %collective-permute-start.4 = (bf16[128,512]{1,0:T(8,128)(2,1)S(1)}, bf16[128,512]{1,0:T(8,128)(2,1)S(1)}, u32[]{:S(2)}, u32[]{:S(2)}) collective-permute-start(bf16[128,512]{1,0:T(8,128)(2,1)S(1)} %get-tuple-element.52), channel_id=1, source_target_pairs={{0,384},{128,0},{256,128},{384,256},{1,385},{129,1},{257,129},{385... | collective-permute-start | bytes 393224 | tf_op jit(solution)/shard_map/ppermute | solution.py:436
  135.1 3.1 %collective-permute-start.3 = (bf16[128,512]{1,0:T(8,128)(2,1)S(1)}, bf16[128,512]{1,0:T(8,128)(2,1)S(1)}, u32[]{:S(2)}, u32[]{:S(2)}) collective-permute-start(bf16[128,512]{1,0:T(8,128)(2,1)S(1)} %get-tuple-element.53), channel_id=1, source_target_pairs={{0,256},{128,384},{256,0},{384,128},{1,257},{129,385},{257,1},{385... | collective-permute-start | bytes 393224 | tf_op jit(solution)/shard_map/ppermute | solution.py:436
  138.2 1.9 %collective-permute-start.2 = (bf16[128,512]{1,0:T(8,128)(2,1)S(1)}, bf16[128,512]{1,0:T(8,128)(2,1)S(1)}, u32[]{:S(2)}, u32[]{:S(2)}) collective-permute-start(bf16[128,512]{1,0:T(8,128)(2,1)S(1)} %get-tuple-element.54), channel_id=1, source_target_pairs={{0,128},{128,256},{256,384},{384,0},{1,129},{129,257},{257,385},{3... | collective-permute-start | bytes 393224 | tf_op jit(solution)/shard_map/ppermute | solution.py:436
  141.0 1.3 collective-permute-done.3.refs_2_
  142.4 3.9 %collective-permute-done.2.refs_1_ = bf16[128,512]{1,0:T(8,128)(2,1)S(1)} collective-permute-done((bf16[128,512]{1,0:T(8,128)(2,1)S(1)}, bf16[128,512]{1,0:T(8,128)(2,1)S(1)}, u32[]{:S(2)}, u32[]{:S(2)}) %collective-permute-start.2) | collective-permute-done | bytes 131104 | tf_op jit(solution)/shard_map/ppermute | solution.py:436
  147.1 13.1 %all-to-all-done.4.grad_ref = bf16[4,2,128,256]{3,2,1,0:T(8,128)(2,1)S(1)} async-done(((bf16[4,2,128,256]{3,2,1,0:T(8,128)(2,1)}), bf16[4,2,128,256]{3,2,1,0:T(8,128)(2,1)S(1)}, u32[]{:S(2)}, u32[]{:S(2)}) %all-to-all-start.4) | async-done | bytes 524320 | tf_op jit(solution)/shard_map/all_to_all | solution.py:434
  (37 shorter events, 10.1 us)
Async XLA Ops:
  0.6 1.0 copy-start
  1.7 1.0 copy-start.1
  2.7 0.8 copy-start.4
  3.6 0.8 copy-start.5
  5.5 35.0 %all-to-all-start = ((bf16[4,256,512]{2,1,0:T(8,128)(2,1)}), bf16[4,256,512]{2,1,0:T(8,128)(2,1)S(1)}, u32[]{:S(2)}, u32[]{:S(2)}) async-start(bf16[4,256,512]{2,1,0:T(8,128)(2,1)} %get-tuple-element.26), calls=%async_computation | async-start | bytes 2097152 | tf_op jit(solution)/shard_map/all_to_all | solution.py:400
  40.6 4.7 %copy-start.8 = (s32[64]{0:T(128)S(1)}, s32[64]{0:T(128)}, u32[]{:S(2)}) copy-start(s32[64]{0:T(128)} %param.9) | copy-start | bytes 772
  41.7 13.7 %all-to-all-start.1 = ((bf16[4,512,256]{2,1,0:T(8,128)(2,1)}), bf16[4,512,256]{2,1,0:T(8,128)(2,1)S(1)}, u32[]{:S(2)}, u32[]{:S(2)}) async-start(bf16[4,512,256]{2,1,0:T(8,128)(2,1)} %pad_maximum_fusion), calls=%async_computation.1 | async-start | bytes 2097152 | tf_op jit(solution)/shard_map/all_to_all | solution.py:404
  55.4 20.5 %collective-permute-start = (bf16[2048,256]{1,0:T(8,128)(2,1)S(1)}, bf16[2048,256]{1,0:T(8,128)(2,1)S(1)}, u32[]{:S(2)}, u32[]{:S(2)}) collective-permute-start(bf16[2048,256]{1,0:T(8,128)(2,1)S(1)} %bitcast.31), channel_id=1, source_target_pairs={{0,1},{1,2},{2,3},{3,4},{4,5},{5,6},{6,7},{7,8},{8,9},{9,10},{10,1... | collective-permute-start | bytes 3145736 | tf_op jit(solution)/shard_map/ppermute | solution.py:407
  86.8 1.0 copy-start.6
  87.8 17.5 %collective-permute-start.1 = (bf16[2048,256]{1,0:T(8,128)(2,1)}, bf16[2048,256]{1,0:T(8,128)(2,1)}, u32[]{:S(2)}, u32[]{:S(2)}) collective-permute-start(bf16[2048,256]{1,0:T(8,128)(2,1)} %get-tuple-element.36), channel_id=1, source_target_pairs={{1,0},{2,1},{3,2},{4,3},{5,4},{6,5},{7,6},{8,7},{9,8},{10,9},{11,1... | collective-permute-start | bytes 3145736 | tf_op jit(solution)/shard_map/ppermute | solution.py:422
  91.2 13.9 %all-to-all-start.2 = ((bf16[4,128,512]{2,1,0:T(8,128)(2,1)}), bf16[4,128,512]{2,1,0:T(8,128)(2,1)}, u32[]{:S(2)}, u32[]{:S(2)}) async-start(bf16[4,128,512]{2,1,0:T(8,128)(2,1)} %get-tuple-element.35), calls=%async_computation.2 | async-start | bytes 1048576 | tf_op jit(solution)/shard_map/all_to_all | solution.py:423
  95.3 1.2 copy-start.7
  104.2 0.8 copy-start.2
  125.7 6.5 %copy-start.3 = (bf16[4,128,512]{2,1,0:T(8,128)(2,1)S(1)}, bf16[4,128,512]{2,1,0:T(8,128)(2,1)}, u32[]{:S(2)}) copy-start(bf16[4,128,512]{2,1,0:T(8,128)(2,1)} %copy-done.2) | copy-start | bytes 1572868
  126.6 33.6 %all-to-all-start.4 = ((bf16[4,2,128,256]{3,2,1,0:T(8,128)(2,1)}), bf16[4,2,128,256]{3,2,1,0:T(8,128)(2,1)S(1)}, u32[]{:S(2)}, u32[]{:S(2)}) async-start(bf16[4,2,128,256]{3,2,1,0:T(8,128)(2,1)} %pad_maximum_fusion.2), calls=%async_computation.4 | async-start | bytes 1048576 | tf_op jit(solution)/shard_map/all_to_all | solution.py:434
  132.3 8.7 %collective-permute-start.4 = (bf16[128,512]{1,0:T(8,128)(2,1)S(1)}, bf16[128,512]{1,0:T(8,128)(2,1)S(1)}, u32[]{:S(2)}, u32[]{:S(2)}) collective-permute-start(bf16[128,512]{1,0:T(8,128)(2,1)S(1)} %get-tuple-element.52), channel_id=1, source_target_pairs={{0,384},{128,0},{256,128},{384,256},{1,385},{129,1},{257,129},{385... | collective-permute-start | bytes 393224 | tf_op jit(solution)/shard_map/ppermute | solution.py:436
  135.1 7.2 %collective-permute-start.3 = (bf16[128,512]{1,0:T(8,128)(2,1)S(1)}, bf16[128,512]{1,0:T(8,128)(2,1)S(1)}, u32[]{:S(2)}, u32[]{:S(2)}) collective-permute-start(bf16[128,512]{1,0:T(8,128)(2,1)S(1)} %get-tuple-element.53), channel_id=1, source_target_pairs={{0,256},{128,384},{256,0},{384,128},{1,257},{129,385},{257,1},{385... | collective-permute-start | bytes 393224 | tf_op jit(solution)/shard_map/ppermute | solution.py:436
  138.2 8.0 %collective-permute-start.2 = (bf16[128,512]{1,0:T(8,128)(2,1)S(1)}, bf16[128,512]{1,0:T(8,128)(2,1)S(1)}, u32[]{:S(2)}, u32[]{:S(2)}) collective-permute-start(bf16[128,512]{1,0:T(8,128)(2,1)S(1)} %get-tuple-element.54), channel_id=1, source_target_pairs={{0,128},{128,256},{256,384},{384,0},{1,129},{129,257},{257,385},{3... | collective-permute-start | bytes 393224 | tf_op jit(solution)/shard_map/ppermute | solution.py:436

commit v5 on v4

--- a/solution.py
+++ b/solution.py
@@ -146,7 +146,7 @@
 def before_part(
     scalars, begin_ref, qd_ref, kv_ref, stats_in, out_in,
     context_ref, grad_ref, stats_ref, grad_query_ref,
-    keys_t, values_t, probs, grad_keys, grad_values, out_t, top, total,
+    keys_t, values_t, probs, grad_keys, grad_values, out_t, grad_query, top, total, sem,
 ):
     first = jnp.minimum(scalars[0] + SPAN, SPAN) // TILE
 
@@ -164,6 +164,11 @@
         return 0
 
     lax.fori_loop(0, first, blank, 0)
+
+    def hand_over(chunk):
+        return pltpu.make_async_copy(
+            grad_query.at[chunk], grad_query_ref.at[chunk], sem.at[chunk]
+        )
 
     def chunk_step(chunk, _):
         low, full_low = before_range(scalars, chunk)
@@ -173,7 +178,7 @@
         own_top, own_total = stats_in[chunk, 0:1], stats_in[chunk, 1:2]
         top[...] = jnp.broadcast_to(own_top, (8, ROWS))
         total[...] = jnp.zeros((8, ROWS), F32)
-        grad_query_ref[chunk] = jnp.zeros((HEAD_SIZE, ROWS), F32)
+        grad_query[chunk] = jnp.zeros((HEAD_SIZE, ROWS), F32)
 
         def scores_step(limits):
             def step(tile, count):
@@ -213,9 +218,10 @@
             grad_scores = (w * (grad_weights - delta)).astype(BF16)
             grad_values[here] += dot(w.astype(BF16), rows_d, ((1,), (0,)))
             grad_keys[here] += dot(grad_scores, rows_q, ((1,), (0,)))
-            grad_query_ref[chunk] += dot(keys_t[:, here], grad_scores, ((1,), (0,)))
+            grad_query[chunk] += dot(keys_t[:, here], grad_scores, ((1,), (0,)))
 
         sweep(low, TILES, gradient_step, GROUP)
+        hand_over(chunk).start()
         return 0
 
     lax.fori_loop(0, 4, chunk_step, 0)
@@ -226,13 +232,24 @@
         return 0
 
     lax.fori_loop(first, TILES, store, 0)
+    for chunk in range(4):
+        hand_over(chunk).wait()
 
 
 def own_backward(
     scalars, begin_ref, qd_ref, kv_ref, stats_in, grad_query_in,
-    grad_query_ref, grad_ref, keys_t, grad_keys, grad_values, grad_query_t,
+    out_0, out_1, out_2, out_3, grad_ref,
+    keys_t, grad_keys, grad_values, grad_query_t, grad_query, sem,
 ):
     first = jnp.maximum(scalars[0], 0) // TILE
+
+    def fetch(chunk):
+        return pltpu.make_async_copy(
+            grad_query_in.at[chunk], grad_query_t.at[chunk], sem.at[chunk]
+        )
+
+    for chunk in range(4):
+        fetch(chunk).start()
 
     def load(tile, _):
         keys_t[:, at(tile)] = kv_ref[at(tile), :HEAD_SIZE].T
@@ -254,7 +271,7 @@
         rows_d = rows_of(qd_ref, chunk, 1)
         limits = (begin_ref[chunk], position_in_rows(start))
         log_total, delta = stats_in[chunk, 0:1], stats_in[chunk, 1:2]
-        grad_query_t[...] = grad_query_in[chunk]
+        fetch(chunk).wait()
 
         def gradient_step(limits):
             def step(tile, count):
@@ -265,14 +282,14 @@
                 grad_scores = (w * (grad_weights - delta)).astype(BF16)
                 grad_values[here] += dot(w.astype(BF16), rows_d, ((1,), (0,)))
                 grad_keys[here] += dot(grad_scores, rows_q, ((1,), (0,)))
-                grad_query_t[...] += dot(keys_t[:, here], grad_scores, ((1,), (0,)))
+                grad_query_t[chunk] += dot(keys_t[:, here], grad_scores, ((1,), (0,)))
 
             return step
 
         sweep(low, full_low, gradient_step(limits), BACK_GROUP)
         sweep(full_low, full_high, gradient_step(None), BACK_GROUP)
         sweep(full_high, high, gradient_step(limits), BACK_GROUP)
-        store_rows(grad_query_ref, (chunk - scalars[9]) & 3, (grad_query_t[...] * SCALE).T)
+        store_rows(grad_query, (chunk - scalars[9]) & 3, (grad_query_t[chunk] * SCALE).T)
         return 0
 
     lax.fori_loop(0, 4, chunk_step, 0)
@@ -283,16 +300,20 @@
         return 0
 
     lax.fori_loop(first, TILES, store, 0)
-
-
-def call(kernel, name, gflops, megabytes, outs, scratch, *args):
-    vmem = pl.BlockSpec(memory_space=pltpu.VMEM)
+    for slot, out in enumerate((out_0, out_1, out_2, out_3)):
+        out[...] = grad_query[slot]
+
+
+def call(kernel, name, gflops, megabytes, outs, scratch, *args, hbm_in=(), hbm_out=(), sems=0):
+    vmem, hbm = pl.BlockSpec(memory_space=pltpu.VMEM), pl.BlockSpec(memory_space=pltpu.HBM)
     return pl.pallas_call(
         kernel,
         out_shape=tuple(jax.ShapeDtypeStruct(shape, dtype) for shape, dtype in outs),
-        in_specs=[pl.BlockSpec(memory_space=pltpu.SMEM)] + [vmem] * (len(args) - 1),
-        out_specs=tuple(vmem for _ in outs),
-        scratch_shapes=[pltpu.VMEM(shape, dtype) for shape, dtype in scratch],
+        in_specs=[pl.BlockSpec(memory_space=pltpu.SMEM)]
+        + [hbm if n in hbm_in else vmem for n in range(1, len(args))],
+        out_specs=tuple(hbm if n in hbm_out else vmem for n in range(len(outs))),
+        scratch_shapes=[pltpu.VMEM(shape, dtype) for shape, dtype in scratch]
+        + ([pltpu.SemaphoreType.DMA((sems,))] if sems else []),
         compiler_params=pltpu.CompilerParams(vmem_limit_bytes=megabytes << 20),
         cost_estimate=pl.CostEstimate(
             flops=gflops * 10**9, bytes_accessed=4 << 20, transcendentals=2 * 10**6
@@ -304,6 +325,7 @@
 STATS = ((4, 2, ROWS), F32)
 ACROSS = ((4, HEAD_SIZE, ROWS), F32)
 RESULT = ((4, CHUNK, ROWS), BF16)
+PIECE = ((CHUNK, ROWS), BF16)
 GRADS = ((SPAN, 2 * HEAD_SIZE), BF16)
 TURNED = ((HEAD_SIZE, SPAN), BF16)
 SQUARE = ((SPAN, ROWS), F32)
@@ -322,15 +344,16 @@
 def run_before_part(scalars, begin, qd, kv, stats, out):
     return call(
         before_part, "before_part", 2, 18, (RESULT, GRADS, STATS, ACROSS),
-        (TURNED, TURNED, SQUARE, SUMS, SUMS, FLAT, EIGHT, EIGHT),
-        scalars, begin, qd, kv, stats, out,
+        (TURNED, TURNED, SQUARE, SUMS, SUMS, FLAT, ACROSS, EIGHT, EIGHT),
+        scalars, begin, qd, kv, stats, out, hbm_out=(3,), sems=4,
     )
 
 
 def run_own_backward(scalars, begin, qd, kv, stats, grad_query):
     return call(
-        own_backward, "own_backward", 3, 14, (RESULT, GRADS), (TURNED, SUMS, SUMS, FLAT),
-        scalars, begin, qd, kv, stats, grad_query,
+        own_backward, "own_backward", 3, 60, (PIECE,) * 4 + (GRADS,),
+        (TURNED, SUMS, SUMS, ACROSS, RESULT), scalars, begin, qd, kv, stats, grad_query,
+        hbm_in=(5,), sems=4,
     )
 
 
@@ -349,18 +372,48 @@
 
 
 def pack(queries, output_gradient, keys, values):
-    def kernel(q_ref, d_ref, k_ref, v_ref, qd_ref, kv_ref):
-        for d in range(4):
-            span = slice(d * ROWS, (d + 1) * ROWS)
-            qd_ref[d, :CHUNK] = q_ref[:, span]
-            qd_ref[d, CHUNK:] = d_ref[:, span]
-        for head in range(2):
-            here = slice(head * HEAD_SIZE, (head + 1) * HEAD_SIZE)
-            kv_ref[:, 2 * head * HEAD_SIZE : (2 * head + 1) * HEAD_SIZE] = k_ref[:, here]
-            kv_ref[:, (2 * head + 1) * HEAD_SIZE : (2 * head + 2) * HEAD_SIZE] = v_ref[:, here]
-
-    outs = (((4, 2 * CHUNK, ROWS), BF16), ((CHUNK, 4 * HEAD_SIZE), BF16))
-    return small(kernel, "pack", outs, None, queries, output_gradient, keys, values)
+    def kernel(q_ref, d_ref, k_ref, v_ref, qd_ref, kv_ref, sem):
+        moves = []
+        for index, source in enumerate((k_ref, v_ref)):
+            for head in range(2):
+                slot = 2 * head + index
+                moves.append(
+                    (
+                        source.at[:, pl.ds(head * HEAD_SIZE, HEAD_SIZE)],
+                        kv_ref.at[:, pl.ds(slot * HEAD_SIZE, HEAD_SIZE)],
+                    )
+                )
+        for index, source in enumerate((q_ref, d_ref)):
+            for d in range(4):
+                moves.append(
+                    (
+                        source.at[:, pl.ds(d * ROWS, ROWS)],
+                        qd_ref.at[d, pl.ds(index * CHUNK, CHUNK)],
+                    )
+                )
+        copies = [
+            pltpu.make_async_copy(source, target, sem.at[n])
+            for n, (source, target) in enumerate(moves)
+        ]
+        for copy in copies:
+            copy.start()
+        for copy in copies:
+            copy.wait()
+
+    hbm = pl.BlockSpec(memory_space=pltpu.HBM)
+    return pl.pallas_call(
+        kernel,
+        out_shape=(
+            jax.ShapeDtypeStruct((4, 2 * CHUNK, ROWS), BF16),
+            jax.ShapeDtypeStruct((CHUNK, 4 * HEAD_SIZE), BF16),
+        ),
+        in_specs=[hbm] * 4,
+        out_specs=(hbm, hbm),
+        scratch_shapes=[pltpu.SemaphoreType.DMA((12,))],
+        compiler_params=pltpu.CompilerParams(vmem_limit_bytes=60 << 20),
+        cost_estimate=pl.CostEstimate(flops=10**6, bytes_accessed=2 << 20, transcendentals=0),
+        name="pack",
+    )(queries, output_gradient, keys, values)
 
 
 def join(y, *pieces):
@@ -421,7 +474,7 @@
     )
     returned = lax.ppermute(grad_before, BLOCK_AXES, [(i + 1, i) for i in range(blocks - 1)])
     context = lax.all_to_all(context, "y", split_axis=0, concat_axis=0, tiled=True)
-    grad_query, grad_own = run_own_backward(scalars, begin, qd, kv_own, stats, grad_query)
+    *grad_query, grad_own = run_own_backward(scalars, begin, qd, kv_own, stats, grad_query)
     context, returned, grad_own = lax.optimization_barrier((context, returned, grad_own))
     grad_own = (grad_own.astype(F32) + returned.astype(F32)).astype(BF16)
     grad = lax.all_to_all(
@@ -430,7 +483,7 @@
 
     grad = grad.astype(F32)
     grad = jnp.stack([grad[0] + grad[1], grad[2] + grad[3]], axis=1).astype(BF16)
-    grad, grad_query = lax.optimization_barrier((grad, grad_query))
+    grad, *grad_query = lax.optimization_barrier((grad, *grad_query))
     grad = lax.all_to_all(grad, "z_hi", split_axis=0, concat_axis=0, tiled=True)
     pieces = [grad_query[0]] + [
         lax.ppermute(grad_query[step], "y", [(i, (i + step) % 4) for i in range(4)])

time: 162 us -> 195 us (1.20)
  the two profiles are of different devices: /device:TPU:3 before, /device:TPU:6 now
where the time goes in v5:
time: 195 us; the launch traced here: 192 us
  Pallas kernels  61.6 us (32%)
  blocking collectives  53.8 us (28%)
  waiting for transfers between devices  36.4 us (19%)
  starting transfers between devices  32.5 us (17%)
  other arithmetic  5.12 us (3%)
    pallas_call x1, Pallas kernels, pack(): pl.pallas_call(kernel, out_shape=(jax.ShapeDtypeStruct((4, 2 * CHUNK, ROW...  36.9 us
    all_gather x1, blocking collectives, per_device(): kv = lax.all_gather(kv, 'z_hi', axis=0, tiled=True)  34.5 us
    pallas_call x3, Pallas kernels, call(): pl.pallas_call(kernel, out_shape=tuple((jax.ShapeDtypeStruct(shape, dtype...  23.1 us
    all_to_all x1, blocking collectives, per_device(): lax.all_to_all(grad_own.reshape(4, 4, CHUNK, 2 * HEAD_SIZE), 'y', split_a...  19.4 us
    all_to_all x1, waiting for transfers between devices, per_device(): grad = lax.all_to_all(grad, 'z_hi', split_axis=0, concat_axis=0, tiled=True)  14.5 us
    all_to_all x1, waiting for transfers between devices, per_device(): lax.all_to_all(jnp.stack([first, first, second, second]), 'y', split_axis...  11.3 us
    ppermute x3, starting transfers between devices, per_device(): lax.ppermute(grad_query[step], 'y', [(i, (i + step) % 4) for i in range(4)])  9.18 us
    ppermute x1, waiting for transfers between devices, per_device(): lax.ppermute(kv_own, BLOCK_AXES, [(i, i + 1) for i in range(blocks - 1)])  7.14 us
  transfers between devices with their start and end apart: 9, of which 5 were waited for; matrix products, arithmetic and copies ran while one was open for 1% of the time, Pallas kernels for 9%

profile of v5, /device:TPU:6, one launch (start us, length us, event | category | flops | bytes accessed | tf_op | source)
XLA Modules:
  0.0 192.2 jit_solution(1124283346337014009)
XLA Ops:
  0.6 36.9 %pack.1 = (bf16[4,256,512]{2,1,0:T(8,128)(2,1)}, bf16[128,512]{1,0:T(8,128)(2,1)}) custom-call(bf16[128,2048]{1,0:T(8,128)(2,1)} %q_ref.1, bf16[128,2048]{1,0:T(8,128)(2,1)} %d_ref.1, bf16[128,256]{1,0:T(8,128)(2,1)} %k_ref.1, bf16[128,256]{1,0:T(8,128)(2,1)} %v_ref.1), custom_call_target="tpu_custom_call" | custom-call | flops 1000000 | bytes 2097152 | tf_op jit(solution)/shard_map/pack/pallas_call | solution.py:404
  37.6 4.6 %all-to-all-start = ((bf16[4,256,512]{2,1,0:T(8,128)(2,1)}), bf16[4,256,512]{2,1,0:T(8,128)(2,1)S(1)}, u32[]{:S(2)}, u32[]{:S(2)}) async-start(bf16[4,256,512]{2,1,0:T(8,128)(2,1)} %get-tuple-element.32), calls=%async_computation | async-start | bytes 2097152 | tf_op jit(solution)/shard_map/all_to_all | solution.py:453
  42.2 34.5 %all_gather.3 = bf16[512,512]{1,0:T(8,128)(2,1)S(1)} all-gather(bf16[128,512]{1,0:T(8,128)(2,1)S(1)} %copy-done.7), channel_id=1, replica_groups=mesh['y'=4,'z_hi'=4,'z_lo'=4,'x'=4,'core'=2] {'z_hi'}, dimensions={0}, use_global_device_ids=true | all-gather | bytes 655360 | tf_op jit(solution)/shard_map/all_gather | solution.py:454
  76.7 1.2 pad_maximum_fusion
  77.9 3.5 %all-to-all-start.1 = ((bf16[4,512,256]{2,1,0:T(8,128)(2,1)}), bf16[4,512,256]{2,1,0:T(8,128)(2,1)S(1)}, u32[]{:S(2)}, u32[]{:S(2)}) async-start(bf16[4,512,256]{2,1,0:T(8,128)(2,1)} %pad_maximum_fusion), calls=%async_computation.1 | async-start | bytes 2097152 | tf_op jit(solution)/shard_map/all_to_all | solution.py:457
  81.6 11.3 %all-to-all-done.1 = bf16[4,512,256]{2,1,0:T(8,128)(2,1)S(1)} async-done(((bf16[4,512,256]{2,1,0:T(8,128)(2,1)}), bf16[4,512,256]{2,1,0:T(8,128)(2,1)S(1)}, u32[]{:S(2)}, u32[]{:S(2)}) %all-to-all-start.1) | async-done | bytes 1048608 | tf_op jit(solution)/shard_map/all_to_all | solution.py:457
  92.9 1.9 collective-permute-start
  95.3 6.6 %own_forward.1 = (f32[4,2,512]{2,1,0:T(2,128)S(1)}, f32[4,128,512]{2,1,0:T(8,128)S(1)}) custom-call(s32[10]{0:T(128)S(1)} %pad_add_fusion.scalars, s32[4,1,512]{2,1,0:T(1,128)S(1)} %bitcast.26, bf16[4,256,512]{2,1,0:T(8,128)(2,1)S(1)} %all-to-all-done.qd_ref, bf16[2048,256]{1,0:T(8,128)(2,1)S(1)} %bitcast.24), custom_call_target="tpu_custom_call" | custom-call | flops 2000000000 | bytes 4194304 | tf_op jit(solution)/shard_map/own_forward/pallas_call | solution.py:309
  101.9 7.1 %collective-permute-done.kv_ref = bf16[2048,256]{1,0:T(8,128)(2,1)S(1)} collective-permute-done((bf16[2048,256]{1,0:T(8,128)(2,1)S(1)}, bf16[2048,256]{1,0:T(8,128)(2,1)S(1)}, u32[]{:S(2)}, u32[]{:S(2)}) %collective-permute-start) | collective-permute-done | bytes 1048608 | tf_op jit(solution)/shard_map/ppermute | solution.py:460
  109.0 6.0 %before_part.1 = (bf16[4,128,512]{2,1,0:T(8,128)(2,1)}, bf16[2048,256]{1,0:T(8,128)(2,1)S(1)}, f32[4,2,512]{2,1,0:T(2,128)S(1)}, f32[4,128,512]{2,1,0:T(8,128)S(1)}) custom-call(s32[10]{0:T(128)S(1)} %pad_add_fusion.scalars, s32[4,1,512]{2,1,0:T(1,128)S(1)} %bitcast.27, bf16[4,256,512]{2,1,0:T(8,128)(2,1)S(1)} %all-to-all-done.qd_ref, ...), custom_call_target="tpu_custom_call" | custom-call | flops 2000000000 | bytes 4194304 | tf_op jit(solution)/shard_map/before_part/pallas_call | solution.py:309
  115.1 1.0 copy-done.5
  116.7 3.3 %collective-permute-start.1 = (bf16[2048,256]{1,0:T(8,128)(2,1)S(1)}, bf16[2048,256]{1,0:T(8,128)(2,1)S(1)}, u32[]{:S(2)}, u32[]{:S(2)}) collective-permute-start(bf16[2048,256]{1,0:T(8,128)(2,1)S(1)} %get-tuple-element.42), channel_id=1, source_target_pairs={{1,0},{2,1},{3,2},{4,3},{5,4},{6,5},{7,6},{8,7},{9,8},{10,9},{11,1... | collective-permute-start | bytes 3145736 | tf_op jit(solution)/shard_map/ppermute | solution.py:475
  119.9 3.5 %all-to-all-start.2 = ((bf16[4,128,512]{2,1,0:T(8,128)(2,1)}), bf16[4,128,512]{2,1,0:T(8,128)(2,1)S(1)}, u32[]{:S(2)}, u32[]{:S(2)}) async-start(bf16[4,128,512]{2,1,0:T(8,128)(2,1)} %get-tuple-element.41), calls=%async_computation.2 | async-start | bytes 1048576 | tf_op jit(solution)/shard_map/all_to_all | solution.py:476
  123.4 10.5 %own_backward.1 = (bf16[128,512]{1,0:T(8,128)(2,1)}, bf16[128,512]{1,0:T(8,128)(2,1)}, bf16[128,512]{1,0:T(8,128)(2,1)}, bf16[128,512]{1,0:T(8,128)(2,1)}, bf16[2048,256]{1,0:T(8,128)(2,1)}) custom-call(s32[10]{0:T(128)} %copy-done.4, s32[4,1,512]{2,1,0:T(1,128)} %bitcast.28, bf16[4,256,512]{2,1,0:T(8,128)(2,1)} %copy-done, bf16[2048,256]{1,0:T(8,128)(2,1)} %bitcast.25, ...), custom_call_target="tpu_custom_call" | custom-call | flops 3000000000 | bytes 4194304 | tf_op jit(solution)/shard_map/own_backward/pallas_call | solution.py:309
  134.0 1.5 add_convert_fusion
  135.5 19.4 %all_to_all.25 = bf16[4,4,128,256]{3,2,1,0:T(8,128)(2,1)S(1)} all-to-all(bf16[4,4,128,256]{3,2,1,0:T(8,128)(2,1)S(1)} %bitcast.29), channel_id=1, replica_groups=mesh['y'=4,'z_hi'=4,'z_lo'=4,'x'=4,'core'=2] {'y'}, dimensions={0} | all-to-all | bytes 2097152 | tf_op jit(solution)/shard_map/all_to_all | solution.py:480
  155.2 0.9 pad_maximum_fusion.2
  156.1 6.6 %all-to-all-start.4 = ((bf16[4,2,128,256]{3,2,1,0:T(8,128)(2,1)}), bf16[4,2,128,256]{3,2,1,0:T(8,128)(2,1)S(1)}, u32[]{:S(2)}, u32[]{:S(2)}) async-start(bf16[4,2,128,256]{3,2,1,0:T(8,128)(2,1)} %pad_maximum_fusion.2), calls=%async_computation.4 | async-start | bytes 1048576 | tf_op jit(solution)/shard_map/all_to_all | solution.py:487
  162.7 2.5 %collective-permute-start.2 = (bf16[128,512]{1,0:T(8,128)(2,1)S(1)}, bf16[128,512]{1,0:T(8,128)(2,1)S(1)}, u32[]{:S(2)}, u32[]{:S(2)}) collective-permute-start(bf16[128,512]{1,0:T(8,128)(2,1)S(1)} %copy-done.10), channel_id=1, source_target_pairs={{0,128},{128,256},{256,384},{384,0},{1,129},{129,257},{257,385},{3... | collective-permute-start | bytes 393224 | tf_op jit(solution)/shard_map/ppermute | solution.py:489
  165.2 4.0 %collective-permute-start.3 = (bf16[128,512]{1,0:T(8,128)(2,1)S(1)}, bf16[128,512]{1,0:T(8,128)(2,1)S(1)}, u32[]{:S(2)}, u32[]{:S(2)}) collective-permute-start(bf16[128,512]{1,0:T(8,128)(2,1)S(1)} %copy-done.9), channel_id=1, source_target_pairs={{0,256},{128,384},{256,0},{384,128},{1,257},{129,385},{257,1},{385... | collective-permute-start | bytes 393224 | tf_op jit(solution)/shard_map/ppermute | solution.py:489
  169.1 2.7 %collective-permute-start.4 = (bf16[128,512]{1,0:T(8,128)(2,1)S(1)}, bf16[128,512]{1,0:T(8,128)(2,1)S(1)}, u32[]{:S(2)}, u32[]{:S(2)}) collective-permute-start(bf16[128,512]{1,0:T(8,128)(2,1)S(1)} %copy-done.8), channel_id=1, source_target_pairs={{0,384},{128,0},{256,128},{384,256},{1,385},{129,1},{257,129},{385... | collective-permute-start | bytes 393224 | tf_op jit(solution)/shard_map/ppermute | solution.py:489
  171.9 0.8 pad_maximum_fusion.1
  173.5 2.6 %collective-permute-done.4.refs_3_ = bf16[128,512]{1,0:T(8,128)(2,1)S(1)} collective-permute-done((bf16[128,512]{1,0:T(8,128)(2,1)S(1)}, bf16[128,512]{1,0:T(8,128)(2,1)S(1)}, u32[]{:S(2)}, u32[]{:S(2)}) %collective-permute-start.4) | collective-permute-done | bytes 131104 | tf_op jit(solution)/shard_map/ppermute | solution.py:489
  177.0 14.5 %all-to-all-done.4.grad_ref = bf16[4,2,128,256]{3,2,1,0:T(8,128)(2,1)S(1)} async-done(((bf16[4,2,128,256]{3,2,1,0:T(8,128)(2,1)}), bf16[4,2,128,256]{3,2,1,0:T(8,128)(2,1)S(1)}, u32[]{:S(2)}, u32[]{:S(2)}) %all-to-all-start.4) | async-done | bytes 524320 | tf_op jit(solution)/shard_map/all_to_all | solution.py:487
  (42 shorter events, 4.0 us)
Async XLA Ops:
  37.6 4.6 %copy-start.7 = (bf16[128,512]{1,0:T(8,128)(2,1)S(1)}, bf16[128,512]{1,0:T(8,128)(2,1)}, u32[]{:S(2)}) copy-start(bf16[128,512]{1,0:T(8,128)(2,1)} %get-tuple-element.33) | copy-start | bytes 393220
  37.6 39.1 %all-to-all-start = ((bf16[4,256,512]{2,1,0:T(8,128)(2,1)}), bf16[4,256,512]{2,1,0:T(8,128)(2,1)S(1)}, u32[]{:S(2)}, u32[]{:S(2)}) async-start(bf16[4,256,512]{2,1,0:T(8,128)(2,1)} %get-tuple-element.32), calls=%async_computation | async-start | bytes 2097152 | tf_op jit(solution)/shard_map/all_to_all | solution.py:453
  76.7 32.3 %copy-start = (bf16[4,256,512]{2,1,0:T(8,128)(2,1)}, bf16[4,256,512]{2,1,0:T(8,128)(2,1)S(1)}, u32[]{:S(2)}) copy-start(bf16[4,256,512]{2,1,0:T(8,128)(2,1)S(1)} %all-to-all-done.qd_ref) | copy-start | bytes 3145732
  76.7 4.8 %copy-start.11 = (s32[64]{0:T(128)S(1)}, s32[64]{0:T(128)}, u32[]{:S(2)}) copy-start(s32[64]{0:T(128)} %param.9) | copy-start | bytes 772
  77.9 15.0 %all-to-all-start.1 = ((bf16[4,512,256]{2,1,0:T(8,128)(2,1)}), bf16[4,512,256]{2,1,0:T(8,128)(2,1)S(1)}, u32[]{:S(2)}, u32[]{:S(2)}) async-start(bf16[4,512,256]{2,1,0:T(8,128)(2,1)} %pad_maximum_fusion), calls=%async_computation.1 | async-start | bytes 2097152 | tf_op jit(solution)/shard_map/all_to_all | solution.py:457
  92.9 9.0 %copy-start.1 = (bf16[4,512,256]{2,1,0:T(8,128)(2,1)}, bf16[4,512,256]{2,1,0:T(8,128)(2,1)S(1)}, u32[]{:S(2)}) copy-start(bf16[4,512,256]{2,1,0:T(8,128)(2,1)S(1)} %all-to-all-done.1) | copy-start | bytes 3145732
  92.9 16.1 %collective-permute-start = (bf16[2048,256]{1,0:T(8,128)(2,1)S(1)}, bf16[2048,256]{1,0:T(8,128)(2,1)S(1)}, u32[]{:S(2)}, u32[]{:S(2)}) collective-permute-start(bf16[2048,256]{1,0:T(8,128)(2,1)S(1)} %bitcast.23), channel_id=1, source_target_pairs={{0,1},{1,2},{2,3},{3,4},{4,5},{5,6},{6,7},{7,8},{8,9},{9,10},{10,1... | collective-permute-start | bytes 3145736 | tf_op jit(solution)/shard_map/ppermute | solution.py:460
  95.3 13.7 %copy-start.4 = (s32[10]{0:T(128)}, s32[10]{0:T(128)S(1)}, u32[]{:S(2)}) copy-start(s32[10]{0:T(128)S(1)} %pad_add_fusion.scalars) | copy-start | bytes 124
  95.3 13.7 %copy-start.3 = (s32[4,4,128]{2,1,0:T(4,128)}, s32[4,4,128]{2,1,0:T(4,128)S(1)}, u32[]{:S(2)}) copy-start(s32[4,4,128]{2,1,0:T(4,128)S(1)} %tile.8) | copy-start | bytes 24580
  115.1 1.0 copy-start.5
  116.0 0.6 copy-start.6
  116.7 17.3 %collective-permute-start.1 = (bf16[2048,256]{1,0:T(8,128)(2,1)S(1)}, bf16[2048,256]{1,0:T(8,128)(2,1)S(1)}, u32[]{:S(2)}, u32[]{:S(2)}) collective-permute-start(bf16[2048,256]{1,0:T(8,128)(2,1)S(1)} %get-tuple-element.42), channel_id=1, source_target_pairs={{1,0},{2,1},{3,2},{4,3},{5,4},{6,5},{7,6},{8,7},{9,8},{10,9},{11,1... | collective-permute-start | bytes 3145736 | tf_op jit(solution)/shard_map/ppermute | solution.py:475
  119.9 14.0 %all-to-all-start.2 = ((bf16[4,128,512]{2,1,0:T(8,128)(2,1)}), bf16[4,128,512]{2,1,0:T(8,128)(2,1)S(1)}, u32[]{:S(2)}, u32[]{:S(2)}) async-start(bf16[4,128,512]{2,1,0:T(8,128)(2,1)} %get-tuple-element.41), calls=%async_computation.2 | async-start | bytes 1048576 | tf_op jit(solution)/shard_map/all_to_all | solution.py:476
  155.2 7.5 %copy-start.10 = (bf16[128,512]{1,0:T(8,128)(2,1)S(1)}, bf16[128,512]{1,0:T(8,128)(2,1)}, u32[]{:S(2)}) copy-start(bf16[128,512]{1,0:T(8,128)(2,1)} %get-tuple-element.54) | copy-start | bytes 393220
  155.2 10.0 %copy-start.9 = (bf16[128,512]{1,0:T(8,128)(2,1)S(1)}, bf16[128,512]{1,0:T(8,128)(2,1)}, u32[]{:S(2)}) copy-start(bf16[128,512]{1,0:T(8,128)(2,1)} %get-tuple-element.55) | copy-start | bytes 393220
  155.2 14.0 %copy-start.8 = (bf16[128,512]{1,0:T(8,128)(2,1)S(1)}, bf16[128,512]{1,0:T(8,128)(2,1)}, u32[]{:S(2)}) copy-start(bf16[128,512]{1,0:T(8,128)(2,1)} %get-tuple-element.56) | copy-start | bytes 393220
  155.2 21.0 %copy-start.2 = (bf16[128,512]{1,0:T(8,128)(2,1)S(1)}, bf16[128,512]{1,0:T(8,128)(2,1)}, u32[]{:S(2)}) copy-start(bf16[128,512]{1,0:T(8,128)(2,1)} %get-tuple-element.53.refs_0_) | copy-start | bytes 393220
  156.1 35.4 %all-to-all-start.4 = ((bf16[4,2,128,256]{3,2,1,0:T(8,128)(2,1)}), bf16[4,2,128,256]{3,2,1,0:T(8,128)(2,1)S(1)}, u32[]{:S(2)}, u32[]{:S(2)}) async-start(bf16[4,2,128,256]{3,2,1,0:T(8,128)(2,1)} %pad_maximum_fusion.2), calls=%async_computation.4 | async-start | bytes 1048576 | tf_op jit(solution)/shard_map/all_to_all | solution.py:487
  162.7 10.1 %collective-permute-start.2 = (bf16[128,512]{1,0:T(8,128)(2,1)S(1)}, bf16[128,512]{1,0:T(8,128)(2,1)S(1)}, u32[]{:S(2)}, u32[]{:S(2)}) collective-permute-start(bf16[128,512]{1,0:T(8,128)(2,1)S(1)} %copy-done.10), channel_id=1, source_target_pairs={{0,128},{128,256},{256,384},{384,0},{1,129},{129,257},{257,385},{3... | collective-permute-start | bytes 393224 | tf_op jit(solution)/shard_map/ppermute | solution.py:489
  165.2 8.4 %collective-permute-start.3 = (bf16[128,512]{1,0:T(8,128)(2,1)S(1)}, bf16[128,512]{1,0:T(8,128)(2,1)S(1)}, u32[]{:S(2)}, u32[]{:S(2)}) collective-permute-start(bf16[128,512]{1,0:T(8,128)(2,1)S(1)} %copy-done.9), channel_id=1, source_target_pairs={{0,256},{128,384},{256,0},{384,128},{1,257},{129,385},{257,1},{385... | collective-permute-start | bytes 393224 | tf_op jit(solution)/shard_map/ppermute | solution.py:489
  169.1 7.0 %collective-permute-start.4 = (bf16[128,512]{1,0:T(8,128)(2,1)S(1)}, bf16[128,512]{1,0:T(8,128)(2,1)S(1)}, u32[]{:S(2)}, u32[]{:S(2)}) collective-permute-start(bf16[128,512]{1,0:T(8,128)(2,1)S(1)} %copy-done.8), channel_id=1, source_target_pairs={{0,384},{128,0},{256,128},{384,256},{1,385},{129,1},{257,129},{385... | collective-permute-start | bytes 393224 | tf_op jit(solution)/shard_map/ppermute | solution.py:489

commit v6 on v5

--- a/solution.py
+++ b/solution.py
@@ -82,6 +82,19 @@
     return start + (lax.broadcasted_iota(jnp.int32, (1, ROWS), 1) & (CHUNK - 1))
 
 
+def load_halves(scalars, first, mine_ref, other_ref, keep):
+    half = TILES // 2
+    for ref, which in ((mine_ref, scalars[9] & 1), (other_ref, 1 - (scalars[9] & 1))):
+        shift = which * half
+
+        def body(tile, _, ref=ref, shift=shift):
+            both = ref[at(tile - shift)]
+            keep(tile, both[:, :HEAD_SIZE], both[:, HEAD_SIZE:])
+            return 0
+
+        lax.fori_loop(jnp.maximum(first, shift), shift + half, body, 0)
+
+
 def scores(keys, rows_q, tile, count, limits):
     s = LOG2_SCALE * dot(keys, rows_q, ((1,), (1,)))
     if limits is not None:
@@ -98,14 +111,17 @@
     return how(value.reshape(value.shape[0] // 8, 8, ROWS), axis=0)
 
 
-def own_forward(scalars, begin_ref, qd_ref, kv_ref, stats_ref, out_ref, values_t, probs, top, total):
+def own_forward(
+    scalars, begin_ref, qd_ref, mine_ref, other_ref,
+    stats_ref, out_ref, keys, values_t, probs, top, total,
+):
     first = jnp.maximum(scalars[0], 0) // TILE
 
-    def load(tile, _):
-        values_t[:, at(tile)] = kv_ref[at(tile), HEAD_SIZE:].T
-        return 0
-
-    lax.fori_loop(first, TILES, load, 0)
+    def keep(tile, k, v):
+        keys[at(tile)] = k
+        values_t[:, at(tile)] = v.T
+
+    load_halves(scalars, first, mine_ref, other_ref, keep)
 
     def chunk_step(chunk, _):
         start, low, high, full_low, full_high = own_range(scalars, chunk)
@@ -118,7 +134,7 @@
         def scores_step(limits):
             def step(tile, count):
                 here = at(tile, count)
-                s = scores(kv_ref[here, :HEAD_SIZE], rows_q, tile, count, limits)
+                s = scores(keys[here], rows_q, tile, count, limits)
                 probs[here] = s
                 top[...] = jnp.maximum(top[...], fold(s, jnp.max))
 
@@ -144,20 +160,21 @@
 
 
 def before_part(
-    scalars, begin_ref, qd_ref, kv_ref, stats_in, out_in,
-    context_ref, grad_ref, stats_ref, grad_query_ref,
+    scalars, begin_ref, qd_ref, mine_ref, other_ref, stats_in, out_in,
+    context_ref, grad_ref, stats_ref, grad_query_ref, keys, values,
     keys_t, values_t, probs, grad_keys, grad_values, out_t, grad_query, top, total, sem,
 ):
     first = jnp.minimum(scalars[0] + SPAN, SPAN) // TILE
 
-    def load(tile, _):
-        keys_t[:, at(tile)] = kv_ref[at(tile), :HEAD_SIZE].T
-        values_t[:, at(tile)] = kv_ref[at(tile), HEAD_SIZE:].T
+    def keep(tile, k, v):
+        keys[at(tile)] = k
+        values[at(tile)] = v
+        keys_t[:, at(tile)] = k.T
+        values_t[:, at(tile)] = v.T
         grad_keys[at(tile)] = jnp.zeros((TILE, HEAD_SIZE), F32)
         grad_values[at(tile)] = jnp.zeros((TILE, HEAD_SIZE), F32)
-        return 0
-
-    lax.fori_loop(first, TILES, load, 0)
+
+    load_halves(scalars, first, mine_ref, other_ref, keep)
 
     def blank(tile, _):
         grad_ref[at(tile)] = jnp.zeros((TILE, 2 * HEAD_SIZE), BF16)
@@ -183,7 +200,7 @@
         def scores_step(limits):
             def step(tile, count):
                 here = at(tile, count)
-                s = scores(kv_ref[here, :HEAD_SIZE], rows_q, tile, count, limits)
+                s = scores(keys[here], rows_q, tile, count, limits)
                 probs[here] = s
                 top[...] = jnp.maximum(top[...], fold(s, jnp.max))
 
@@ -214,7 +231,7 @@
         def gradient_step(tile, count):
             here = at(tile, count)
             w = probs[here] * inverse
-            grad_weights = dot(kv_ref[here, HEAD_SIZE:], rows_d, ((1,), (1,)))
+            grad_weights = dot(values[here], rows_d, ((1,), (1,)))
             grad_scores = (w * (grad_weights - delta)).astype(BF16)
             grad_values[here] += dot(w.astype(BF16), rows_d, ((1,), (0,)))
             grad_keys[here] += dot(grad_scores, rows_q, ((1,), (0,)))
@@ -237,8 +254,8 @@
 
 
 def own_backward(
-    scalars, begin_ref, qd_ref, kv_ref, stats_in, grad_query_in,
-    out_0, out_1, out_2, out_3, grad_ref,
+    scalars, begin_ref, qd_ref, mine_ref, other_ref, stats_in, grad_query_in,
+    out_0, out_1, out_2, out_3, grad_ref, keys, values,
     keys_t, grad_keys, grad_values, grad_query_t, grad_query, sem,
 ):
     first = jnp.maximum(scalars[0], 0) // TILE
@@ -251,13 +268,14 @@
     for chunk in range(4):
         fetch(chunk).start()
 
-    def load(tile, _):
-        keys_t[:, at(tile)] = kv_ref[at(tile), :HEAD_SIZE].T
+    def keep(tile, k, v):
+        keys[at(tile)] = k
+        values[at(tile)] = v
+        keys_t[:, at(tile)] = k.T
         grad_keys[at(tile)] = jnp.zeros((TILE, HEAD_SIZE), F32)
         grad_values[at(tile)] = jnp.zeros((TILE, HEAD_SIZE), F32)
-        return 0
-
-    lax.fori_loop(first, TILES, load, 0)
+
+    load_halves(scalars, first, mine_ref, other_ref, keep)
 
     def blank(tile, _):
         grad_ref[at(tile)] = jnp.zeros((TILE, 2 * HEAD_SIZE), BF16)
@@ -276,9 +294,9 @@
         def gradient_step(limits):
             def step(tile, count):
                 here = at(tile, count)
-                s = scores(kv_ref[here, :HEAD_SIZE], rows_q, tile, count, limits)
+                s = scores(keys[here], rows_q, tile, count, limits)
                 w = jnp.exp2(s - log_total)
-                grad_weights = dot(kv_ref[here, HEAD_SIZE:], rows_d, ((1,), (1,)))
+                grad_weights = dot(values[here], rows_d, ((1,), (1,)))
                 grad_scores = (w * (grad_weights - delta)).astype(BF16)
                 grad_values[here] += dot(w.astype(BF16), rows_d, ((1,), (0,)))
                 grad_keys[here] += dot(grad_scores, rows_q, ((1,), (0,)))
@@ -327,6 +345,7 @@
 RESULT = ((4, CHUNK, ROWS), BF16)
 PIECE = ((CHUNK, ROWS), BF16)
 GRADS = ((SPAN, 2 * HEAD_SIZE), BF16)
+LINES = ((SPAN, HEAD_SIZE), BF16)
 TURNED = ((HEAD_SIZE, SPAN), BF16)
 SQUARE = ((SPAN, ROWS), F32)
 SUMS = ((SPAN, HEAD_SIZE), F32)
@@ -334,26 +353,26 @@
 EIGHT = ((8, ROWS), F32)
 
 
-def run_own_forward(scalars, begin, qd, kv):
+def run_own_forward(scalars, begin, qd, mine, other):
     return call(
-        own_forward, "own_forward", 2, 12, (STATS, ACROSS), (TURNED, SQUARE, EIGHT, EIGHT),
-        scalars, begin, qd, kv,
-    )
-
-
-def run_before_part(scalars, begin, qd, kv, stats, out):
+        own_forward, "own_forward", 2, 12, (STATS, ACROSS), (LINES, TURNED, SQUARE, EIGHT, EIGHT),
+        scalars, begin, qd, mine, other,
+    )
+
+
+def run_before_part(scalars, begin, qd, mine, other, stats, out):
     return call(
         before_part, "before_part", 2, 18, (RESULT, GRADS, STATS, ACROSS),
-        (TURNED, TURNED, SQUARE, SUMS, SUMS, FLAT, ACROSS, EIGHT, EIGHT),
-        scalars, begin, qd, kv, stats, out, hbm_out=(3,), sems=4,
-    )
-
-
-def run_own_backward(scalars, begin, qd, kv, stats, grad_query):
+        (LINES, LINES, TURNED, TURNED, SQUARE, SUMS, SUMS, FLAT, ACROSS, EIGHT, EIGHT),
+        scalars, begin, qd, mine, other, stats, out, hbm_out=(3,), sems=4,
+    )
+
+
+def run_own_backward(scalars, begin, qd, mine, other, stats, grad_query):
     return call(
         own_backward, "own_backward", 3, 60, (PIECE,) * 4 + (GRADS,),
-        (TURNED, SUMS, SUMS, ACROSS, RESULT), scalars, begin, qd, kv, stats, grad_query,
-        hbm_in=(5,), sems=4,
+        (LINES, LINES, TURNED, SUMS, SUMS, ACROSS, RESULT),
+        scalars, begin, qd, mine, other, stats, grad_query, hbm_in=(6,), sems=4,
     )
 
 
@@ -371,16 +390,15 @@
     )(*([scalar] if scalar is not None else []), *args)
 
 
-def pack(queries, output_gradient, keys, values):
-    def kernel(q_ref, d_ref, k_ref, v_ref, qd_ref, kv_ref, sem):
+def pack(y, queries, output_gradient, keys, values):
+    def kernel(y_ref, q_ref, d_ref, k_ref, v_ref, qd_ref, one_ref, two_ref, sem):
         moves = []
         for index, source in enumerate((k_ref, v_ref)):
-            for head in range(2):
-                slot = 2 * head + index
+            for head, target in ((y_ref[0] & 1, one_ref), (1 - (y_ref[0] & 1), two_ref)):
                 moves.append(
                     (
-                        source.at[:, pl.ds(head * HEAD_SIZE, HEAD_SIZE)],
-                        kv_ref.at[:, pl.ds(slot * HEAD_SIZE, HEAD_SIZE)],
+                        source.at[:, pl.ds(pl.multiple_of(head * HEAD_SIZE, HEAD_SIZE), HEAD_SIZE)],
+                        target.at[:, pl.ds(index * HEAD_SIZE, HEAD_SIZE)],
                     )
                 )
         for index, source in enumerate((q_ref, d_ref)):
@@ -400,20 +418,18 @@
         for copy in copies:
             copy.wait()
 
-    hbm = pl.BlockSpec(memory_space=pltpu.HBM)
+    hbm, vmem = pl.BlockSpec(memory_space=pltpu.HBM), pl.BlockSpec(memory_space=pltpu.VMEM)
+    half = jax.ShapeDtypeStruct((CHUNK, 2 * HEAD_SIZE), BF16)
     return pl.pallas_call(
         kernel,
-        out_shape=(
-            jax.ShapeDtypeStruct((4, 2 * CHUNK, ROWS), BF16),
-            jax.ShapeDtypeStruct((CHUNK, 4 * HEAD_SIZE), BF16),
-        ),
-        in_specs=[hbm] * 4,
-        out_specs=(hbm, hbm),
+        out_shape=(jax.ShapeDtypeStruct((4, 2 * CHUNK, ROWS), BF16), half, half),
+        in_specs=[pl.BlockSpec(memory_space=pltpu.SMEM)] + [hbm] * 4,
+        out_specs=(vmem,) * 3,
         scratch_shapes=[pltpu.SemaphoreType.DMA((12,))],
         compiler_params=pltpu.CompilerParams(vmem_limit_bytes=60 << 20),
         cost_estimate=pl.CostEstimate(flops=10**6, bytes_accessed=2 << 20, transcendentals=0),
         name="pack",
-    )(queries, output_gradient, keys, values)
+    )(y, queries, output_gradient, keys, values)
 
 
 def join(y, *pieces):
@@ -449,15 +465,19 @@
     block = lax.axis_index(BLOCK_AXES).astype(jnp.int32)
     blocks = lax.axis_size(BLOCK_AXES)
     own_start = block * SPAN
-    qd, kv = pack(queries, output_gradient, key_projection, value_projection)
+    qd, one, two = pack(y[None], queries, output_gradient, key_projection, value_projection)
+    one = lax.ppermute(one, "y", [(0, 0), (1, 2), (2, 1), (3, 3)])
+    two = lax.ppermute(two, "y", [(0, 2), (1, 0), (2, 3), (3, 1)])
+    mine = jnp.where(y < 2, jnp.stack([one, two]), jnp.stack([two, one]))
+    qd, mine = lax.optimization_barrier((qd, mine))
     qd = lax.all_to_all(qd, "y", split_axis=0, concat_axis=0, tiled=True)
-    kv = lax.all_gather(kv, "z_hi", axis=0, tiled=True)
-    qd, kv = lax.optimization_barrier((qd, kv))
-    first, second = columns(kv, 0, 2), columns(kv, 1, 2)
-    kv_own = lax.all_to_all(
-        jnp.stack([first, first, second, second]), "y", split_axis=0, concat_axis=0, tiled=True
-    ).reshape(SPAN, 2 * HEAD_SIZE)
-    kv_before = lax.ppermute(kv_own, BLOCK_AXES, [(i, i + 1) for i in range(blocks - 1)])
+    mine = lax.all_gather(mine, "z_hi", axis=1, tiled=True)
+    qd, mine = lax.optimization_barrier((qd, mine))
+    mine = mine.reshape(SPAN // 2, 2 * HEAD_SIZE)
+    to_next = [(i, i + 1) for i in range(blocks - 1)]
+    other = lax.ppermute(mine, "y", [(0, 1), (1, 0), (2, 3), (3, 2)])
+    kv_own = (mine, other)
+    kv_before = (lax.ppermute(mine, BLOCK_AXES, to_next), lax.ppermute(other, BLOCK_AXES, to_next))
     docs = doc_lengths.shape[0]
     order = jnp.arange(docs)
     starts = jnp.sum(jnp.where(order[None, :] < order[:, None], doc_lengths[None, :], 0), axis=1)
@@ -467,14 +487,14 @@
     scalars = jnp.concatenate([begin[:, 0], begin[:, -1], z_hi[None], y[None]])
     begin = jnp.tile(begin, (1, HEADS)).reshape(4, 1, ROWS)
 
-    stats, out = run_own_forward(scalars, begin, qd, kv_own)
+    stats, out = run_own_forward(scalars, begin, qd, *kv_own)
     kv_before, stats, out = lax.optimization_barrier((kv_before, stats, out))
     context, grad_before, stats, grad_query = run_before_part(
-        scalars, begin, qd, kv_before, stats, out
+        scalars, begin, qd, *kv_before, stats, out
     )
     returned = lax.ppermute(grad_before, BLOCK_AXES, [(i + 1, i) for i in range(blocks - 1)])
     context = lax.all_to_all(context, "y", split_axis=0, concat_axis=0, tiled=True)
-    *grad_query, grad_own = run_own_backward(scalars, begin, qd, kv_own, stats, grad_query)
+    *grad_query, grad_own = run_own_backward(scalars, begin, qd, *kv_own, stats, grad_query)
     context, returned, grad_own = lax.optimization_barrier((context, returned, grad_own))
     grad_own = (grad_own.astype(F32) + returned.astype(F32)).astype(BF16)
     grad = lax.all_to_all(

time: 195 us -> 162 us (0.83)
  Pallas kernels: 61.6 us -> 30.2 us
  starting transfers between devices: 32.5 us -> 42.2 us
  waiting for transfers between devices: 36.4 us -> 27.1 us
    pallas_call x1, Pallas kernels: 36.9 us -> 2.46 us  [pack(): pl.pallas_call(kernel, out_shape=(jax.ShapeDtypeStruct((4, 2 * CHUNK, ROW...]
    ppermute x1 -> x5, starting transfers between devices: 1.91 us -> 14.9 us  [the longest x1 5.97 us: per_device(): two = lax.ppermute(two, 'y', [(0, 2), (1, 0), (2, 3), (3, 1)])]
    all_to_all x1 -> x0, waiting for transfers between devices: 11.3 us -> none  [per_device(): lax.all_to_all(jnp.stack([first, first, second, second]), 'y', split_axis...]
    all_to_all x1 -> x0, starting transfers between devices: 3.51 us -> none  [per_device(): lax.all_to_all(jnp.stack([first, first, second, second]), 'y', split_axis...]
    pallas_call x3, Pallas kernels: 23.1 us -> 26.2 us  [call(): pl.pallas_call(kernel, out_shape=tuple((jax.ShapeDtypeStruct(shape, dtype...]
    all_to_all x1, waiting for transfers between devices: 14.5 us -> 11.8 us  [per_device(): grad = lax.all_to_all(grad, 'z_hi', split_axis=0, concat_axis=0, tiled=True)]
    ppermute x1 -> x5, waiting for transfers between devices: 7.14 us -> 9.8 us  [the longest x1 5.23 us: per_device(): other = lax.ppermute(mine, 'y', [(0, 1), (1, 0), (2, 3), (3, 2)])]
  transfers between devices with their start and end apart: 9 -> 12, of which waited for: 5 -> 7; matrix products, arithmetic and copies ran while one was open for 1% -> 1% of each run, Pallas kernels for 9% -> 10%
where the time goes in v6:
time: 162 us; the launch traced here: 161 us
  blocking collectives  54.2 us (33%)
  starting transfers between devices  42.2 us (26%)
  Pallas kernels  30.2 us (19%)
  waiting for transfers between devices  27.1 us (17%)
  other arithmetic  4.23 us (3%)
  local copies, waits for them, and re-layouts  1.81 us (1%)
    all_gather x1, blocking collectives, per_device(): mine = lax.all_gather(mine, 'z_hi', axis=1, tiled=True)  34.6 us
    pallas_call x3, Pallas kernels, call(): pl.pallas_call(kernel, out_shape=tuple((jax.ShapeDtypeStruct(shape, dtype...  26.2 us
    all_to_all x1, blocking collectives, per_device(): lax.all_to_all(grad_own.reshape(4, 4, CHUNK, 2 * HEAD_SIZE), 'y', split_a...  19.6 us
    all_to_all x1, waiting for transfers between devices, per_device(): grad = lax.all_to_all(grad, 'z_hi', split_axis=0, concat_axis=0, tiled=True)  11.8 us
    ppermute x3, starting transfers between devices, per_device(): lax.ppermute(grad_query[step], 'y', [(i, (i + step) % 4) for i in range(4)])  8.97 us
    all_to_all x1, starting transfers between devices, per_device(): grad = lax.all_to_all(grad, 'z_hi', split_axis=0, concat_axis=0, tiled=True)  7.89 us
    ppermute x1, starting transfers between devices, per_device(): two = lax.ppermute(two, 'y', [(0, 2), (1, 0), (2, 3), (3, 1)])  5.97 us
    ppermute x1, waiting for transfers between devices, per_device(): other = lax.ppermute(mine, 'y', [(0, 1), (1, 0), (2, 3), (3, 2)])  5.23 us
  transfers between devices with their start and end apart: 12, of which 7 were waited for; matrix products, arithmetic and copies ran while one was open for 1% of the time, Pallas kernels for 10%

profile of v6, /device:TPU:6, one launch (start us, length us, event | category | flops | bytes accessed | tf_op | source)
XLA Modules:
  0.0 160.6 jit_solution(13998824089522944815)
XLA Ops:
  0.6 2.5 %pack.1 = (bf16[4,256,512]{2,1,0:T(8,128)(2,1)}, bf16[128,256]{1,0:T(8,128)(2,1)}, bf16[128,256]{1,0:T(8,128)(2,1)}) custom-call(s32[1]{0:T(128)} %bitcast.1.y_ref, bf16[128,2048]{1,0:T(8,128)(2,1)} %q_ref.1, bf16[128,2048]{1,0:T(8,128)(2,1)} %d_ref.1, bf16[128,256]{1,0:T(8,128)(2,1)} %k_ref.1, bf16[128,256]{1,0:T(8,128)(2,1)} %v_ref.1), custom_call_target="tpu_custom_call" | custom-call | flops 1000000 | bytes 2097152 | tf_op jit(solution)/shard_map/pack/pallas_call | solution.py:423
  4.6 6.0 %collective-permute-start.1 = (bf16[128,256]{1,0:T(8,128)(2,1)}, bf16[128,256]{1,0:T(8,128)(2,1)S(1)}, u32[]{:S(2)}, u32[]{:S(2)}) collective-permute-start(bf16[128,256]{1,0:T(8,128)(2,1)} %get-tuple-element.38), channel_id=1, source_target_pairs={{0,256},{128,0},{256,384},{384,128},{1,257},{129,1},{257,385},{385... | collective-permute-start | bytes 196616 | tf_op jit(solution)/shard_map/ppermute | solution.py:470
  10.6 2.2 %collective-permute-done.1 = bf16[128,256]{1,0:T(8,128)(2,1)S(1)} collective-permute-done((bf16[128,256]{1,0:T(8,128)(2,1)}, bf16[128,256]{1,0:T(8,128)(2,1)S(1)}, u32[]{:S(2)}, u32[]{:S(2)}) %collective-permute-start.1) | collective-permute-done | bytes 65568 | tf_op jit(solution)/shard_map/ppermute | solution.py:470
  12.8 5.0 %all-to-all-start = ((bf16[4,256,512]{2,1,0:T(8,128)(2,1)}), bf16[4,256,512]{2,1,0:T(8,128)(2,1)S(1)}, u32[]{:S(2)}, u32[]{:S(2)}) async-start(bf16[4,256,512]{2,1,0:T(8,128)(2,1)} %get-tuple-element.39), calls=%async_computation | async-start | bytes 2097152 | tf_op jit(solution)/shard_map/all_to_all | solution.py:473
  17.9 34.6 %all_gather.3 = bf16[2,512,256]{2,1,0:T(8,128)(2,1)S(1)} all-gather(bf16[2,128,256]{2,1,0:T(8,128)(2,1)S(1)} %maximum_select_fusion), channel_id=1, replica_groups=mesh['y'=4,'z_hi'=4,'z_lo'=4,'x'=4,'core'=2] {'z_hi'}, dimensions={1}, use_global_device_ids=true | all-gather | bytes 655360 | tf_op jit(solution)/shard_map/all_gather | solution.py:474
  52.5 3.6 %collective-permute-start.3 = (bf16[1024,256]{1,0:T(8,128)(2,1)S(1)}, bf16[1024,256]{1,0:T(8,128)(2,1)S(1)}, u32[]{:S(2)}, u32[]{:S(2)}) collective-permute-start(bf16[1024,256]{1,0:T(8,128)(2,1)S(1)} %bitcast.21), channel_id=1, source_target_pairs={{0,128},{128,0},{256,384},{384,256},{1,129},{129,1},{257,385},{385... | collective-permute-start | bytes 1572872 | tf_op jit(solution)/shard_map/ppermute | solution.py:478
  56.4 1.9 %collective-permute-start.2 = (bf16[1024,256]{1,0:T(8,128)(2,1)S(1)}, bf16[1024,256]{1,0:T(8,128)(2,1)S(1)}, u32[]{:S(2)}, u32[]{:S(2)}) collective-permute-start(bf16[1024,256]{1,0:T(8,128)(2,1)S(1)} %bitcast.22), channel_id=1, source_target_pairs={{0,1},{1,2},{2,3},{3,4},{4,5},{5,6},{6,7},{7,8},{8,9},{9,10},{10,1... | collective-permute-start | bytes 1572872 | tf_op jit(solution)/shard_map/ppermute | solution.py:480
  58.3 5.2 %collective-permute-done.3.other_ref = bf16[1024,256]{1,0:T(8,128)(2,1)S(1)} collective-permute-done((bf16[1024,256]{1,0:T(8,128)(2,1)S(1)}, bf16[1024,256]{1,0:T(8,128)(2,1)S(1)}, u32[]{:S(2)}, u32[]{:S(2)}) %collective-permute-start.3) | collective-permute-done | bytes 524320 | tf_op jit(solution)/shard_map/ppermute | solution.py:478
  63.5 1.9 %collective-permute-start.4 = (bf16[1024,256]{1,0:T(8,128)(2,1)S(1)}, bf16[1024,256]{1,0:T(8,128)(2,1)S(1)}, u32[]{:S(2)}, u32[]{:S(2)}) collective-permute-start(bf16[1024,256]{1,0:T(8,128)(2,1)S(1)} %collective-permute-done.3.other_ref), channel_id=1, source_target_pairs={{0,1},{1,2},{2,3},{3,4},{4,5},{5,6},{6,7},{7,8},{8,9},{9,10},{10,1... | collective-permute-start | bytes 1572872 | tf_op jit(solution)/shard_map/ppermute | solution.py:480
  65.7 5.9 %own_forward.1 = (f32[4,2,512]{2,1,0:T(2,128)S(1)}, f32[4,128,512]{2,1,0:T(8,128)S(1)}) custom-call(s32[10]{0:T(128)S(1)} %pad_add_fusion.scalars, s32[4,1,512]{2,1,0:T(1,128)S(1)} %bitcast.25, bf16[4,256,512]{2,1,0:T(8,128)(2,1)S(1)} %all-to-all-done.qd_ref, bf16[1024,256]{1,0:T(8,128)(2,1)S(1)} %bitcast.23, ...), custom_call_target="tpu_custom_call" | custom-call | flops 2000000000 | bytes 4194304 | tf_op jit(solution)/shard_map/own_forward/pallas_call | solution.py:327
  71.6 2.4 %collective-permute-done.4.other_ref = bf16[1024,256]{1,0:T(8,128)(2,1)S(1)} collective-permute-done((bf16[1024,256]{1,0:T(8,128)(2,1)S(1)}, bf16[1024,256]{1,0:T(8,128)(2,1)S(1)}, u32[]{:S(2)}, u32[]{:S(2)}) %collective-permute-start.4) | collective-permute-done | bytes 524320 | tf_op jit(solution)/shard_map/ppermute | solution.py:480
  74.0 10.7 %before_part.1 = (bf16[4,128,512]{2,1,0:T(8,128)(2,1)}, bf16[2048,256]{1,0:T(8,128)(2,1)S(1)}, f32[4,2,512]{2,1,0:T(2,128)S(1)}, f32[4,128,512]{2,1,0:T(8,128)S(1)}) custom-call(s32[10]{0:T(128)S(1)} %pad_add_fusion.scalars, s32[4,1,512]{2,1,0:T(1,128)S(1)} %bitcast.26, bf16[4,256,512]{2,1,0:T(8,128)(2,1)S(1)} %all-to-all-done.qd_ref, ...), custom_call_target="tpu_custom_call" | custom-call | flops 2000000000 | bytes 4194304 | tf_op jit(solution)/shard_map/before_part/pallas_call | solution.py:327
  86.3 1.9 %collective-permute-start.5 = (bf16[2048,256]{1,0:T(8,128)(2,1)S(1)}, bf16[2048,256]{1,0:T(8,128)(2,1)}, u32[]{:S(2)}, u32[]{:S(2)}) collective-permute-start(bf16[2048,256]{1,0:T(8,128)(2,1)S(1)} %get-tuple-element.50), channel_id=1, source_target_pairs={{1,0},{2,1},{3,2},{4,3},{5,4},{6,5},{7,6},{8,7},{9,8},{10,9},{11,1... | collective-permute-start | bytes 3145736 | tf_op jit(solution)/shard_map/ppermute | solution.py:495
  88.2 3.5 %all-to-all-start.1 = ((bf16[4,128,512]{2,1,0:T(8,128)(2,1)}), bf16[4,128,512]{2,1,0:T(8,128)(2,1)S(1)}, u32[]{:S(2)}, u32[]{:S(2)}) async-start(bf16[4,128,512]{2,1,0:T(8,128)(2,1)} %get-tuple-element.49), calls=%async_computation.1 | async-start | bytes 1048576 | tf_op jit(solution)/shard_map/all_to_all | solution.py:496
  91.7 9.6 %own_backward.1 = (bf16[128,512]{1,0:T(8,128)(2,1)}, bf16[128,512]{1,0:T(8,128)(2,1)}, bf16[128,512]{1,0:T(8,128)(2,1)}, bf16[128,512]{1,0:T(8,128)(2,1)}, bf16[2048,256]{1,0:T(8,128)(2,1)}) custom-call(s32[10]{0:T(128)} %copy-done.4, s32[4,1,512]{2,1,0:T(1,128)} %bitcast.27, bf16[4,256,512]{2,1,0:T(8,128)(2,1)} %copy-done, bf16[1024,256]{1,0:T(8,128)(2,1)} %bitcast.24, ...), custom_call_target="tpu_custom_call" | custom-call | flops 3000000000 | bytes 4194304 | tf_op jit(solution)/shard_map/own_backward/pallas_call | solution.py:327
  102.1 1.8 %add_convert_fusion = bf16[2048,256]{1,0:T(8,128)(2,1)S(1)} fusion(bf16[2048,256]{1,0:T(8,128)(2,1)} %collective-permute-done.5, bf16[2048,256]{1,0:T(8,128)(2,1)} %get-tuple-element.55), kind=kLoop, calls=%fused_computation | loop fusion | flops 2097152 | bytes 3145728 | tf_op jit(solution)/shard_map/convert_element_type | solution.py:499
  103.9 19.6 %all_to_all.20 = bf16[4,4,128,256]{3,2,1,0:T(8,128)(2,1)S(1)} all-to-all(bf16[4,4,128,256]{3,2,1,0:T(8,128)(2,1)S(1)} %bitcast.28), channel_id=1, replica_groups=mesh['y'=4,'z_hi'=4,'z_lo'=4,'x'=4,'core'=2] {'y'}, dimensions={0} | all-to-all | bytes 2097152 | tf_op jit(solution)/shard_map/all_to_all | solution.py:500
  124.8 7.9 %all-to-all-start.3 = ((bf16[4,2,128,256]{3,2,1,0:T(8,128)(2,1)}), bf16[4,2,128,256]{3,2,1,0:T(8,128)(2,1)S(1)}, u32[]{:S(2)}, u32[]{:S(2)}) async-start(bf16[4,2,128,256]{3,2,1,0:T(8,128)(2,1)} %pad_maximum_fusion.1), calls=%async_computation.3 | async-start | bytes 1048576 | tf_op jit(solution)/shard_map/all_to_all | solution.py:507
  132.7 2.5 %collective-permute-start.6 = (bf16[128,512]{1,0:T(8,128)(2,1)S(1)}, bf16[128,512]{1,0:T(8,128)(2,1)S(1)}, u32[]{:S(2)}, u32[]{:S(2)}) collective-permute-start(bf16[128,512]{1,0:T(8,128)(2,1)S(1)} %copy-done.10), channel_id=1, source_target_pairs={{0,128},{128,256},{256,384},{384,0},{1,129},{129,257},{257,385},{3... | collective-permute-start | bytes 393224 | tf_op jit(solution)/shard_map/ppermute | solution.py:509
  135.2 4.0 %collective-permute-start.7 = (bf16[128,512]{1,0:T(8,128)(2,1)S(1)}, bf16[128,512]{1,0:T(8,128)(2,1)S(1)}, u32[]{:S(2)}, u32[]{:S(2)}) collective-permute-start(bf16[128,512]{1,0:T(8,128)(2,1)S(1)} %copy-done.9), channel_id=1, source_target_pairs={{0,256},{128,384},{256,0},{384,128},{1,257},{129,385},{257,1},{385... | collective-permute-start | bytes 393224 | tf_op jit(solution)/shard_map/ppermute | solution.py:509
  139.2 2.5 %collective-permute-start.8 = (bf16[128,512]{1,0:T(8,128)(2,1)S(1)}, bf16[128,512]{1,0:T(8,128)(2,1)S(1)}, u32[]{:S(2)}, u32[]{:S(2)}) collective-permute-start(bf16[128,512]{1,0:T(8,128)(2,1)S(1)} %copy-done.8), channel_id=1, source_target_pairs={{0,384},{128,0},{256,128},{384,256},{1,385},{129,1},{257,129},{385... | collective-permute-start | bytes 393224 | tf_op jit(solution)/shard_map/ppermute | solution.py:509
  142.6 2.3 %collective-permute-done.6.refs_1_ = bf16[128,512]{1,0:T(8,128)(2,1)S(1)} collective-permute-done((bf16[128,512]{1,0:T(8,128)(2,1)S(1)}, bf16[128,512]{1,0:T(8,128)(2,1)S(1)}, u32[]{:S(2)}, u32[]{:S(2)}) %collective-permute-start.6) | collective-permute-done | bytes 131104 | tf_op jit(solution)/shard_map/ppermute | solution.py:509
  144.8 2.5 %collective-permute-done.8.refs_3_ = bf16[128,512]{1,0:T(8,128)(2,1)S(1)} collective-permute-done((bf16[128,512]{1,0:T(8,128)(2,1)S(1)}, bf16[128,512]{1,0:T(8,128)(2,1)S(1)}, u32[]{:S(2)}, u32[]{:S(2)}) %collective-permute-start.8) | collective-permute-done | bytes 131104 | tf_op jit(solution)/shard_map/ppermute | solution.py:509
  148.2 11.8 %all-to-all-done.3.grad_ref = bf16[4,2,128,256]{3,2,1,0:T(8,128)(2,1)S(1)} async-done(((bf16[4,2,128,256]{3,2,1,0:T(8,128)(2,1)}), bf16[4,2,128,256]{3,2,1,0:T(8,128)(2,1)S(1)}, u32[]{:S(2)}, u32[]{:S(2)}) %all-to-all-start.3) | async-done | bytes 524320 | tf_op jit(solution)/shard_map/all_to_all | solution.py:507
  (47 shorter events, 8.0 us)
Async XLA Ops:
  0.6 55.4 %copy-start.11 = (s32[64]{0:T(128)S(1)}, s32[64]{0:T(128)}, u32[]{:S(2)}) copy-start(s32[64]{0:T(128)} %param.9) | copy-start | bytes 772
  3.1 7.5 %collective-permute-start = (bf16[128,256]{1,0:T(8,128)(2,1)}, bf16[128,256]{1,0:T(8,128)(2,1)S(1)}, u32[]{:S(2)}, u32[]{:S(2)}) collective-permute-start(bf16[128,256]{1,0:T(8,128)(2,1)} %get-tuple-element.37), channel_id=1, source_target_pairs={{0,0},{128,256},{256,128},{384,384},{1,1},{129,257},{257,129},{385... | collective-permute-start | bytes 196616 | tf_op jit(solution)/shard_map/ppermute | solution.py:469
  4.6 8.2 %collective-permute-start.1 = (bf16[128,256]{1,0:T(8,128)(2,1)}, bf16[128,256]{1,0:T(8,128)(2,1)S(1)}, u32[]{:S(2)}, u32[]{:S(2)}) collective-permute-start(bf16[128,256]{1,0:T(8,128)(2,1)} %get-tuple-element.38), channel_id=1, source_target_pairs={{0,256},{128,0},{256,384},{384,128},{1,257},{129,1},{257,385},{385... | collective-permute-start | bytes 196616 | tf_op jit(solution)/shard_map/ppermute | solution.py:470
  12.8 39.6 %all-to-all-start = ((bf16[4,256,512]{2,1,0:T(8,128)(2,1)}), bf16[4,256,512]{2,1,0:T(8,128)(2,1)S(1)}, u32[]{:S(2)}, u32[]{:S(2)}) async-start(bf16[4,256,512]{2,1,0:T(8,128)(2,1)} %get-tuple-element.39), calls=%async_computation | async-start | bytes 2097152 | tf_op jit(solution)/shard_map/all_to_all | solution.py:473
  52.4 19.2 %copy-start.1 = (bf16[2,512,256]{2,1,0:T(8,128)(2,1)}, bf16[2,512,256]{2,1,0:T(8,128)(2,1)S(1)}, u32[]{:S(2)}) copy-start(bf16[2,512,256]{2,1,0:T(8,128)(2,1)S(1)} %all_gather.3) | copy-start | bytes 1572868
  52.5 21.6 %copy-start = (bf16[4,256,512]{2,1,0:T(8,128)(2,1)}, bf16[4,256,512]{2,1,0:T(8,128)(2,1)S(1)}, u32[]{:S(2)}) copy-start(bf16[4,256,512]{2,1,0:T(8,128)(2,1)S(1)} %all-to-all-done.qd_ref) | copy-start | bytes 3145732
  52.5 11.1 %collective-permute-start.3 = (bf16[1024,256]{1,0:T(8,128)(2,1)S(1)}, bf16[1024,256]{1,0:T(8,128)(2,1)S(1)}, u32[]{:S(2)}, u32[]{:S(2)}) collective-permute-start(bf16[1024,256]{1,0:T(8,128)(2,1)S(1)} %bitcast.21), channel_id=1, source_target_pairs={{0,128},{128,0},{256,384},{384,256},{1,129},{129,1},{257,385},{385... | collective-permute-start | bytes 1572872 | tf_op jit(solution)/shard_map/ppermute | solution.py:478
  56.4 15.3 %collective-permute-start.2 = (bf16[1024,256]{1,0:T(8,128)(2,1)S(1)}, bf16[1024,256]{1,0:T(8,128)(2,1)S(1)}, u32[]{:S(2)}, u32[]{:S(2)}) collective-permute-start(bf16[1024,256]{1,0:T(8,128)(2,1)S(1)} %bitcast.22), channel_id=1, source_target_pairs={{0,1},{1,2},{2,3},{3,4},{4,5},{5,6},{6,7},{7,8},{8,9},{9,10},{10,1... | collective-permute-start | bytes 1572872 | tf_op jit(solution)/shard_map/ppermute | solution.py:480
  63.5 8.1 %copy-start.5 = (bf16[1024,256]{1,0:T(8,128)(2,1)}, bf16[1024,256]{1,0:T(8,128)(2,1)S(1)}, u32[]{:S(2)}) copy-start(bf16[1024,256]{1,0:T(8,128)(2,1)S(1)} %collective-permute-done.3.other_ref) | copy-start | bytes 1572868
  63.5 10.5 %collective-permute-start.4 = (bf16[1024,256]{1,0:T(8,128)(2,1)S(1)}, bf16[1024,256]{1,0:T(8,128)(2,1)S(1)}, u32[]{:S(2)}, u32[]{:S(2)}) collective-permute-start(bf16[1024,256]{1,0:T(8,128)(2,1)S(1)} %collective-permute-done.3.other_ref), channel_id=1, source_target_pairs={{0,1},{1,2},{2,3},{3,4},{4,5},{5,6},{6,7},{7,8},{8,9},{9,10},{10,1... | collective-permute-start | bytes 1572872 | tf_op jit(solution)/shard_map/ppermute | solution.py:480
  65.7 8.3 %copy-start.4 = (s32[10]{0:T(128)}, s32[10]{0:T(128)S(1)}, u32[]{:S(2)}) copy-start(s32[10]{0:T(128)S(1)} %pad_add_fusion.scalars) | copy-start | bytes 124
  65.7 8.3 %copy-start.3 = (s32[4,4,128]{2,1,0:T(4,128)}, s32[4,4,128]{2,1,0:T(4,128)S(1)}, u32[]{:S(2)}) copy-start(s32[4,4,128]{2,1,0:T(4,128)S(1)} %tile.8) | copy-start | bytes 24580
  84.8 1.0 copy-start.6
  85.7 0.6 copy-start.7
  86.3 15.8 %collective-permute-start.5 = (bf16[2048,256]{1,0:T(8,128)(2,1)S(1)}, bf16[2048,256]{1,0:T(8,128)(2,1)}, u32[]{:S(2)}, u32[]{:S(2)}) collective-permute-start(bf16[2048,256]{1,0:T(8,128)(2,1)S(1)} %get-tuple-element.50), channel_id=1, source_target_pairs={{1,0},{2,1},{3,2},{4,3},{5,4},{6,5},{7,6},{8,7},{9,8},{10,9},{11,1... | collective-permute-start | bytes 3145736 | tf_op jit(solution)/shard_map/ppermute | solution.py:495
  88.2 13.9 %all-to-all-start.1 = ((bf16[4,128,512]{2,1,0:T(8,128)(2,1)}), bf16[4,128,512]{2,1,0:T(8,128)(2,1)S(1)}, u32[]{:S(2)}, u32[]{:S(2)}) async-start(bf16[4,128,512]{2,1,0:T(8,128)(2,1)} %get-tuple-element.49), calls=%async_computation.1 | async-start | bytes 1048576 | tf_op jit(solution)/shard_map/all_to_all | solution.py:496
  123.9 8.8 %copy-start.10 = (bf16[128,512]{1,0:T(8,128)(2,1)S(1)}, bf16[128,512]{1,0:T(8,128)(2,1)}, u32[]{:S(2)}) copy-start(bf16[128,512]{1,0:T(8,128)(2,1)} %get-tuple-element.62) | copy-start | bytes 393220
  123.9 11.3 %copy-start.9 = (bf16[128,512]{1,0:T(8,128)(2,1)S(1)}, bf16[128,512]{1,0:T(8,128)(2,1)}, u32[]{:S(2)}) copy-start(bf16[128,512]{1,0:T(8,128)(2,1)} %get-tuple-element.63) | copy-start | bytes 393220
  123.9 15.3 %copy-start.8 = (bf16[128,512]{1,0:T(8,128)(2,1)S(1)}, bf16[128,512]{1,0:T(8,128)(2,1)}, u32[]{:S(2)}) copy-start(bf16[128,512]{1,0:T(8,128)(2,1)} %get-tuple-element.64) | copy-start | bytes 393220
  123.9 23.4 %copy-start.2 = (bf16[128,512]{1,0:T(8,128)(2,1)S(1)}, bf16[128,512]{1,0:T(8,128)(2,1)}, u32[]{:S(2)}) copy-start(bf16[128,512]{1,0:T(8,128)(2,1)} %get-tuple-element.61.refs_0_) | copy-start | bytes 393220
  124.8 35.2 %all-to-all-start.3 = ((bf16[4,2,128,256]{3,2,1,0:T(8,128)(2,1)}), bf16[4,2,128,256]{3,2,1,0:T(8,128)(2,1)S(1)}, u32[]{:S(2)}, u32[]{:S(2)}) async-start(bf16[4,2,128,256]{3,2,1,0:T(8,128)(2,1)} %pad_maximum_fusion.1), calls=%async_computation.3 | async-start | bytes 1048576 | tf_op jit(solution)/shard_map/all_to_all | solution.py:507
  132.7 12.1 %collective-permute-start.6 = (bf16[128,512]{1,0:T(8,128)(2,1)S(1)}, bf16[128,512]{1,0:T(8,128)(2,1)S(1)}, u32[]{:S(2)}, u32[]{:S(2)}) collective-permute-start(bf16[128,512]{1,0:T(8,128)(2,1)S(1)} %copy-done.10), channel_id=1, source_target_pairs={{0,128},{128,256},{256,384},{384,0},{1,129},{129,257},{257,385},{3... | collective-permute-start | bytes 393224 | tf_op jit(solution)/shard_map/ppermute | solution.py:509
  135.2 9.6 %collective-permute-start.7 = (bf16[128,512]{1,0:T(8,128)(2,1)S(1)}, bf16[128,512]{1,0:T(8,128)(2,1)S(1)}, u32[]{:S(2)}, u32[]{:S(2)}) collective-permute-start(bf16[128,512]{1,0:T(8,128)(2,1)S(1)} %copy-done.9), channel_id=1, source_target_pairs={{0,256},{128,384},{256,0},{384,128},{1,257},{129,385},{257,1},{385... | collective-permute-start | bytes 393224 | tf_op jit(solution)/shard_map/ppermute | solution.py:509
  139.2 8.1 %collective-permute-start.8 = (bf16[128,512]{1,0:T(8,128)(2,1)S(1)}, bf16[128,512]{1,0:T(8,128)(2,1)S(1)}, u32[]{:S(2)}, u32[]{:S(2)}) collective-permute-start(bf16[128,512]{1,0:T(8,128)(2,1)S(1)} %copy-done.8), channel_id=1, source_target_pairs={{0,384},{128,0},{256,128},{384,256},{1,385},{129,1},{257,129},{385... | collective-permute-start | bytes 393224 | tf_op jit(solution)/shard_map/ppermute | solution.py:509

commit v7 on v6

--- a/solution.py
+++ b/solution.py
@@ -14,8 +14,8 @@
 CHUNK = 128
 TILE = 256
 TILES = SPAN // TILE
-GROUP = 4
-BACK_GROUP = 2
+GROUP = (4, 2, 1)
+BACK_GROUP = (2, 1)
 HEADS = 4
 ROWS = HEADS * CHUNK
 BLOCK_AXES = ("z_lo", "x", "core")
@@ -38,29 +38,23 @@
 
 def store_rows(ref, chunk, value):
     for h in range(HEADS):
-        ref[chunk, :, h * HEAD_SIZE : (h + 1) * HEAD_SIZE] = value[
-            h * CHUNK : (h + 1) * CHUNK
-        ].astype(BF16)
+        ref[chunk, :, h * HEAD_SIZE : (h + 1) * HEAD_SIZE] = value[h * CHUNK : (h + 1) * CHUNK]
 
 
 def at(tile, count=1):
     return pl.ds(pl.multiple_of(tile * TILE, TILE), count * TILE)
 
 
-def sweep(low, high, step, group):
-    groups = (high - low) // group
-
-    def many(i, _):
-        step(low + i * group, group)
-        return 0
-
-    def one(i, _):
-        step(i, 1)
-        return 0
-
-    lax.fori_loop(0, groups, many, 0)
-    if group > 1:
-        lax.fori_loop(low + groups * group, high, one, 0)
+def sweep(low, high, step, sizes):
+    for size in sizes:
+        groups = (high - low) // size
+
+        def many(i, _, low=low, size=size):
+            step(low + i * size, size)
+            return 0
+
+        lax.fori_loop(0, groups, many, 0)
+        low = low + groups * size
 
 
 def own_range(scalars, chunk):
@@ -161,8 +155,8 @@
 
 def before_part(
     scalars, begin_ref, qd_ref, mine_ref, other_ref, stats_in, out_in,
-    context_ref, grad_ref, stats_ref, grad_query_ref, keys, values,
-    keys_t, values_t, probs, grad_keys, grad_values, out_t, grad_query, top, total, sem,
+    context_ref, grad_ref, handed_ref, keys, values,
+    keys_t, values_t, probs, grad_keys, grad_values, out_t, handed, top, total, sem,
 ):
     first = jnp.minimum(scalars[0] + SPAN, SPAN) // TILE
 
@@ -184,7 +178,7 @@
 
     def hand_over(chunk):
         return pltpu.make_async_copy(
-            grad_query.at[chunk], grad_query_ref.at[chunk], sem.at[chunk]
+            handed.at[chunk], handed_ref.at[chunk], sem.at[chunk]
         )
 
     def chunk_step(chunk, _):
@@ -195,7 +189,7 @@
         own_top, own_total = stats_in[chunk, 0:1], stats_in[chunk, 1:2]
         top[...] = jnp.broadcast_to(own_top, (8, ROWS))
         total[...] = jnp.zeros((8, ROWS), F32)
-        grad_query[chunk] = jnp.zeros((HEAD_SIZE, ROWS), F32)
+        handed[chunk, :HEAD_SIZE] = jnp.zeros((HEAD_SIZE, ROWS), F32)
 
         def scores_step(limits):
             def step(tile, count):
@@ -223,10 +217,10 @@
         row_total = jnp.sum(total[...], axis=0, keepdims=True) + own_total * rescale
         inverse = 1.0 / row_total
         attended = out_t[...] * inverse
-        delta = jnp.sum(rows_d.astype(F32).T * attended, axis=0, keepdims=True)
-        store_rows(context_ref, chunk, attended.T)
-        stats_ref[chunk, 0:1] = row_top + jnp.log2(row_total)
-        stats_ref[chunk, 1:2] = delta
+        delta = jnp.sum(rows_d.T.astype(F32) * attended, axis=0, keepdims=True)
+        store_rows(context_ref, chunk, attended.astype(BF16).T)
+        handed[chunk, HEAD_SIZE : HEAD_SIZE + 1] = row_top + jnp.log2(row_total)
+        handed[chunk, HEAD_SIZE + 1 : HEAD_SIZE + 2] = delta
 
         def gradient_step(tile, count):
             here = at(tile, count)
@@ -235,7 +229,7 @@
             grad_scores = (w * (grad_weights - delta)).astype(BF16)
             grad_values[here] += dot(w.astype(BF16), rows_d, ((1,), (0,)))
             grad_keys[here] += dot(grad_scores, rows_q, ((1,), (0,)))
-            grad_query[chunk] += dot(keys_t[:, here], grad_scores, ((1,), (0,)))
+            handed[chunk, :HEAD_SIZE] += dot(keys_t[:, here], grad_scores, ((1,), (0,)))
 
         sweep(low, TILES, gradient_step, GROUP)
         hand_over(chunk).start()
@@ -254,15 +248,15 @@
 
 
 def own_backward(
-    scalars, begin_ref, qd_ref, mine_ref, other_ref, stats_in, grad_query_in,
+    scalars, begin_ref, qd_ref, mine_ref, other_ref, handed_in,
     out_0, out_1, out_2, out_3, grad_ref, keys, values,
-    keys_t, grad_keys, grad_values, grad_query_t, grad_query, sem,
+    keys_t, grad_keys, grad_values, handed, grad_query, sem,
 ):
     first = jnp.maximum(scalars[0], 0) // TILE
 
     def fetch(chunk):
         return pltpu.make_async_copy(
-            grad_query_in.at[chunk], grad_query_t.at[chunk], sem.at[chunk]
+            handed_in.at[chunk], handed.at[chunk], sem.at[chunk]
         )
 
     for chunk in range(4):
@@ -288,8 +282,9 @@
         rows_q = rows_of(qd_ref, chunk, 0)
         rows_d = rows_of(qd_ref, chunk, 1)
         limits = (begin_ref[chunk], position_in_rows(start))
-        log_total, delta = stats_in[chunk, 0:1], stats_in[chunk, 1:2]
         fetch(chunk).wait()
+        log_total = handed[chunk, HEAD_SIZE : HEAD_SIZE + 1]
+        delta = handed[chunk, HEAD_SIZE + 1 : HEAD_SIZE + 2]
 
         def gradient_step(limits):
             def step(tile, count):
@@ -300,14 +295,14 @@
                 grad_scores = (w * (grad_weights - delta)).astype(BF16)
                 grad_values[here] += dot(w.astype(BF16), rows_d, ((1,), (0,)))
                 grad_keys[here] += dot(grad_scores, rows_q, ((1,), (0,)))
-                grad_query_t[chunk] += dot(keys_t[:, here], grad_scores, ((1,), (0,)))
+                handed[chunk, :HEAD_SIZE] += dot(keys_t[:, here], grad_scores, ((1,), (0,)))
 
             return step
 
         sweep(low, full_low, gradient_step(limits), BACK_GROUP)
         sweep(full_low, full_high, gradient_step(None), BACK_GROUP)
         sweep(full_high, high, gradient_step(limits), BACK_GROUP)
-        store_rows(grad_query, (chunk - scalars[9]) & 3, (grad_query_t[chunk] * SCALE).T)
+        store_rows(grad_query, (chunk - scalars[9]) & 3, (handed[chunk, :HEAD_SIZE] * SCALE).astype(BF16).T)
         return 0
 
     lax.fori_loop(0, 4, chunk_step, 0)
@@ -342,6 +337,7 @@
 
 STATS = ((4, 2, ROWS), F32)
 ACROSS = ((4, HEAD_SIZE, ROWS), F32)
+HANDED = ((4, HEAD_SIZE + 8, ROWS), F32)
 RESULT = ((4, CHUNK, ROWS), BF16)
 PIECE = ((CHUNK, ROWS), BF16)
 GRADS = ((SPAN, 2 * HEAD_SIZE), BF16)
@@ -362,17 +358,17 @@
 
 def run_before_part(scalars, begin, qd, mine, other, stats, out):
     return call(
-        before_part, "before_part", 2, 18, (RESULT, GRADS, STATS, ACROSS),
-        (LINES, LINES, TURNED, TURNED, SQUARE, SUMS, SUMS, FLAT, ACROSS, EIGHT, EIGHT),
-        scalars, begin, qd, mine, other, stats, out, hbm_out=(3,), sems=4,
-    )
-
-
-def run_own_backward(scalars, begin, qd, mine, other, stats, grad_query):
+        before_part, "before_part", 2, 18, (RESULT, GRADS, HANDED),
+        (LINES, LINES, TURNED, TURNED, SQUARE, SUMS, SUMS, FLAT, HANDED, EIGHT, EIGHT),
+        scalars, begin, qd, mine, other, stats, out, hbm_out=(2,), sems=4,
+    )
+
+
+def run_own_backward(scalars, begin, qd, mine, other, handed):
     return call(
         own_backward, "own_backward", 3, 60, (PIECE,) * 4 + (GRADS,),
-        (LINES, LINES, TURNED, SUMS, SUMS, ACROSS, RESULT),
-        scalars, begin, qd, mine, other, stats, grad_query, hbm_in=(6,), sems=4,
+        (LINES, LINES, TURNED, SUMS, SUMS, HANDED, RESULT),
+        scalars, begin, qd, mine, other, handed, hbm_in=(5,), sems=4,
     )
 
 
@@ -390,46 +386,77 @@
     )(*([scalar] if scalar is not None else []), *args)
 
 
-def pack(y, queries, output_gradient, keys, values):
-    def kernel(y_ref, q_ref, d_ref, k_ref, v_ref, qd_ref, one_ref, two_ref, sem):
-        moves = []
-        for index, source in enumerate((k_ref, v_ref)):
-            for head, target in ((y_ref[0] & 1, one_ref), (1 - (y_ref[0] & 1), two_ref)):
-                moves.append(
-                    (
-                        source.at[:, pl.ds(pl.multiple_of(head * HEAD_SIZE, HEAD_SIZE), HEAD_SIZE)],
-                        target.at[:, pl.ds(index * HEAD_SIZE, HEAD_SIZE)],
-                    )
-                )
-        for index, source in enumerate((q_ref, d_ref)):
-            for d in range(4):
-                moves.append(
-                    (
-                        source.at[:, pl.ds(d * ROWS, ROWS)],
-                        qd_ref.at[d, pl.ds(index * CHUNK, CHUNK)],
-                    )
-                )
-        copies = [
-            pltpu.make_async_copy(source, target, sem.at[n])
-            for n, (source, target) in enumerate(moves)
-        ]
-        for copy in copies:
-            copy.start()
-        for copy in copies:
-            copy.wait()
-
+def copy_all(moves, sem):
+    copies = [
+        pltpu.make_async_copy(source, target, sem.at[n]) for n, (source, target) in enumerate(moves)
+    ]
+    for copy in copies:
+        copy.start()
+    for copy in copies:
+        copy.wait()
+
+
+def packing(kernel, name, outs, scalar, *args, sems):
     hbm, vmem = pl.BlockSpec(memory_space=pltpu.HBM), pl.BlockSpec(memory_space=pltpu.VMEM)
-    half = jax.ShapeDtypeStruct((CHUNK, 2 * HEAD_SIZE), BF16)
+    smem = [pl.BlockSpec(memory_space=pltpu.SMEM)] if scalar is not None else []
     return pl.pallas_call(
         kernel,
-        out_shape=(jax.ShapeDtypeStruct((4, 2 * CHUNK, ROWS), BF16), half, half),
-        in_specs=[pl.BlockSpec(memory_space=pltpu.SMEM)] + [hbm] * 4,
-        out_specs=(vmem,) * 3,
-        scratch_shapes=[pltpu.SemaphoreType.DMA((12,))],
+        out_shape=tuple(jax.ShapeDtypeStruct(shape, dtype) for shape, dtype in outs),
+        in_specs=smem + [hbm] * len(args),
+        out_specs=(vmem,) * len(outs),
+        scratch_shapes=[pltpu.SemaphoreType.DMA((sems,))],
         compiler_params=pltpu.CompilerParams(vmem_limit_bytes=60 << 20),
         cost_estimate=pl.CostEstimate(flops=10**6, bytes_accessed=2 << 20, transcendentals=0),
-        name="pack",
-    )(y, queries, output_gradient, keys, values)
+        name=name,
+    )(*([scalar] if scalar is not None else []), *args)
+
+
+def pack_rows(queries, output_gradient):
+    def kernel(q_ref, d_ref, qd_ref, sem):
+        copy_all(
+            [
+                (
+                    source.at[:, pl.ds(d * ROWS, ROWS)],
+                    qd_ref.at[d, pl.ds(index * CHUNK, CHUNK)],
+                )
+                for index, source in enumerate((q_ref, d_ref))
+                for d in range(4)
+            ],
+            sem,
+        )
+
+    outs = (((4, 2 * CHUNK, ROWS), BF16),)
+    return packing(kernel, "pack_rows", outs, None, queries, output_gradient, sems=8)[0]
+
+
+def pack_heads(y, keys, values):
+    def kernel(y_ref, k_ref, v_ref, one_ref, two_ref, sem):
+        parity = y_ref[0] & 1
+        copy_all(
+            [
+                (
+                    source.at[:, pl.ds(pl.multiple_of(head * HEAD_SIZE, HEAD_SIZE), HEAD_SIZE)],
+                    target.at[:, pl.ds(index * HEAD_SIZE, HEAD_SIZE)],
+                )
+                for index, source in enumerate((k_ref, v_ref))
+                for head, target in ((parity, one_ref), (1 - parity, two_ref))
+            ],
+            sem,
+        )
+
+    outs = (((CHUNK, 2 * HEAD_SIZE), BF16),) * 2
+    return packing(kernel, "pack_heads", outs, y, keys, values, sems=4)
+
+
+def pair_sum(grad):
+    def kernel(grad_ref, out_ref):
+        for place in range(4):
+            for head in range(2):
+                out_ref[place, head] = (
+                    grad_ref[2 * head, place].astype(F32) + grad_ref[2 * head + 1, place].astype(F32)
+                ).astype(BF16)
+
+    return small(kernel, "pair_sum", (((4, 2, CHUNK, 2 * HEAD_SIZE), BF16),), None, grad)[0]
 
 
 def join(y, *pieces):
@@ -465,7 +492,8 @@
     block = lax.axis_index(BLOCK_AXES).astype(jnp.int32)
     blocks = lax.axis_size(BLOCK_AXES)
     own_start = block * SPAN
-    qd, one, two = pack(y[None], queries, output_gradient, key_projection, value_projection)
+    one, two = pack_heads(y[None], key_projection, value_projection)
+    qd = pack_rows(queries, output_gradient)
     one = lax.ppermute(one, "y", [(0, 0), (1, 2), (2, 1), (3, 3)])
     two = lax.ppermute(two, "y", [(0, 2), (1, 0), (2, 3), (3, 1)])
     mine = jnp.where(y < 2, jnp.stack([one, two]), jnp.stack([two, one]))
@@ -489,20 +517,19 @@
 
     stats, out = run_own_forward(scalars, begin, qd, *kv_own)
     kv_before, stats, out = lax.optimization_barrier((kv_before, stats, out))
-    context, grad_before, stats, grad_query = run_before_part(
+    context, grad_before, handed = run_before_part(
         scalars, begin, qd, *kv_before, stats, out
     )
     returned = lax.ppermute(grad_before, BLOCK_AXES, [(i + 1, i) for i in range(blocks - 1)])
     context = lax.all_to_all(context, "y", split_axis=0, concat_axis=0, tiled=True)
-    *grad_query, grad_own = run_own_backward(scalars, begin, qd, *kv_own, stats, grad_query)
+    *grad_query, grad_own = run_own_backward(scalars, begin, qd, *kv_own, handed)
     context, returned, grad_own = lax.optimization_barrier((context, returned, grad_own))
     grad_own = (grad_own.astype(F32) + returned.astype(F32)).astype(BF16)
     grad = lax.all_to_all(
         grad_own.reshape(4, 4, CHUNK, 2 * HEAD_SIZE), "y", split_axis=0, concat_axis=0, tiled=True
     )
 
-    grad = grad.astype(F32)
-    grad = jnp.stack([grad[0] + grad[1], grad[2] + grad[3]], axis=1).astype(BF16)
+    grad = pair_sum(grad)
     grad, *grad_query = lax.optimization_barrier((grad, *grad_query))
     grad = lax.all_to_all(grad, "z_hi", split_axis=0, concat_axis=0, tiled=True)
     pieces = [grad_query[0]] + [

time: 162 us -> 157 us (0.969)
  the two profiles are of different devices: /device:TPU:6 before, /device:TPU:32 now
where the time goes in v7:
time: 157 us; the launch traced here: 156 us
  blocking collectives  51.8 us (33%)
  starting transfers between devices  39.7 us (25%)
  Pallas kernels  33 us (21%)
  waiting for transfers between devices  26.7 us (17%)
  other arithmetic  2.74 us (2%)
    all_gather x1, blocking collectives, per_device(): mine = lax.all_gather(mine, 'z_hi', axis=1, tiled=True)  30.9 us
    pallas_call x3, Pallas kernels, call(): pl.pallas_call(kernel, out_shape=tuple((jax.ShapeDtypeStruct(shape, dtype...  26.7 us
    all_to_all x1, blocking collectives, per_device(): lax.all_to_all(grad_own.reshape(4, 4, CHUNK, 2 * HEAD_SIZE), 'y', split_a...  20.9 us
    all_to_all x1, waiting for transfers between devices, per_device(): grad = lax.all_to_all(grad, 'z_hi', split_axis=0, concat_axis=0, tiled=True)  11.8 us
    ppermute x3, starting transfers between devices, per_device(): lax.ppermute(grad_query[step], 'y', [(i, (i + step) % 4) for i in range(4)])  9.03 us
    ppermute x1, waiting for transfers between devices, per_device(): other = lax.ppermute(mine, 'y', [(0, 1), (1, 0), (2, 3), (3, 2)])  6.18 us
    ppermute x1, starting transfers between devices, per_device(): two = lax.ppermute(two, 'y', [(0, 2), (1, 0), (2, 3), (3, 1)])  5.97 us
    all_to_all x1, starting transfers between devices, per_device(): lax.all_to_all(context, 'y', split_axis=0, concat_axis=0, tiled=True)  5.32 us
  transfers between devices with their start and end apart: 12, of which 5 were waited for; matrix products, arithmetic and copies ran while one was open for 1% of the time, Pallas kernels for 13%

profile of v7, /device:TPU:32, one launch (start us, length us, event | category | flops | bytes accessed | tf_op | source)
XLA Modules:
  0.0 156.2 jit_solution(8030261706943146469)
XLA Ops:
  0.6 1.5 pack_heads.1
  2.1 1.5 collective-permute-start
  3.6 6.0 %collective-permute-start.1 = (bf16[128,256]{1,0:T(8,128)(2,1)}, bf16[128,256]{1,0:T(8,128)(2,1)S(1)}, u32[]{:S(2)}, u32[]{:S(2)}) collective-permute-start(bf16[128,256]{1,0:T(8,128)(2,1)} %get-tuple-element.35), channel_id=1, source_target_pairs={{0,256},{128,0},{256,384},{384,128},{1,257},{129,1},{257,385},{385... | collective-permute-start | bytes 196616 | tf_op jit(solution)/shard_map/ppermute | solution.py:498
  9.6 2.3 %pack_rows.1 = bf16[4,256,512]{2,1,0:T(8,128)(2,1)} custom-call(bf16[128,2048]{1,0:T(8,128)(2,1)} %q_ref.1, bf16[128,2048]{1,0:T(8,128)(2,1)} %d_ref.1), custom_call_target="tpu_custom_call" | custom-call | flops 1000000 | bytes 2097152 | tf_op jit(solution)/shard_map/pack_rows/pallas_call | solution.py:402
  12.0 4.9 %all-to-all-start = ((bf16[4,256,512]{2,1,0:T(8,128)(2,1)}), bf16[4,256,512]{2,1,0:T(8,128)(2,1)S(1)}, u32[]{:S(2)}, u32[]{:S(2)}) async-start(bf16[4,256,512]{2,1,0:T(8,128)(2,1)} %pack_rows.1), calls=%async_computation | async-start | bytes 2097152 | tf_op jit(solution)/shard_map/all_to_all | solution.py:501
  16.9 30.9 %all_gather.3 = bf16[2,512,256]{2,1,0:T(8,128)(2,1)S(1)} all-gather(bf16[2,128,256]{2,1,0:T(8,128)(2,1)S(1)} %maximum_select_fusion), channel_id=1, replica_groups=mesh['y'=4,'z_hi'=4,'z_lo'=4,'x'=4,'core'=2] {'z_hi'}, dimensions={1}, use_global_device_ids=true | all-gather | bytes 655360 | tf_op jit(solution)/shard_map/all_gather | solution.py:502
  47.8 3.7 %collective-permute-start.3 = (bf16[1024,256]{1,0:T(8,128)(2,1)S(1)}, bf16[1024,256]{1,0:T(8,128)(2,1)S(1)}, u32[]{:S(2)}, u32[]{:S(2)}) collective-permute-start(bf16[1024,256]{1,0:T(8,128)(2,1)S(1)} %bitcast.15), channel_id=1, source_target_pairs={{0,128},{128,0},{256,384},{384,256},{1,129},{129,1},{257,385},{385... | collective-permute-start | bytes 1572872 | tf_op jit(solution)/shard_map/ppermute | solution.py:506
  51.8 1.9 %collective-permute-start.2 = (bf16[1024,256]{1,0:T(8,128)(2,1)S(1)}, bf16[1024,256]{1,0:T(8,128)(2,1)S(1)}, u32[]{:S(2)}, u32[]{:S(2)}) collective-permute-start(bf16[1024,256]{1,0:T(8,128)(2,1)S(1)} %bitcast.16), channel_id=1, source_target_pairs={{0,1},{1,2},{2,3},{3,4},{4,5},{5,6},{6,7},{7,8},{8,9},{9,10},{10,1... | collective-permute-start | bytes 1572872 | tf_op jit(solution)/shard_map/ppermute | solution.py:508
  53.7 6.2 %collective-permute-done.3.other_ref = bf16[1024,256]{1,0:T(8,128)(2,1)S(1)} collective-permute-done((bf16[1024,256]{1,0:T(8,128)(2,1)S(1)}, bf16[1024,256]{1,0:T(8,128)(2,1)S(1)}, u32[]{:S(2)}, u32[]{:S(2)}) %collective-permute-start.3) | collective-permute-done | bytes 524320 | tf_op jit(solution)/shard_map/ppermute | solution.py:506
  59.9 1.9 %collective-permute-start.4 = (bf16[1024,256]{1,0:T(8,128)(2,1)S(1)}, bf16[1024,256]{1,0:T(8,128)(2,1)S(1)}, u32[]{:S(2)}, u32[]{:S(2)}) collective-permute-start(bf16[1024,256]{1,0:T(8,128)(2,1)S(1)} %collective-permute-done.3.other_ref), channel_id=1, source_target_pairs={{0,1},{1,2},{2,3},{3,4},{4,5},{5,6},{6,7},{7,8},{8,9},{9,10},{10,1... | collective-permute-start | bytes 1572872 | tf_op jit(solution)/shard_map/ppermute | solution.py:508
  62.1 6.3 %own_forward.1 = (f32[4,2,512]{2,1,0:T(2,128)S(1)}, f32[4,128,512]{2,1,0:T(8,128)S(1)}) custom-call(s32[10]{0:T(128)S(1)} %pad_add_fusion.scalars, s32[4,1,512]{2,1,0:T(1,128)S(1)} %bitcast.19, bf16[4,256,512]{2,1,0:T(8,128)(2,1)S(1)} %all-to-all-done.qd_ref, bf16[1024,256]{1,0:T(8,128)(2,1)S(1)} %bitcast.17, ...), custom_call_target="tpu_custom_call" | custom-call | flops 2000000000 | bytes 4194304 | tf_op jit(solution)/shard_map/own_forward/pallas_call | solution.py:322
  68.4 4.1 %collective-permute-done.4.other_ref = bf16[1024,256]{1,0:T(8,128)(2,1)S(1)} collective-permute-done((bf16[1024,256]{1,0:T(8,128)(2,1)S(1)}, bf16[1024,256]{1,0:T(8,128)(2,1)S(1)}, u32[]{:S(2)}, u32[]{:S(2)}) %collective-permute-start.4) | collective-permute-done | bytes 524320 | tf_op jit(solution)/shard_map/ppermute | solution.py:508
  72.5 10.2 %before_part.1 = (bf16[4,128,512]{2,1,0:T(8,128)(2,1)}, bf16[2048,256]{1,0:T(8,128)(2,1)S(1)}, f32[4,136,512]{2,1,0:T(8,128)S(1)}) custom-call(s32[10]{0:T(128)S(1)} %pad_add_fusion.scalars, s32[4,1,512]{2,1,0:T(1,128)S(1)} %bitcast.20, bf16[4,256,512]{2,1,0:T(8,128)(2,1)S(1)} %all-to-all-done.qd_ref, bf16[1024,256]{1,0:T(8,128)(2,1)S(1)} %collective-permute-done.2.mine_ref, ...), custom_call_target="tpu_custom_call" | custom-call | flops 2000000000 | bytes 4194304 | tf_op jit(solution)/shard_map/before_part/pallas_call | solution.py:322
  83.7 1.9 %collective-permute-start.5 = (bf16[2048,256]{1,0:T(8,128)(2,1)S(1)}, bf16[2048,256]{1,0:T(8,128)(2,1)S(1)}, u32[]{:S(2)}, u32[]{:S(2)}) collective-permute-start(bf16[2048,256]{1,0:T(8,128)(2,1)S(1)} %get-tuple-element.47), channel_id=1, source_target_pairs={{1,0},{2,1},{3,2},{4,3},{5,4},{6,5},{7,6},{8,7},{9,8},{10,9},{11,1... | collective-permute-start | bytes 3145736 | tf_op jit(solution)/shard_map/ppermute | solution.py:523
  85.7 5.3 %all-to-all-start.1 = ((bf16[4,128,512]{2,1,0:T(8,128)(2,1)}), bf16[4,128,512]{2,1,0:T(8,128)(2,1)S(1)}, u32[]{:S(2)}, u32[]{:S(2)}) async-start(bf16[4,128,512]{2,1,0:T(8,128)(2,1)} %get-tuple-element.46), calls=%async_computation.1 | async-start | bytes 1048576 | tf_op jit(solution)/shard_map/all_to_all | solution.py:524
  91.0 10.3 %own_backward.1 = (bf16[128,512]{1,0:T(8,128)(2,1)}, bf16[128,512]{1,0:T(8,128)(2,1)}, bf16[128,512]{1,0:T(8,128)(2,1)}, bf16[128,512]{1,0:T(8,128)(2,1)}, bf16[2048,256]{1,0:T(8,128)(2,1)}) custom-call(s32[10]{0:T(128)} %copy-done.4, s32[4,1,512]{2,1,0:T(1,128)} %bitcast.21, bf16[4,256,512]{2,1,0:T(8,128)(2,1)} %copy-done, bf16[1024,256]{1,0:T(8,128)(2,1)} %bitcast.18, ...), custom_call_target="tpu_custom_call" | custom-call | flops 3000000000 | bytes 4194304 | tf_op jit(solution)/shard_map/own_backward/pallas_call | solution.py:322
  102.8 20.9 %all_to_all.20.grad_ref = bf16[4,4,128,256]{3,2,1,0:T(8,128)(2,1)S(1)} all-to-all(bf16[4,4,128,256]{3,2,1,0:T(8,128)(2,1)S(1)} %bitcast.22), channel_id=1, replica_groups=mesh['y'=4,'z_hi'=4,'z_lo'=4,'x'=4,'core'=2] {'y'}, dimensions={0} | all-to-all | bytes 2097152 | tf_op jit(solution)/shard_map/all_to_all | solution.py:528
  124.6 3.6 %all-to-all-start.3 = ((bf16[4,2,128,256]{3,2,1,0:T(8,128)(2,1)}), bf16[4,2,128,256]{3,2,1,0:T(8,128)(2,1)S(1)}, u32[]{:S(2)}, u32[]{:S(2)}) async-start(bf16[4,2,128,256]{3,2,1,0:T(8,128)(2,1)} %pair_sum.1), calls=%async_computation.3 | async-start | bytes 1048576 | tf_op jit(solution)/shard_map/all_to_all | solution.py:534
  128.3 2.5 %collective-permute-start.6 = (bf16[128,512]{1,0:T(8,128)(2,1)S(1)}, bf16[128,512]{1,0:T(8,128)(2,1)S(1)}, u32[]{:S(2)}, u32[]{:S(2)}) collective-permute-start(bf16[128,512]{1,0:T(8,128)(2,1)S(1)} %copy-done.9), channel_id=1, source_target_pairs={{0,128},{128,256},{256,384},{384,0},{1,129},{129,257},{257,385},{3... | collective-permute-start | bytes 393224 | tf_op jit(solution)/shard_map/ppermute | solution.py:536
  130.8 4.0 %collective-permute-start.7 = (bf16[128,512]{1,0:T(8,128)(2,1)S(1)}, bf16[128,512]{1,0:T(8,128)(2,1)S(1)}, u32[]{:S(2)}, u32[]{:S(2)}) collective-permute-start(bf16[128,512]{1,0:T(8,128)(2,1)S(1)} %copy-done.8), channel_id=1, source_target_pairs={{0,256},{128,384},{256,0},{384,128},{1,257},{129,385},{257,1},{385... | collective-permute-start | bytes 393224 | tf_op jit(solution)/shard_map/ppermute | solution.py:536
  134.8 2.6 %collective-permute-start.8 = (bf16[128,512]{1,0:T(8,128)(2,1)S(1)}, bf16[128,512]{1,0:T(8,128)(2,1)S(1)}, u32[]{:S(2)}, u32[]{:S(2)}) collective-permute-start(bf16[128,512]{1,0:T(8,128)(2,1)S(1)} %copy-done.7), channel_id=1, source_target_pairs={{0,384},{128,0},{256,128},{384,256},{1,385},{129,1},{257,129},{385... | collective-permute-start | bytes 393224 | tf_op jit(solution)/shard_map/ppermute | solution.py:536
  138.2 2.1 %collective-permute-done.6.refs_1_ = bf16[128,512]{1,0:T(8,128)(2,1)S(1)} collective-permute-done((bf16[128,512]{1,0:T(8,128)(2,1)S(1)}, bf16[128,512]{1,0:T(8,128)(2,1)S(1)}, u32[]{:S(2)}, u32[]{:S(2)}) %collective-permute-start.6) | collective-permute-done | bytes 131104 | tf_op jit(solution)/shard_map/ppermute | solution.py:536
  140.4 2.5 %collective-permute-done.8.refs_3_ = bf16[128,512]{1,0:T(8,128)(2,1)S(1)} collective-permute-done((bf16[128,512]{1,0:T(8,128)(2,1)S(1)}, bf16[128,512]{1,0:T(8,128)(2,1)S(1)}, u32[]{:S(2)}, u32[]{:S(2)}) %collective-permute-start.8) | collective-permute-done | bytes 131104 | tf_op jit(solution)/shard_map/ppermute | solution.py:536
  143.7 11.8 %all-to-all-done.3.grad_ref = bf16[4,2,128,256]{3,2,1,0:T(8,128)(2,1)S(1)} async-done(((bf16[4,2,128,256]{3,2,1,0:T(8,128)(2,1)}), bf16[4,2,128,256]{3,2,1,0:T(8,128)(2,1)S(1)}, u32[]{:S(2)}, u32[]{:S(2)}) %all-to-all-start.3) | async-done | bytes 524320 | tf_op jit(solution)/shard_map/all_to_all | solution.py:534
  (44 shorter events, 6.5 us)
Async XLA Ops:
  2.1 9.8 %collective-permute-start = (bf16[128,256]{1,0:T(8,128)(2,1)}, bf16[128,256]{1,0:T(8,128)(2,1)S(1)}, u32[]{:S(2)}, u32[]{:S(2)}) collective-permute-start(bf16[128,256]{1,0:T(8,128)(2,1)} %get-tuple-element.34), channel_id=1, source_target_pairs={{0,0},{128,256},{256,128},{384,384},{1,1},{129,257},{257,129},{385... | collective-permute-start | bytes 196616 | tf_op jit(solution)/shard_map/ppermute | solution.py:497
  3.6 8.3 %collective-permute-start.1 = (bf16[128,256]{1,0:T(8,128)(2,1)}, bf16[128,256]{1,0:T(8,128)(2,1)S(1)}, u32[]{:S(2)}, u32[]{:S(2)}) collective-permute-start(bf16[128,256]{1,0:T(8,128)(2,1)} %get-tuple-element.35), channel_id=1, source_target_pairs={{0,256},{128,0},{256,384},{384,128},{1,257},{129,1},{257,385},{385... | collective-permute-start | bytes 196616 | tf_op jit(solution)/shard_map/ppermute | solution.py:498
  12.0 39.5 %copy-start.10 = (s32[64]{0:T(128)S(1)}, s32[64]{0:T(128)}, u32[]{:S(2)}) copy-start(s32[64]{0:T(128)} %param.9) | copy-start | bytes 772
  12.0 35.7 %all-to-all-start = ((bf16[4,256,512]{2,1,0:T(8,128)(2,1)}), bf16[4,256,512]{2,1,0:T(8,128)(2,1)S(1)}, u32[]{:S(2)}, u32[]{:S(2)}) async-start(bf16[4,256,512]{2,1,0:T(8,128)(2,1)} %pack_rows.1), calls=%async_computation | async-start | bytes 2097152 | tf_op jit(solution)/shard_map/all_to_all | solution.py:501
  47.8 20.6 %copy-start.1 = (bf16[2,512,256]{2,1,0:T(8,128)(2,1)}, bf16[2,512,256]{2,1,0:T(8,128)(2,1)S(1)}, u32[]{:S(2)}) copy-start(bf16[2,512,256]{2,1,0:T(8,128)(2,1)S(1)} %all_gather.3) | copy-start | bytes 1572868
  47.8 24.8 %copy-start = (bf16[4,256,512]{2,1,0:T(8,128)(2,1)}, bf16[4,256,512]{2,1,0:T(8,128)(2,1)S(1)}, u32[]{:S(2)}) copy-start(bf16[4,256,512]{2,1,0:T(8,128)(2,1)S(1)} %all-to-all-done.qd_ref) | copy-start | bytes 3145732
  47.8 12.2 %collective-permute-start.3 = (bf16[1024,256]{1,0:T(8,128)(2,1)S(1)}, bf16[1024,256]{1,0:T(8,128)(2,1)S(1)}, u32[]{:S(2)}, u32[]{:S(2)}) collective-permute-start(bf16[1024,256]{1,0:T(8,128)(2,1)S(1)} %bitcast.15), channel_id=1, source_target_pairs={{0,128},{128,0},{256,384},{384,256},{1,129},{129,1},{257,385},{385... | collective-permute-start | bytes 1572872 | tf_op jit(solution)/shard_map/ppermute | solution.py:506
  51.8 16.6 %collective-permute-start.2 = (bf16[1024,256]{1,0:T(8,128)(2,1)S(1)}, bf16[1024,256]{1,0:T(8,128)(2,1)S(1)}, u32[]{:S(2)}, u32[]{:S(2)}) collective-permute-start(bf16[1024,256]{1,0:T(8,128)(2,1)S(1)} %bitcast.16), channel_id=1, source_target_pairs={{0,1},{1,2},{2,3},{3,4},{4,5},{5,6},{6,7},{7,8},{8,9},{9,10},{10,1... | collective-permute-start | bytes 1572872 | tf_op jit(solution)/shard_map/ppermute | solution.py:508
  59.9 8.5 %copy-start.5 = (bf16[1024,256]{1,0:T(8,128)(2,1)}, bf16[1024,256]{1,0:T(8,128)(2,1)S(1)}, u32[]{:S(2)}) copy-start(bf16[1024,256]{1,0:T(8,128)(2,1)S(1)} %collective-permute-done.3.other_ref) | copy-start | bytes 1572868
  59.9 12.6 %collective-permute-start.4 = (bf16[1024,256]{1,0:T(8,128)(2,1)S(1)}, bf16[1024,256]{1,0:T(8,128)(2,1)S(1)}, u32[]{:S(2)}, u32[]{:S(2)}) collective-permute-start(bf16[1024,256]{1,0:T(8,128)(2,1)S(1)} %collective-permute-done.3.other_ref), channel_id=1, source_target_pairs={{0,1},{1,2},{2,3},{3,4},{4,5},{5,6},{6,7},{7,8},{8,9},{9,10},{10,1... | collective-permute-start | bytes 1572872 | tf_op jit(solution)/shard_map/ppermute | solution.py:508
  62.1 10.4 %copy-start.4 = (s32[10]{0:T(128)}, s32[10]{0:T(128)S(1)}, u32[]{:S(2)}) copy-start(s32[10]{0:T(128)S(1)} %pad_add_fusion.scalars) | copy-start | bytes 124
  62.1 10.4 %copy-start.3 = (s32[4,4,128]{2,1,0:T(4,128)}, s32[4,4,128]{2,1,0:T(4,128)S(1)}, u32[]{:S(2)}) copy-start(s32[4,4,128]{2,1,0:T(4,128)S(1)} %tile.8) | copy-start | bytes 24580
  82.7 1.0 copy-start.6
  83.7 17.5 %collective-permute-start.5 = (bf16[2048,256]{1,0:T(8,128)(2,1)S(1)}, bf16[2048,256]{1,0:T(8,128)(2,1)S(1)}, u32[]{:S(2)}, u32[]{:S(2)}) collective-permute-start(bf16[2048,256]{1,0:T(8,128)(2,1)S(1)} %get-tuple-element.47), channel_id=1, source_target_pairs={{1,0},{2,1},{3,2},{4,3},{5,4},{6,5},{7,6},{8,7},{9,8},{10,9},{11,1... | collective-permute-start | bytes 3145736 | tf_op jit(solution)/shard_map/ppermute | solution.py:523
  85.7 15.6 %all-to-all-start.1 = ((bf16[4,128,512]{2,1,0:T(8,128)(2,1)}), bf16[4,128,512]{2,1,0:T(8,128)(2,1)S(1)}, u32[]{:S(2)}, u32[]{:S(2)}) async-start(bf16[4,128,512]{2,1,0:T(8,128)(2,1)} %get-tuple-element.46), calls=%async_computation.1 | async-start | bytes 1048576 | tf_op jit(solution)/shard_map/all_to_all | solution.py:524
  124.6 3.7 %copy-start.9 = (bf16[128,512]{1,0:T(8,128)(2,1)S(1)}, bf16[128,512]{1,0:T(8,128)(2,1)}, u32[]{:S(2)}) copy-start(bf16[128,512]{1,0:T(8,128)(2,1)} %get-tuple-element.58) | copy-start | bytes 393220
  124.6 6.2 %copy-start.8 = (bf16[128,512]{1,0:T(8,128)(2,1)S(1)}, bf16[128,512]{1,0:T(8,128)(2,1)}, u32[]{:S(2)}) copy-start(bf16[128,512]{1,0:T(8,128)(2,1)} %get-tuple-element.59) | copy-start | bytes 393220
  124.6 10.2 %copy-start.7 = (bf16[128,512]{1,0:T(8,128)(2,1)S(1)}, bf16[128,512]{1,0:T(8,128)(2,1)}, u32[]{:S(2)}) copy-start(bf16[128,512]{1,0:T(8,128)(2,1)} %get-tuple-element.60) | copy-start | bytes 393220
  124.6 30.9 %all-to-all-start.3 = ((bf16[4,2,128,256]{3,2,1,0:T(8,128)(2,1)}), bf16[4,2,128,256]{3,2,1,0:T(8,128)(2,1)S(1)}, u32[]{:S(2)}, u32[]{:S(2)}) async-start(bf16[4,2,128,256]{3,2,1,0:T(8,128)(2,1)} %pair_sum.1), calls=%async_computation.3 | async-start | bytes 1048576 | tf_op jit(solution)/shard_map/all_to_all | solution.py:534
  128.2 14.6 %copy-start.2 = (bf16[128,512]{1,0:T(8,128)(2,1)S(1)}, bf16[128,512]{1,0:T(8,128)(2,1)}, u32[]{:S(2)}) copy-start(bf16[128,512]{1,0:T(8,128)(2,1)} %get-tuple-element.57.refs_0_) | copy-start | bytes 393220
  128.3 12.1 %collective-permute-start.6 = (bf16[128,512]{1,0:T(8,128)(2,1)S(1)}, bf16[128,512]{1,0:T(8,128)(2,1)S(1)}, u32[]{:S(2)}, u32[]{:S(2)}) collective-permute-start(bf16[128,512]{1,0:T(8,128)(2,1)S(1)} %copy-done.9), channel_id=1, source_target_pairs={{0,128},{128,256},{256,384},{384,0},{1,129},{129,257},{257,385},{3... | collective-permute-start | bytes 393224 | tf_op jit(solution)/shard_map/ppermute | solution.py:536
  130.8 9.6 %collective-permute-start.7 = (bf16[128,512]{1,0:T(8,128)(2,1)S(1)}, bf16[128,512]{1,0:T(8,128)(2,1)S(1)}, u32[]{:S(2)}, u32[]{:S(2)}) collective-permute-start(bf16[128,512]{1,0:T(8,128)(2,1)S(1)} %copy-done.8), channel_id=1, source_target_pairs={{0,256},{128,384},{256,0},{384,128},{1,257},{129,385},{257,1},{385... | collective-permute-start | bytes 393224 | tf_op jit(solution)/shard_map/ppermute | solution.py:536
  134.8 8.1 %collective-permute-start.8 = (bf16[128,512]{1,0:T(8,128)(2,1)S(1)}, bf16[128,512]{1,0:T(8,128)(2,1)S(1)}, u32[]{:S(2)}, u32[]{:S(2)}) collective-permute-start(bf16[128,512]{1,0:T(8,128)(2,1)S(1)} %copy-done.7), channel_id=1, source_target_pairs={{0,384},{128,0},{256,128},{384,256},{1,385},{129,1},{257,129},{385... | collective-permute-start | bytes 393224 | tf_op jit(solution)/shard_map/ppermute | solution.py:536

commit v8 on v7

--- a/solution.py
+++ b/solution.py
@@ -76,17 +76,17 @@
     return start + (lax.broadcasted_iota(jnp.int32, (1, ROWS), 1) & (CHUNK - 1))
 
 
-def load_halves(scalars, first, mine_ref, other_ref, keep):
-    half = TILES // 2
-    for ref, which in ((mine_ref, scalars[9] & 1), (other_ref, 1 - (scalars[9] & 1))):
-        shift = which * half
+def load_quads(scalars, first, quads, keep):
+    span = TILES // 4
+    for place, ref in enumerate(quads):
+        shift = (scalars[9] ^ place) * span
 
         def body(tile, _, ref=ref, shift=shift):
             both = ref[at(tile - shift)]
             keep(tile, both[:, :HEAD_SIZE], both[:, HEAD_SIZE:])
             return 0
 
-        lax.fori_loop(jnp.maximum(first, shift), shift + half, body, 0)
+        lax.fori_loop(jnp.maximum(first, shift), shift + span, body, 0)
 
 
 def scores(keys, rows_q, tile, count, limits):
@@ -106,7 +106,7 @@
 
 
 def own_forward(
-    scalars, begin_ref, qd_ref, mine_ref, other_ref,
+    scalars, begin_ref, qd_ref, quad_0, quad_1, quad_2, quad_3,
     stats_ref, out_ref, keys, values_t, probs, top, total,
 ):
     first = jnp.maximum(scalars[0], 0) // TILE
@@ -115,7 +115,7 @@
         keys[at(tile)] = k
         values_t[:, at(tile)] = v.T
 
-    load_halves(scalars, first, mine_ref, other_ref, keep)
+    load_quads(scalars, first, (quad_0, quad_1, quad_2, quad_3), keep)
 
     def chunk_step(chunk, _):
         start, low, high, full_low, full_high = own_range(scalars, chunk)
@@ -154,7 +154,7 @@
 
 
 def before_part(
-    scalars, begin_ref, qd_ref, mine_ref, other_ref, stats_in, out_in,
+    scalars, begin_ref, qd_ref, quad_0, quad_1, quad_2, quad_3, stats_in, out_in,
     context_ref, grad_ref, handed_ref, keys, values,
     keys_t, values_t, probs, grad_keys, grad_values, out_t, handed, top, total, sem,
 ):
@@ -168,7 +168,7 @@
         grad_keys[at(tile)] = jnp.zeros((TILE, HEAD_SIZE), F32)
         grad_values[at(tile)] = jnp.zeros((TILE, HEAD_SIZE), F32)
 
-    load_halves(scalars, first, mine_ref, other_ref, keep)
+    load_quads(scalars, first, (quad_0, quad_1, quad_2, quad_3), keep)
 
     def blank(tile, _):
         grad_ref[at(tile)] = jnp.zeros((TILE, 2 * HEAD_SIZE), BF16)
@@ -248,7 +248,7 @@
 
 
 def own_backward(
-    scalars, begin_ref, qd_ref, mine_ref, other_ref, handed_in,
+    scalars, begin_ref, qd_ref, quad_0, quad_1, quad_2, quad_3, handed_in,
     out_0, out_1, out_2, out_3, grad_ref, keys, values,
     keys_t, grad_keys, grad_values, handed, grad_query, sem,
 ):
@@ -269,7 +269,7 @@
         grad_keys[at(tile)] = jnp.zeros((TILE, HEAD_SIZE), F32)
         grad_values[at(tile)] = jnp.zeros((TILE, HEAD_SIZE), F32)
 
-    load_halves(scalars, first, mine_ref, other_ref, keep)
+    load_quads(scalars, first, (quad_0, quad_1, quad_2, quad_3), keep)
 
     def blank(tile, _):
         grad_ref[at(tile)] = jnp.zeros((TILE, 2 * HEAD_SIZE), BF16)
@@ -349,26 +349,26 @@
 EIGHT = ((8, ROWS), F32)
 
 
-def run_own_forward(scalars, begin, qd, mine, other):
+def run_own_forward(scalars, begin, qd, kv):
     return call(
         own_forward, "own_forward", 2, 12, (STATS, ACROSS), (LINES, TURNED, SQUARE, EIGHT, EIGHT),
-        scalars, begin, qd, mine, other,
-    )
-
-
-def run_before_part(scalars, begin, qd, mine, other, stats, out):
+        scalars, begin, qd, *kv,
+    )
+
+
+def run_before_part(scalars, begin, qd, kv, stats, out):
     return call(
         before_part, "before_part", 2, 18, (RESULT, GRADS, HANDED),
         (LINES, LINES, TURNED, TURNED, SQUARE, SUMS, SUMS, FLAT, HANDED, EIGHT, EIGHT),
-        scalars, begin, qd, mine, other, stats, out, hbm_out=(2,), sems=4,
-    )
-
-
-def run_own_backward(scalars, begin, qd, mine, other, handed):
+        scalars, begin, qd, *kv, stats, out, hbm_out=(2,), sems=4,
+    )
+
+
+def run_own_backward(scalars, begin, qd, kv, handed):
     return call(
         own_backward, "own_backward", 3, 60, (PIECE,) * 4 + (GRADS,),
         (LINES, LINES, TURNED, SUMS, SUMS, HANDED, RESULT),
-        scalars, begin, qd, mine, other, handed, hbm_in=(5,), sems=4,
+        scalars, begin, qd, *kv, handed, hbm_in=(7,), sems=4,
     )
 
 
@@ -430,22 +430,22 @@
 
 
 def pack_heads(y, keys, values):
-    def kernel(y_ref, k_ref, v_ref, one_ref, two_ref, sem):
-        parity = y_ref[0] & 1
+    def kernel(y_ref, k_ref, v_ref, out_ref, sem):
+        mine = y_ref[0] >> 1
         copy_all(
             [
                 (
                     source.at[:, pl.ds(pl.multiple_of(head * HEAD_SIZE, HEAD_SIZE), HEAD_SIZE)],
-                    target.at[:, pl.ds(index * HEAD_SIZE, HEAD_SIZE)],
+                    out_ref.at[slot, :, pl.ds(index * HEAD_SIZE, HEAD_SIZE)],
                 )
                 for index, source in enumerate((k_ref, v_ref))
-                for head, target in ((parity, one_ref), (1 - parity, two_ref))
+                for slot, head in enumerate((mine, 1 - mine))
             ],
             sem,
         )
 
-    outs = (((CHUNK, 2 * HEAD_SIZE), BF16),) * 2
-    return packing(kernel, "pack_heads", outs, y, keys, values, sems=4)
+    outs = (((2, CHUNK, 2 * HEAD_SIZE), BF16),)
+    return packing(kernel, "pack_heads", outs, y, keys, values, sems=4)[0]
 
 
 def pair_sum(grad):
@@ -492,20 +492,20 @@
     block = lax.axis_index(BLOCK_AXES).astype(jnp.int32)
     blocks = lax.axis_size(BLOCK_AXES)
     own_start = block * SPAN
-    one, two = pack_heads(y[None], key_projection, value_projection)
+    kv = pack_heads(y[None], key_projection, value_projection)
     qd = pack_rows(queries, output_gradient)
-    one = lax.ppermute(one, "y", [(0, 0), (1, 2), (2, 1), (3, 3)])
-    two = lax.ppermute(two, "y", [(0, 2), (1, 0), (2, 3), (3, 1)])
-    mine = jnp.where(y < 2, jnp.stack([one, two]), jnp.stack([two, one]))
-    qd, mine = lax.optimization_barrier((qd, mine))
     qd = lax.all_to_all(qd, "y", split_axis=0, concat_axis=0, tiled=True)
-    mine = lax.all_gather(mine, "z_hi", axis=1, tiled=True)
-    qd, mine = lax.optimization_barrier((qd, mine))
-    mine = mine.reshape(SPAN // 2, 2 * HEAD_SIZE)
+    kv = lax.all_gather(kv, "z_hi", axis=1, tiled=True)
+    qd, kv = lax.optimization_barrier((qd, kv))
+    across = [(i, i ^ 3) for i in range(4)]
+    beside = [(i, i ^ 1) for i in range(4)]
     to_next = [(i, i + 1) for i in range(blocks - 1)]
-    other = lax.ppermute(mine, "y", [(0, 1), (1, 0), (2, 3), (3, 2)])
-    kv_own = (mine, other)
-    kv_before = (lax.ppermute(mine, BLOCK_AXES, to_next), lax.ppermute(other, BLOCK_AXES, to_next))
+    quad_0 = kv[0]
+    quad_3 = lax.ppermute(kv[1], "y", across)
+    quad_1 = lax.ppermute(quad_0, "y", beside)
+    quad_2 = lax.ppermute(quad_3, "y", beside)
+    kv_own = (quad_0, quad_1, quad_2, quad_3)
+    kv_before = tuple(lax.ppermute(quad, BLOCK_AXES, to_next) for quad in kv_own)
     docs = doc_lengths.shape[0]
     order = jnp.arange(docs)
     starts = jnp.sum(jnp.where(order[None, :] < order[:, None], doc_lengths[None, :], 0), axis=1)
@@ -515,14 +515,14 @@
     scalars = jnp.concatenate([begin[:, 0], begin[:, -1], z_hi[None], y[None]])
     begin = jnp.tile(begin, (1, HEADS)).reshape(4, 1, ROWS)
 
-    stats, out = run_own_forward(scalars, begin, qd, *kv_own)
+    stats, out = run_own_forward(scalars, begin, qd, kv_own)
     kv_before, stats, out = lax.optimization_barrier((kv_before, stats, out))
     context, grad_before, handed = run_before_part(
-        scalars, begin, qd, *kv_before, stats, out
+        scalars, begin, qd, kv_before, stats, out
     )
     returned = lax.ppermute(grad_before, BLOCK_AXES, [(i + 1, i) for i in range(blocks - 1)])
     context = lax.all_to_all(context, "y", split_axis=0, concat_axis=0, tiled=True)
-    *grad_query, grad_own = run_own_backward(scalars, begin, qd, *kv_own, handed)
+    *grad_query, grad_own = run_own_backward(scalars, begin, qd, kv_own, handed)
     context, returned, grad_own = lax.optimization_barrier((context, returned, grad_own))
     grad_own = (grad_own.astype(F32) + returned.astype(F32)).astype(BF16)
     grad = lax.all_to_all(

time: 157 us -> 155 us (0.987)
  the two profiles are of different devices: /device:TPU:32 before, /device:TPU:6 now
where the time goes in v8:
time: 155 us; the launch traced here: 154 us
  blocking collectives  54.3 us (35%)
  starting transfers between devices  40.9 us (26%)
  Pallas kernels  30.7 us (20%)
  waiting for transfers between devices  22.9 us (15%)
  other arithmetic  2.72 us (2%)
    all_gather x1, blocking collectives, per_device(): kv = lax.all_gather(kv, 'z_hi', axis=1, tiled=True)  34.7 us
    pallas_call x3, Pallas kernels, call(): pl.pallas_call(kernel, out_shape=tuple((jax.ShapeDtypeStruct(shape, dtype...  24.4 us
    all_to_all x1, blocking collectives, per_device(): lax.all_to_all(grad_own.reshape(4, 4, CHUNK, 2 * HEAD_SIZE), 'y', split_a...  19.6 us
    all_to_all x1, waiting for transfers between devices, per_device(): grad = lax.all_to_all(grad, 'z_hi', split_axis=0, concat_axis=0, tiled=True)  12.9 us
    ppermute x4, starting transfers between devices, per_device(): lax.ppermute(quad, BLOCK_AXES, to_next)  9.43 us
    ppermute x3, starting transfers between devices, per_device(): lax.ppermute(grad_query[step], 'y', [(i, (i + step) % 4) for i in range(4)])  9.11 us
    ppermute x3, waiting for transfers between devices, per_device(): lax.ppermute(grad_query[step], 'y', [(i, (i + step) % 4) for i in range(4)])  5.15 us
    all_to_all x1, starting transfers between devices, per_device(): lax.all_to_all(context, 'y', split_axis=0, concat_axis=0, tiled=True)  4.99 us
  transfers between devices with their start and end apart: 14, of which 7 were waited for; matrix products, arithmetic and copies ran while one was open for 1% of the time, Pallas kernels for 12%

profile of v8, /device:TPU:6, one launch (start us, length us, event | category | flops | bytes accessed | tf_op | source)
XLA Modules:
  0.0 153.8 jit_solution(9970262904765947094)
XLA Ops:
  0.6 2.4 %pack_rows.1 = bf16[4,256,512]{2,1,0:T(8,128)(2,1)} custom-call(bf16[128,2048]{1,0:T(8,128)(2,1)} %q_ref.1, bf16[128,2048]{1,0:T(8,128)(2,1)} %d_ref.1), custom_call_target="tpu_custom_call" | custom-call | flops 1000000 | bytes 2097152 | tf_op jit(solution)/shard_map/pack_rows/pallas_call | solution.py:402
  3.0 4.5 %all-to-all-start = ((bf16[4,256,512]{2,1,0:T(8,128)(2,1)}), bf16[4,256,512]{2,1,0:T(8,128)(2,1)S(1)}, u32[]{:S(2)}, u32[]{:S(2)}) async-start(bf16[4,256,512]{2,1,0:T(8,128)(2,1)} %pack_rows.1), calls=%async_computation | async-start | bytes 2097152 | tf_op jit(solution)/shard_map/all_to_all | solution.py:497
  9.0 34.7 %all_gather.3 = bf16[2,512,256]{2,1,0:T(8,128)(2,1)S(1)} all-gather(bf16[2,128,256]{2,1,0:T(8,128)(2,1)} %pack_heads.1), channel_id=1, replica_groups=mesh['y'=4,'z_hi'=4,'z_lo'=4,'x'=4,'core'=2] {'z_hi'}, dimensions={1}, use_global_device_ids=true | all-gather | bytes 655360 | tf_op jit(solution)/shard_map/all_gather | solution.py:498
  43.7 2.9 %collective-permute-start.3 = (bf16[512,256]{1,0:T(8,128)(2,1)S(1)}, bf16[512,256]{1,0:T(8,128)(2,1)S(1)}, u32[]{:S(2)}, u32[]{:S(2)}) collective-permute-start(bf16[512,256]{1,0:T(8,128)(2,1)S(1)} %get-tuple-element.66), channel_id=1, source_target_pairs={{0,384},{128,256},{256,128},{384,0},{1,385},{129,257},{257,129},{3... | collective-permute-start | bytes 786440 | tf_op jit(solution)/shard_map/ppermute | solution.py:504
  47.0 2.2 %collective-permute-start.1 = (bf16[512,256]{1,0:T(8,128)(2,1)S(1)}, bf16[512,256]{1,0:T(8,128)(2,1)S(1)}, u32[]{:S(2)}, u32[]{:S(2)}) collective-permute-start(bf16[512,256]{1,0:T(8,128)(2,1)S(1)} %get-tuple-element.67.quad_0), channel_id=1, source_target_pairs={{0,128},{128,0},{256,384},{384,256},{1,129},{129,1},{257,385},{385... | collective-permute-start | bytes 786440 | tf_op jit(solution)/shard_map/ppermute | solution.py:505
  49.1 4.1 %collective-permute-done.3.quad_3 = bf16[512,256]{1,0:T(8,128)(2,1)S(1)} collective-permute-done((bf16[512,256]{1,0:T(8,128)(2,1)S(1)}, bf16[512,256]{1,0:T(8,128)(2,1)S(1)}, u32[]{:S(2)}, u32[]{:S(2)}) %collective-permute-start.3) | collective-permute-done | bytes 262176 | tf_op jit(solution)/shard_map/ppermute | solution.py:504
  53.2 1.9 %collective-permute-start.4 = (bf16[512,256]{1,0:T(8,128)(2,1)S(1)}, bf16[512,256]{1,0:T(8,128)(2,1)S(1)}, u32[]{:S(2)}, u32[]{:S(2)}) collective-permute-start(bf16[512,256]{1,0:T(8,128)(2,1)S(1)} %collective-permute-done.3.quad_3), channel_id=1, source_target_pairs={{0,128},{128,0},{256,384},{384,256},{1,129},{129,1},{257,385},{385... | collective-permute-start | bytes 786440 | tf_op jit(solution)/shard_map/ppermute | solution.py:506
  55.3 1.9 %collective-permute-start = (bf16[512,256]{1,0:T(8,128)(2,1)S(1)}, bf16[512,256]{1,0:T(8,128)(2,1)S(1)}, u32[]{:S(2)}, u32[]{:S(2)}) collective-permute-start(bf16[512,256]{1,0:T(8,128)(2,1)S(1)} %get-tuple-element.67.quad_0), channel_id=1, source_target_pairs={{0,1},{1,2},{2,3},{3,4},{4,5},{5,6},{6,7},{7,8},{8,9},{9,10},{10,1... | collective-permute-start | bytes 786440 | tf_op jit(solution)/shard_map/ppermute | solution.py:508
  57.3 2.2 %collective-permute-start.6 = (bf16[512,256]{1,0:T(8,128)(2,1)S(1)}, bf16[512,256]{1,0:T(8,128)(2,1)S(1)}, u32[]{:S(2)}, u32[]{:S(2)}) collective-permute-start(bf16[512,256]{1,0:T(8,128)(2,1)S(1)} %collective-permute-done.3.quad_3), channel_id=1, source_target_pairs={{0,1},{1,2},{2,3},{3,4},{4,5},{5,6},{6,7},{7,8},{8,9},{9,10},{10,1... | collective-permute-start | bytes 786440 | tf_op jit(solution)/shard_map/ppermute | solution.py:508
  59.5 1.9 %collective-permute-start.2 = (bf16[512,256]{1,0:T(8,128)(2,1)S(1)}, bf16[512,256]{1,0:T(8,128)(2,1)S(1)}, u32[]{:S(2)}, u32[]{:S(2)}) collective-permute-start(bf16[512,256]{1,0:T(8,128)(2,1)S(1)} %collective-permute-done.1.quad_1), channel_id=1, source_target_pairs={{0,1},{1,2},{2,3},{3,4},{4,5},{5,6},{6,7},{7,8},{8,9},{9,10},{10,1... | collective-permute-start | bytes 786440 | tf_op jit(solution)/shard_map/ppermute | solution.py:508
  61.5 3.4 %collective-permute-start.5 = (bf16[512,256]{1,0:T(8,128)(2,1)S(1)}, bf16[512,256]{1,0:T(8,128)(2,1)S(1)}, u32[]{:S(2)}, u32[]{:S(2)}) collective-permute-start(bf16[512,256]{1,0:T(8,128)(2,1)S(1)} %collective-permute-done.4.quad_2), channel_id=1, source_target_pairs={{0,1},{1,2},{2,3},{3,4},{4,5},{5,6},{6,7},{7,8},{8,9},{9,10},{10,1... | collective-permute-start | bytes 786440 | tf_op jit(solution)/shard_map/ppermute | solution.py:508
  65.0 6.2 %own_forward.1 = (f32[4,2,512]{2,1,0:T(2,128)S(1)}, f32[4,128,512]{2,1,0:T(8,128)S(1)}) custom-call(s32[10]{0:T(128)S(1)} %pad_add_fusion.scalars, s32[4,1,512]{2,1,0:T(1,128)S(1)} %bitcast.16, bf16[4,256,512]{2,1,0:T(8,128)(2,1)S(1)} %all-to-all-done.qd_ref, bf16[512,256]{1,0:T(8,128)(2,1)S(1)} %get-tuple-element.67.quad_0, ...), custom_call_target="tpu_custom_call" | custom-call | flops 2000000000 | bytes 4194304 | tf_op jit(solution)/shard_map/own_forward/pallas_call | solution.py:322
  71.5 8.2 %before_part.1 = (bf16[4,128,512]{2,1,0:T(8,128)(2,1)}, bf16[2048,256]{1,0:T(8,128)(2,1)S(1)}, f32[4,136,512]{2,1,0:T(8,128)S(1)}) custom-call(s32[10]{0:T(128)S(1)} %pad_add_fusion.scalars, s32[4,1,512]{2,1,0:T(1,128)S(1)} %bitcast.17, bf16[4,256,512]{2,1,0:T(8,128)(2,1)S(1)} %all-to-all-done.qd_ref, bf16[512,256]{1,0:T(8,128)(2,1)S(1)} %collective-permute-done.quad_0, ...), custom_call_target="tpu_custom_call" | custom-call | flops 2000000000 | bytes 4194304 | tf_op jit(solution)/shard_map/before_part/pallas_call | solution.py:322
  80.7 1.9 %collective-permute-start.7 = (bf16[2048,256]{1,0:T(8,128)(2,1)S(1)}, bf16[2048,256]{1,0:T(8,128)(2,1)S(1)}, u32[]{:S(2)}, u32[]{:S(2)}) collective-permute-start(bf16[2048,256]{1,0:T(8,128)(2,1)S(1)} %get-tuple-element.43), channel_id=1, source_target_pairs={{1,0},{2,1},{3,2},{4,3},{5,4},{6,5},{7,6},{8,7},{9,8},{10,9},{11,1... | collective-permute-start | bytes 3145736 | tf_op jit(solution)/shard_map/ppermute | solution.py:523
  82.6 5.0 %all-to-all-start.1 = ((bf16[4,128,512]{2,1,0:T(8,128)(2,1)}), bf16[4,128,512]{2,1,0:T(8,128)(2,1)S(1)}, u32[]{:S(2)}, u32[]{:S(2)}) async-start(bf16[4,128,512]{2,1,0:T(8,128)(2,1)} %get-tuple-element.42), calls=%async_computation.1 | async-start | bytes 1048576 | tf_op jit(solution)/shard_map/all_to_all | solution.py:524
  87.6 10.0 %own_backward.1 = (bf16[128,512]{1,0:T(8,128)(2,1)}, bf16[128,512]{1,0:T(8,128)(2,1)}, bf16[128,512]{1,0:T(8,128)(2,1)}, bf16[128,512]{1,0:T(8,128)(2,1)}, bf16[2048,256]{1,0:T(8,128)(2,1)}) custom-call(s32[10]{0:T(128)} %copy-done.4, s32[4,1,512]{2,1,0:T(1,128)} %bitcast.18, bf16[4,256,512]{2,1,0:T(8,128)(2,1)} %copy-done, bf16[512,256]{1,0:T(8,128)(2,1)} %copy-done.1, ...), custom_call_target="tpu_custom_call" | custom-call | flops 3000000000 | bytes 4194304 | tf_op jit(solution)/shard_map/own_backward/pallas_call | solution.py:322
  99.6 19.6 %all_to_all.20.grad_ref = bf16[4,4,128,256]{3,2,1,0:T(8,128)(2,1)S(1)} all-to-all(bf16[4,4,128,256]{3,2,1,0:T(8,128)(2,1)S(1)} %bitcast.19), channel_id=1, replica_groups=mesh['y'=4,'z_hi'=4,'z_lo'=4,'x'=4,'core'=2] {'y'}, dimensions={0} | all-to-all | bytes 2097152 | tf_op jit(solution)/shard_map/all_to_all | solution.py:528
  120.1 4.0 %all-to-all-start.3 = ((bf16[4,2,128,256]{3,2,1,0:T(8,128)(2,1)}), bf16[4,2,128,256]{3,2,1,0:T(8,128)(2,1)S(1)}, u32[]{:S(2)}, u32[]{:S(2)}) async-start(bf16[4,2,128,256]{3,2,1,0:T(8,128)(2,1)} %pair_sum.1), calls=%async_computation.3 | async-start | bytes 1048576 | tf_op jit(solution)/shard_map/all_to_all | solution.py:534
  124.2 2.6 %collective-permute-start.8 = (bf16[128,512]{1,0:T(8,128)(2,1)S(1)}, bf16[128,512]{1,0:T(8,128)(2,1)S(1)}, u32[]{:S(2)}, u32[]{:S(2)}) collective-permute-start(bf16[128,512]{1,0:T(8,128)(2,1)S(1)} %copy-done.11), channel_id=1, source_target_pairs={{0,128},{128,256},{256,384},{384,0},{1,129},{129,257},{257,385},{3... | collective-permute-start | bytes 393224 | tf_op jit(solution)/shard_map/ppermute | solution.py:536
  126.8 4.0 %collective-permute-start.9 = (bf16[128,512]{1,0:T(8,128)(2,1)S(1)}, bf16[128,512]{1,0:T(8,128)(2,1)S(1)}, u32[]{:S(2)}, u32[]{:S(2)}) collective-permute-start(bf16[128,512]{1,0:T(8,128)(2,1)S(1)} %copy-done.10), channel_id=1, source_target_pairs={{0,256},{128,384},{256,0},{384,128},{1,257},{129,385},{257,1},{385... | collective-permute-start | bytes 393224 | tf_op jit(solution)/shard_map/ppermute | solution.py:536
  130.8 2.5 %collective-permute-start.10 = (bf16[128,512]{1,0:T(8,128)(2,1)S(1)}, bf16[128,512]{1,0:T(8,128)(2,1)S(1)}, u32[]{:S(2)}, u32[]{:S(2)}) collective-permute-start(bf16[128,512]{1,0:T(8,128)(2,1)S(1)} %copy-done.9), channel_id=1, source_target_pairs={{0,384},{128,0},{256,128},{384,256},{1,385},{129,1},{257,129},{385... | collective-permute-start | bytes 393224 | tf_op jit(solution)/shard_map/ppermute | solution.py:536
  134.2 2.4 %collective-permute-done.9.refs_2_ = bf16[128,512]{1,0:T(8,128)(2,1)S(1)} collective-permute-done((bf16[128,512]{1,0:T(8,128)(2,1)S(1)}, bf16[128,512]{1,0:T(8,128)(2,1)S(1)}, u32[]{:S(2)}, u32[]{:S(2)}) %collective-permute-start.9) | collective-permute-done | bytes 131104 | tf_op jit(solution)/shard_map/ppermute | solution.py:536
  136.6 2.7 %collective-permute-done.10.refs_3_ = bf16[128,512]{1,0:T(8,128)(2,1)S(1)} collective-permute-done((bf16[128,512]{1,0:T(8,128)(2,1)S(1)}, bf16[128,512]{1,0:T(8,128)(2,1)S(1)}, u32[]{:S(2)}, u32[]{:S(2)}) %collective-permute-start.10) | collective-permute-done | bytes 131104 | tf_op jit(solution)/shard_map/ppermute | solution.py:536
  140.2 12.9 %all-to-all-done.3.grad_ref = bf16[4,2,128,256]{3,2,1,0:T(8,128)(2,1)S(1)} async-done(((bf16[4,2,128,256]{3,2,1,0:T(8,128)(2,1)}), bf16[4,2,128,256]{3,2,1,0:T(8,128)(2,1)S(1)}, u32[]{:S(2)}, u32[]{:S(2)}) %all-to-all-start.3) | async-done | bytes 524320 | tf_op jit(solution)/shard_map/all_to_all | solution.py:534
  (52 shorter events, 8.8 us)
Async XLA Ops:
  3.0 40.7 %all-to-all-start = ((bf16[4,256,512]{2,1,0:T(8,128)(2,1)}), bf16[4,256,512]{2,1,0:T(8,128)(2,1)S(1)}, u32[]{:S(2)}, u32[]{:S(2)}) async-start(bf16[4,256,512]{2,1,0:T(8,128)(2,1)} %pack_rows.1), calls=%async_computation | async-start | bytes 2097152 | tf_op jit(solution)/shard_map/all_to_all | solution.py:497
  7.5 39.3 %copy-start.12 = (s32[64]{0:T(128)S(1)}, s32[64]{0:T(128)}, u32[]{:S(2)}) copy-start(s32[64]{0:T(128)} %param.9) | copy-start | bytes 772
  43.7 27.8 %copy-start = (bf16[4,256,512]{2,1,0:T(8,128)(2,1)}, bf16[4,256,512]{2,1,0:T(8,128)(2,1)S(1)}, u32[]{:S(2)}) copy-start(bf16[4,256,512]{2,1,0:T(8,128)(2,1)S(1)} %all-to-all-done.qd_ref) | copy-start | bytes 3145732
  43.7 27.4 %copy-start.1 = (bf16[512,256]{1,0:T(8,128)(2,1)}, bf16[512,256]{1,0:T(8,128)(2,1)S(1)}, u32[]{:S(2)}) copy-start(bf16[512,256]{1,0:T(8,128)(2,1)S(1)} %get-tuple-element.67.quad_0) | copy-start | bytes 786436
  43.7 9.5 %collective-permute-start.3 = (bf16[512,256]{1,0:T(8,128)(2,1)S(1)}, bf16[512,256]{1,0:T(8,128)(2,1)S(1)}, u32[]{:S(2)}, u32[]{:S(2)}) collective-permute-start(bf16[512,256]{1,0:T(8,128)(2,1)S(1)} %get-tuple-element.66), channel_id=1, source_target_pairs={{0,384},{128,256},{256,128},{384,0},{1,385},{129,257},{257,129},{3... | collective-permute-start | bytes 786440 | tf_op jit(solution)/shard_map/ppermute | solution.py:504
  47.0 12.5 %collective-permute-start.1 = (bf16[512,256]{1,0:T(8,128)(2,1)S(1)}, bf16[512,256]{1,0:T(8,128)(2,1)S(1)}, u32[]{:S(2)}, u32[]{:S(2)}) collective-permute-start(bf16[512,256]{1,0:T(8,128)(2,1)S(1)} %get-tuple-element.67.quad_0), channel_id=1, source_target_pairs={{0,128},{128,0},{256,384},{384,256},{1,129},{129,1},{257,385},{385... | collective-permute-start | bytes 786440 | tf_op jit(solution)/shard_map/ppermute | solution.py:505
  53.2 18.0 %copy-start.5 = (bf16[512,256]{1,0:T(8,128)(2,1)}, bf16[512,256]{1,0:T(8,128)(2,1)S(1)}, u32[]{:S(2)}) copy-start(bf16[512,256]{1,0:T(8,128)(2,1)S(1)} %collective-permute-done.3.quad_3) | copy-start | bytes 786436
  53.2 8.3 %collective-permute-start.4 = (bf16[512,256]{1,0:T(8,128)(2,1)S(1)}, bf16[512,256]{1,0:T(8,128)(2,1)S(1)}, u32[]{:S(2)}, u32[]{:S(2)}) collective-permute-start(bf16[512,256]{1,0:T(8,128)(2,1)S(1)} %collective-permute-done.3.quad_3), channel_id=1, source_target_pairs={{0,128},{128,0},{256,384},{384,256},{1,129},{129,1},{257,385},{385... | collective-permute-start | bytes 786440 | tf_op jit(solution)/shard_map/ppermute | solution.py:506
  55.3 15.9 %collective-permute-start = (bf16[512,256]{1,0:T(8,128)(2,1)S(1)}, bf16[512,256]{1,0:T(8,128)(2,1)S(1)}, u32[]{:S(2)}, u32[]{:S(2)}) collective-permute-start(bf16[512,256]{1,0:T(8,128)(2,1)S(1)} %get-tuple-element.67.quad_0), channel_id=1, source_target_pairs={{0,1},{1,2},{2,3},{3,4},{4,5},{5,6},{6,7},{7,8},{8,9},{9,10},{10,1... | collective-permute-start | bytes 786440 | tf_op jit(solution)/shard_map/ppermute | solution.py:508
  57.3 14.0 %collective-permute-start.6 = (bf16[512,256]{1,0:T(8,128)(2,1)S(1)}, bf16[512,256]{1,0:T(8,128)(2,1)S(1)}, u32[]{:S(2)}, u32[]{:S(2)}) collective-permute-start(bf16[512,256]{1,0:T(8,128)(2,1)S(1)} %collective-permute-done.3.quad_3), channel_id=1, source_target_pairs={{0,1},{1,2},{2,3},{3,4},{4,5},{5,6},{6,7},{7,8},{8,9},{9,10},{10,1... | collective-permute-start | bytes 786440 | tf_op jit(solution)/shard_map/ppermute | solution.py:508
  59.4 11.8 %copy-start.6 = (bf16[512,256]{1,0:T(8,128)(2,1)}, bf16[512,256]{1,0:T(8,128)(2,1)S(1)}, u32[]{:S(2)}) copy-start(bf16[512,256]{1,0:T(8,128)(2,1)S(1)} %collective-permute-done.1.quad_1) | copy-start | bytes 786436
  59.5 11.8 %collective-permute-start.2 = (bf16[512,256]{1,0:T(8,128)(2,1)S(1)}, bf16[512,256]{1,0:T(8,128)(2,1)S(1)}, u32[]{:S(2)}, u32[]{:S(2)}) collective-permute-start(bf16[512,256]{1,0:T(8,128)(2,1)S(1)} %collective-permute-done.1.quad_1), channel_id=1, source_target_pairs={{0,1},{1,2},{2,3},{3,4},{4,5},{5,6},{6,7},{7,8},{8,9},{9,10},{10,1... | collective-permute-start | bytes 786440 | tf_op jit(solution)/shard_map/ppermute | solution.py:508
  61.5 9.7 %copy-start.7 = (bf16[512,256]{1,0:T(8,128)(2,1)}, bf16[512,256]{1,0:T(8,128)(2,1)S(1)}, u32[]{:S(2)}) copy-start(bf16[512,256]{1,0:T(8,128)(2,1)S(1)} %collective-permute-done.4.quad_2) | copy-start | bytes 786436
  61.5 10.0 %collective-permute-start.5 = (bf16[512,256]{1,0:T(8,128)(2,1)S(1)}, bf16[512,256]{1,0:T(8,128)(2,1)S(1)}, u32[]{:S(2)}, u32[]{:S(2)}) collective-permute-start(bf16[512,256]{1,0:T(8,128)(2,1)S(1)} %collective-permute-done.4.quad_2), channel_id=1, source_target_pairs={{0,1},{1,2},{2,3},{3,4},{4,5},{5,6},{6,7},{7,8},{8,9},{9,10},{10,1... | collective-permute-start | bytes 786440 | tf_op jit(solution)/shard_map/ppermute | solution.py:508
  65.0 6.5 %copy-start.4 = (s32[10]{0:T(128)}, s32[10]{0:T(128)S(1)}, u32[]{:S(2)}) copy-start(s32[10]{0:T(128)S(1)} %pad_add_fusion.scalars) | copy-start | bytes 124
  80.7 17.4 %collective-permute-start.7 = (bf16[2048,256]{1,0:T(8,128)(2,1)S(1)}, bf16[2048,256]{1,0:T(8,128)(2,1)S(1)}, u32[]{:S(2)}, u32[]{:S(2)}) collective-permute-start(bf16[2048,256]{1,0:T(8,128)(2,1)S(1)} %get-tuple-element.43), channel_id=1, source_target_pairs={{1,0},{2,1},{3,2},{4,3},{5,4},{6,5},{7,6},{8,7},{9,8},{10,9},{11,1... | collective-permute-start | bytes 3145736 | tf_op jit(solution)/shard_map/ppermute | solution.py:523
  82.6 15.5 %all-to-all-start.1 = ((bf16[4,128,512]{2,1,0:T(8,128)(2,1)}), bf16[4,128,512]{2,1,0:T(8,128)(2,1)S(1)}, u32[]{:S(2)}, u32[]{:S(2)}) async-start(bf16[4,128,512]{2,1,0:T(8,128)(2,1)} %get-tuple-element.42), calls=%async_computation.1 | async-start | bytes 1048576 | tf_op jit(solution)/shard_map/all_to_all | solution.py:524
  120.1 6.7 %copy-start.10 = (bf16[128,512]{1,0:T(8,128)(2,1)S(1)}, bf16[128,512]{1,0:T(8,128)(2,1)}, u32[]{:S(2)}) copy-start(bf16[128,512]{1,0:T(8,128)(2,1)} %get-tuple-element.55) | copy-start | bytes 393220
  120.1 10.7 %copy-start.9 = (bf16[128,512]{1,0:T(8,128)(2,1)S(1)}, bf16[128,512]{1,0:T(8,128)(2,1)}, u32[]{:S(2)}) copy-start(bf16[128,512]{1,0:T(8,128)(2,1)} %get-tuple-element.56) | copy-start | bytes 393220
  120.1 32.9 %all-to-all-start.3 = ((bf16[4,2,128,256]{3,2,1,0:T(8,128)(2,1)}), bf16[4,2,128,256]{3,2,1,0:T(8,128)(2,1)S(1)}, u32[]{:S(2)}, u32[]{:S(2)}) async-start(bf16[4,2,128,256]{3,2,1,0:T(8,128)(2,1)} %pair_sum.1), calls=%async_computation.3 | async-start | bytes 1048576 | tf_op jit(solution)/shard_map/all_to_all | solution.py:534
  124.1 15.2 %copy-start.2 = (bf16[128,512]{1,0:T(8,128)(2,1)S(1)}, bf16[128,512]{1,0:T(8,128)(2,1)}, u32[]{:S(2)}) copy-start(bf16[128,512]{1,0:T(8,128)(2,1)} %get-tuple-element.53.refs_0_) | copy-start | bytes 393220
  124.2 10.0 %collective-permute-start.8 = (bf16[128,512]{1,0:T(8,128)(2,1)S(1)}, bf16[128,512]{1,0:T(8,128)(2,1)S(1)}, u32[]{:S(2)}, u32[]{:S(2)}) collective-permute-start(bf16[128,512]{1,0:T(8,128)(2,1)S(1)} %copy-done.11), channel_id=1, source_target_pairs={{0,128},{128,256},{256,384},{384,0},{1,129},{129,257},{257,385},{3... | collective-permute-start | bytes 393224 | tf_op jit(solution)/shard_map/ppermute | solution.py:536
  126.8 9.8 %collective-permute-start.9 = (bf16[128,512]{1,0:T(8,128)(2,1)S(1)}, bf16[128,512]{1,0:T(8,128)(2,1)S(1)}, u32[]{:S(2)}, u32[]{:S(2)}) collective-permute-start(bf16[128,512]{1,0:T(8,128)(2,1)S(1)} %copy-done.10), channel_id=1, source_target_pairs={{0,256},{128,384},{256,0},{384,128},{1,257},{129,385},{257,1},{385... | collective-permute-start | bytes 393224 | tf_op jit(solution)/shard_map/ppermute | solution.py:536
  130.8 8.5 %collective-permute-start.10 = (bf16[128,512]{1,0:T(8,128)(2,1)S(1)}, bf16[128,512]{1,0:T(8,128)(2,1)S(1)}, u32[]{:S(2)}, u32[]{:S(2)}) collective-permute-start(bf16[128,512]{1,0:T(8,128)(2,1)S(1)} %copy-done.9), channel_id=1, source_target_pairs={{0,384},{128,0},{256,128},{384,256},{1,385},{129,1},{257,129},{385... | collective-permute-start | bytes 393224 | tf_op jit(solution)/shard_map/ppermute | solution.py:536
  (3 other events, 11.5 us)

commit v9 on v8

--- a/solution.py
+++ b/solution.py
@@ -218,7 +218,7 @@
         inverse = 1.0 / row_total
         attended = out_t[...] * inverse
         delta = jnp.sum(rows_d.T.astype(F32) * attended, axis=0, keepdims=True)
-        store_rows(context_ref, chunk, attended.astype(BF16).T)
+        store_rows(context_ref, (chunk - scalars[9]) & 3, attended.astype(BF16).T)
         handed[chunk, HEAD_SIZE : HEAD_SIZE + 1] = row_top + jnp.log2(row_total)
         handed[chunk, HEAD_SIZE + 1 : HEAD_SIZE + 2] = delta
 
@@ -248,7 +248,7 @@
 
 
 def own_backward(
-    scalars, begin_ref, qd_ref, quad_0, quad_1, quad_2, quad_3, handed_in,
+    scalars, begin_ref, qd_ref, quad_0, quad_1, quad_2, quad_3, handed_in, context_in,
     out_0, out_1, out_2, out_3, grad_ref, keys, values,
     keys_t, grad_keys, grad_values, handed, grad_query, sem,
 ):
@@ -314,7 +314,8 @@
 
     lax.fori_loop(first, TILES, store, 0)
     for slot, out in enumerate((out_0, out_1, out_2, out_3)):
-        out[...] = grad_query[slot]
+        out[:CHUNK] = context_in[slot]
+        out[CHUNK:] = grad_query[slot]
 
 
 def call(kernel, name, gflops, megabytes, outs, scratch, *args, hbm_in=(), hbm_out=(), sems=0):
@@ -339,7 +340,7 @@
 ACROSS = ((4, HEAD_SIZE, ROWS), F32)
 HANDED = ((4, HEAD_SIZE + 8, ROWS), F32)
 RESULT = ((4, CHUNK, ROWS), BF16)
-PIECE = ((CHUNK, ROWS), BF16)
+PIECE = ((2 * CHUNK, ROWS), BF16)
 GRADS = ((SPAN, 2 * HEAD_SIZE), BF16)
 LINES = ((SPAN, HEAD_SIZE), BF16)
 TURNED = ((HEAD_SIZE, SPAN), BF16)
@@ -364,11 +365,11 @@
     )
 
 
-def run_own_backward(scalars, begin, qd, kv, handed):
+def run_own_backward(scalars, begin, qd, kv, handed, context):
     return call(
         own_backward, "own_backward", 3, 60, (PIECE,) * 4 + (GRADS,),
         (LINES, LINES, TURNED, SUMS, SUMS, HANDED, RESULT),
-        scalars, begin, qd, *kv, handed, hbm_in=(7,), sems=4,
+        scalars, begin, qd, *kv, handed, context, hbm_in=(7,), sems=4,
     )
 
 
@@ -461,12 +462,14 @@
 
 def join(y, *pieces):
     def kernel(y_ref, *refs):
-        out = refs[-1]
+        context_ref, grad_ref = refs[4:]
         for step in range(4):
             group = (y_ref[0] - step) & 3
-            out[:, pl.ds(pl.multiple_of(group * ROWS, ROWS), ROWS)] = refs[step][...]
-
-    return small(kernel, "join", (((CHUNK, 4 * ROWS), BF16),), y, *pieces)[0]
+            here = pl.ds(pl.multiple_of(group * ROWS, ROWS), ROWS)
+            context_ref[:, here] = refs[step][:CHUNK]
+            grad_ref[:, here] = refs[step][CHUNK:]
+
+    return small(kernel, "join", (((CHUNK, 4 * ROWS), BF16),) * 2, y, *pieces)
 
 
 def last_sum(grad):
@@ -521,25 +524,23 @@
         scalars, begin, qd, kv_before, stats, out
     )
     returned = lax.ppermute(grad_before, BLOCK_AXES, [(i + 1, i) for i in range(blocks - 1)])
-    context = lax.all_to_all(context, "y", split_axis=0, concat_axis=0, tiled=True)
-    *grad_query, grad_own = run_own_backward(scalars, begin, qd, kv_own, handed)
-    context, returned, grad_own = lax.optimization_barrier((context, returned, grad_own))
+    *results, grad_own = run_own_backward(scalars, begin, qd, kv_own, handed, context)
     grad_own = (grad_own.astype(F32) + returned.astype(F32)).astype(BF16)
     grad = lax.all_to_all(
         grad_own.reshape(4, 4, CHUNK, 2 * HEAD_SIZE), "y", split_axis=0, concat_axis=0, tiled=True
     )
 
     grad = pair_sum(grad)
-    grad, *grad_query = lax.optimization_barrier((grad, *grad_query))
+    grad, *results = lax.optimization_barrier((grad, *results))
     grad = lax.all_to_all(grad, "z_hi", split_axis=0, concat_axis=0, tiled=True)
-    pieces = [grad_query[0]] + [
-        lax.ppermute(grad_query[step], "y", [(i, (i + step) % 4) for i in range(4)])
+    pieces = [results[0]] + [
+        lax.ppermute(results[step], "y", [(i, (i + step) % 4) for i in range(4)])
         for step in (1, 2, 3)
     ]
-    grad_queries = join(y[None], *pieces)
+    context, grad_queries = join(y[None], *pieces)
     keys_gradient, values_gradient = last_sum(grad)
     return (
-        jnp.concatenate([context[i] for i in range(4)], axis=1),
+        context,
         grad_queries,
         keys_gradient,
         values_gradient,

time: 155 us -> 156 us (level)
  the two profiles are of different devices: /device:TPU:6 before, /device:TPU:2 now
where the time goes in v9:
time: 156 us; the launch traced here: 155 us
  blocking collectives  54.6 us (35%)
  starting transfers between devices  42.1 us (27%)
  Pallas kernels  27.6 us (18%)
  waiting for transfers between devices  25.9 us (17%)
  local copies, waits for them, and re-layouts  2.07 us (1%)
  other arithmetic  1.87 us (1%)
    all_gather x1, blocking collectives, per_device(): kv = lax.all_gather(kv, 'z_hi', axis=1, tiled=True)  34.7 us
    pallas_call x3, Pallas kernels, call(): pl.pallas_call(kernel, out_shape=tuple((jax.ShapeDtypeStruct(shape, dtype...  21.1 us
    all_to_all x1, blocking collectives, per_device(): lax.all_to_all(grad_own.reshape(4, 4, CHUNK, 2 * HEAD_SIZE), 'y', split_a...  19.9 us
    ppermute x4, starting transfers between devices, per_device(): lax.ppermute(quad, BLOCK_AXES, to_next)  10.6 us
    ppermute x3, waiting for transfers between devices, per_device(): lax.ppermute(results[step], 'y', [(i, (i + step) % 4) for i in range(4)])  10.3 us
    all_to_all x1, waiting for transfers between devices, per_device(): grad = lax.all_to_all(grad, 'z_hi', split_axis=0, concat_axis=0, tiled=True)  9.55 us
    ppermute x3, starting transfers between devices, per_device(): lax.ppermute(results[step], 'y', [(i, (i + step) % 4) for i in range(4)])  8.96 us
    ppermute x1, starting transfers between devices, per_device(): lax.ppermute(grad_before, BLOCK_AXES, [(i + 1, i) for i in range(blocks -...  6.57 us
  transfers between devices with their start and end apart: 13, of which 5 were waited for; matrix products, arithmetic and copies ran while one was open for 0% of the time, Pallas kernels for 12%

profile of v9, /device:TPU:2, one launch (start us, length us, event | category | flops | bytes accessed | tf_op | source)
XLA Modules:
  0.0 155.1 jit_solution(9198218107337780080)
XLA Ops:
  0.6 2.3 %pack_rows.1 = bf16[4,256,512]{2,1,0:T(8,128)(2,1)} custom-call(bf16[128,2048]{1,0:T(8,128)(2,1)} %q_ref.1, bf16[128,2048]{1,0:T(8,128)(2,1)} %d_ref.1), custom_call_target="tpu_custom_call" | custom-call | flops 1000000 | bytes 2097152 | tf_op jit(solution)/shard_map/pack_rows/pallas_call | solution.py:403
  3.0 4.5 %all-to-all-start = ((bf16[4,256,512]{2,1,0:T(8,128)(2,1)}), bf16[4,256,512]{2,1,0:T(8,128)(2,1)S(1)}, u32[]{:S(2)}, u32[]{:S(2)}) async-start(bf16[4,256,512]{2,1,0:T(8,128)(2,1)} %pack_rows.1), calls=%async_computation | async-start | bytes 2097152 | tf_op jit(solution)/shard_map/all_to_all | solution.py:500
  9.0 34.7 %all_gather.3 = bf16[2,512,256]{2,1,0:T(8,128)(2,1)S(1)} all-gather(bf16[2,128,256]{2,1,0:T(8,128)(2,1)} %pack_heads.1), channel_id=1, replica_groups=mesh['y'=4,'z_hi'=4,'z_lo'=4,'x'=4,'core'=2] {'z_hi'}, dimensions={1}, use_global_device_ids=true | all-gather | bytes 655360 | tf_op jit(solution)/shard_map/all_gather | solution.py:501
  43.7 2.9 %collective-permute-start.1 = (bf16[512,256]{1,0:T(8,128)(2,1)S(1)}, bf16[512,256]{1,0:T(8,128)(2,1)S(1)}, u32[]{:S(2)}, u32[]{:S(2)}) collective-permute-start(bf16[512,256]{1,0:T(8,128)(2,1)S(1)} %get-tuple-element.60), channel_id=1, source_target_pairs={{0,384},{128,256},{256,128},{384,0},{1,385},{129,257},{257,129},{3... | collective-permute-start | bytes 786440 | tf_op jit(solution)/shard_map/ppermute | solution.py:507
  47.0 2.2 %collective-permute-start = (bf16[512,256]{1,0:T(8,128)(2,1)S(1)}, bf16[512,256]{1,0:T(8,128)(2,1)S(1)}, u32[]{:S(2)}, u32[]{:S(2)}) collective-permute-start(bf16[512,256]{1,0:T(8,128)(2,1)S(1)} %get-tuple-element.61.quad_0), channel_id=1, source_target_pairs={{0,128},{128,0},{256,384},{384,256},{1,129},{129,1},{257,385},{385... | collective-permute-start | bytes 786440 | tf_op jit(solution)/shard_map/ppermute | solution.py:508
  49.1 4.1 %collective-permute-done.1.quad_3 = bf16[512,256]{1,0:T(8,128)(2,1)S(1)} collective-permute-done((bf16[512,256]{1,0:T(8,128)(2,1)S(1)}, bf16[512,256]{1,0:T(8,128)(2,1)S(1)}, u32[]{:S(2)}, u32[]{:S(2)}) %collective-permute-start.1) | collective-permute-done | bytes 262176 | tf_op jit(solution)/shard_map/ppermute | solution.py:507
  53.2 1.9 %collective-permute-start.2 = (bf16[512,256]{1,0:T(8,128)(2,1)S(1)}, bf16[512,256]{1,0:T(8,128)(2,1)S(1)}, u32[]{:S(2)}, u32[]{:S(2)}) collective-permute-start(bf16[512,256]{1,0:T(8,128)(2,1)S(1)} %collective-permute-done.1.quad_3), channel_id=1, source_target_pairs={{0,128},{128,0},{256,384},{384,256},{1,129},{129,1},{257,385},{385... | collective-permute-start | bytes 786440 | tf_op jit(solution)/shard_map/ppermute | solution.py:509
  55.3 1.9 %collective-permute-start.3 = (bf16[512,256]{1,0:T(8,128)(2,1)S(1)}, bf16[512,256]{1,0:T(8,128)(2,1)S(1)}, u32[]{:S(2)}, u32[]{:S(2)}) collective-permute-start(bf16[512,256]{1,0:T(8,128)(2,1)S(1)} %get-tuple-element.61.quad_0), channel_id=1, source_target_pairs={{0,1},{1,2},{2,3},{3,4},{4,5},{5,6},{6,7},{7,8},{8,9},{9,10},{10,1... | collective-permute-start | bytes 786440 | tf_op jit(solution)/shard_map/ppermute | solution.py:511
  57.3 3.5 %collective-permute-start.6 = (bf16[512,256]{1,0:T(8,128)(2,1)S(1)}, bf16[512,256]{1,0:T(8,128)(2,1)S(1)}, u32[]{:S(2)}, u32[]{:S(2)}) collective-permute-start(bf16[512,256]{1,0:T(8,128)(2,1)S(1)} %collective-permute-done.1.quad_3), channel_id=1, source_target_pairs={{0,1},{1,2},{2,3},{3,4},{4,5},{5,6},{6,7},{7,8},{8,9},{9,10},{10,1... | collective-permute-start | bytes 786440 | tf_op jit(solution)/shard_map/ppermute | solution.py:511
  60.8 1.9 %collective-permute-start.4 = (bf16[512,256]{1,0:T(8,128)(2,1)S(1)}, bf16[512,256]{1,0:T(8,128)(2,1)S(1)}, u32[]{:S(2)}, u32[]{:S(2)}) collective-permute-start(bf16[512,256]{1,0:T(8,128)(2,1)S(1)} %collective-permute-done.quad_1), channel_id=1, source_target_pairs={{0,1},{1,2},{2,3},{3,4},{4,5},{5,6},{6,7},{7,8},{8,9},{9,10},{10,1... | collective-permute-start | bytes 786440 | tf_op jit(solution)/shard_map/ppermute | solution.py:511
  62.7 3.2 %collective-permute-start.5 = (bf16[512,256]{1,0:T(8,128)(2,1)S(1)}, bf16[512,256]{1,0:T(8,128)(2,1)S(1)}, u32[]{:S(2)}, u32[]{:S(2)}) collective-permute-start(bf16[512,256]{1,0:T(8,128)(2,1)S(1)} %collective-permute-done.2.quad_2), channel_id=1, source_target_pairs={{0,1},{1,2},{2,3},{3,4},{4,5},{5,6},{6,7},{7,8},{8,9},{9,10},{10,1... | collective-permute-start | bytes 786440 | tf_op jit(solution)/shard_map/ppermute | solution.py:511
  66.0 6.1 %own_forward.1 = (f32[4,2,512]{2,1,0:T(2,128)S(1)}, f32[4,128,512]{2,1,0:T(8,128)S(1)}) custom-call(s32[10]{0:T(128)S(1)} %pad_add_fusion.scalars, s32[4,1,512]{2,1,0:T(1,128)S(1)} %bitcast.8, bf16[4,256,512]{2,1,0:T(8,128)(2,1)S(1)} %all-to-all-done.qd_ref, bf16[512,256]{1,0:T(8,128)(2,1)S(1)} %get-tuple-element.61.quad_0, ...), custom_call_target="tpu_custom_call" | custom-call | flops 2000000000 | bytes 4194304 | tf_op jit(solution)/shard_map/own_forward/pallas_call | solution.py:323
  72.2 4.7 %before_part.1 = (bf16[4,128,512]{2,1,0:T(8,128)(2,1)S(1)}, bf16[2048,256]{1,0:T(8,128)(2,1)S(1)}, f32[4,136,512]{2,1,0:T(8,128)S(1)}) custom-call(s32[10]{0:T(128)S(1)} %pad_add_fusion.scalars, s32[4,1,512]{2,1,0:T(1,128)S(1)} %bitcast.9, bf16[4,256,512]{2,1,0:T(8,128)(2,1)S(1)} %all-to-all-done.qd_ref, bf16[512,256]{1,0:T(8,128)(2,1)S(1)} %collective-permute-done.3.quad_0, ...), custom_call_target="tpu_custom_call" | custom-call | flops 2000000000 | bytes 4194304 | tf_op jit(solution)/shard_map/before_part/pallas_call | solution.py:323
  78.7 6.6 %collective-permute-start.7 = (bf16[2048,256]{1,0:T(8,128)(2,1)S(1)}, bf16[2048,256]{1,0:T(8,128)(2,1)S(1)}, u32[]{:S(2)}, u32[]{:S(2)}) collective-permute-start(bf16[2048,256]{1,0:T(8,128)(2,1)S(1)} %get-tuple-element.44), channel_id=1, source_target_pairs={{1,0},{2,1},{3,2},{4,3},{5,4},{6,5},{7,6},{8,7},{9,8},{10,9},{11,1... | collective-permute-start | bytes 3145736 | tf_op jit(solution)/shard_map/ppermute | solution.py:526
  85.3 10.4 %own_backward.1 = (bf16[256,512]{1,0:T(8,128)(2,1)}, bf16[256,512]{1,0:T(8,128)(2,1)}, bf16[256,512]{1,0:T(8,128)(2,1)}, bf16[256,512]{1,0:T(8,128)(2,1)}, bf16[2048,256]{1,0:T(8,128)(2,1)}) custom-call(s32[10]{0:T(128)} %copy-done.4, s32[4,1,512]{2,1,0:T(1,128)} %bitcast.10, bf16[4,256,512]{2,1,0:T(8,128)(2,1)} %copy-done, bf16[512,256]{1,0:T(8,128)(2,1)} %copy-done.1, ...), custom_call_target="tpu_custom_call" | custom-call | flops 3000000000 | bytes 4194304 | tf_op jit(solution)/shard_map/own_backward/pallas_call | solution.py:323
  95.7 1.9 %collective-permute-done.7 = bf16[2048,256]{1,0:T(8,128)(2,1)S(1)} collective-permute-done((bf16[2048,256]{1,0:T(8,128)(2,1)S(1)}, bf16[2048,256]{1,0:T(8,128)(2,1)S(1)}, u32[]{:S(2)}, u32[]{:S(2)}) %collective-permute-start.7) | collective-permute-done | bytes 1048608 | tf_op jit(solution)/shard_map/ppermute | solution.py:526
  99.1 19.9 %all_to_all.15.grad_ref = bf16[4,4,128,256]{3,2,1,0:T(8,128)(2,1)S(1)} all-to-all(bf16[4,4,128,256]{3,2,1,0:T(8,128)(2,1)S(1)} %bitcast.11), channel_id=1, replica_groups=mesh['y'=4,'z_hi'=4,'z_lo'=4,'x'=4,'core'=2] {'y'}, dimensions={0} | all-to-all | bytes 2097152 | tf_op jit(solution)/shard_map/all_to_all | solution.py:529
  120.0 4.5 %all-to-all-start.2 = ((bf16[4,2,128,256]{3,2,1,0:T(8,128)(2,1)}), bf16[4,2,128,256]{3,2,1,0:T(8,128)(2,1)S(1)}, u32[]{:S(2)}, u32[]{:S(2)}) async-start(bf16[4,2,128,256]{3,2,1,0:T(8,128)(2,1)} %pair_sum.1), calls=%async_computation.2 | async-start | bytes 1048576 | tf_op jit(solution)/shard_map/all_to_all | solution.py:535
  124.5 2.5 %collective-permute-start.8 = (bf16[256,512]{1,0:T(8,128)(2,1)S(1)}, bf16[256,512]{1,0:T(8,128)(2,1)S(1)}, u32[]{:S(2)}, u32[]{:S(2)}) collective-permute-start(bf16[256,512]{1,0:T(8,128)(2,1)S(1)} %copy-done.12), channel_id=1, source_target_pairs={{0,128},{128,256},{256,384},{384,0},{1,129},{129,257},{257,385},{3... | collective-permute-start | bytes 786440 | tf_op jit(solution)/shard_map/ppermute | solution.py:537
  127.0 4.0 %collective-permute-start.9 = (bf16[256,512]{1,0:T(8,128)(2,1)S(1)}, bf16[256,512]{1,0:T(8,128)(2,1)S(1)}, u32[]{:S(2)}, u32[]{:S(2)}) collective-permute-start(bf16[256,512]{1,0:T(8,128)(2,1)S(1)} %copy-done.11), channel_id=1, source_target_pairs={{0,256},{128,384},{256,0},{384,128},{1,257},{129,385},{257,1},{385... | collective-permute-start | bytes 786440 | tf_op jit(solution)/shard_map/ppermute | solution.py:537
  131.0 2.5 %collective-permute-start.10 = (bf16[256,512]{1,0:T(8,128)(2,1)S(1)}, bf16[256,512]{1,0:T(8,128)(2,1)S(1)}, u32[]{:S(2)}, u32[]{:S(2)}) collective-permute-start(bf16[256,512]{1,0:T(8,128)(2,1)S(1)} %copy-done.10), channel_id=1, source_target_pairs={{0,384},{128,0},{256,128},{384,256},{1,385},{129,1},{257,129},{385... | collective-permute-start | bytes 786440 | tf_op jit(solution)/shard_map/ppermute | solution.py:537
  133.5 7.8 %collective-permute-done.8.refs_1_ = bf16[256,512]{1,0:T(8,128)(2,1)S(1)} collective-permute-done((bf16[256,512]{1,0:T(8,128)(2,1)S(1)}, bf16[256,512]{1,0:T(8,128)(2,1)S(1)}, u32[]{:S(2)}, u32[]{:S(2)}) %collective-permute-start.8) | collective-permute-done | bytes 262176 | tf_op jit(solution)/shard_map/ppermute | solution.py:537
  141.2 2.5 %collective-permute-done.10.refs_3_ = bf16[256,512]{1,0:T(8,128)(2,1)S(1)} collective-permute-done((bf16[256,512]{1,0:T(8,128)(2,1)S(1)}, bf16[256,512]{1,0:T(8,128)(2,1)S(1)}, u32[]{:S(2)}, u32[]{:S(2)}) %collective-permute-start.10) | collective-permute-done | bytes 262176 | tf_op jit(solution)/shard_map/ppermute | solution.py:537
  144.8 9.6 %all-to-all-done.2.grad_ref = bf16[4,2,128,256]{3,2,1,0:T(8,128)(2,1)S(1)} async-done(((bf16[4,2,128,256]{3,2,1,0:T(8,128)(2,1)}), bf16[4,2,128,256]{3,2,1,0:T(8,128)(2,1)S(1)}, u32[]{:S(2)}, u32[]{:S(2)}) %all-to-all-start.2) | async-done | bytes 524320 | tf_op jit(solution)/shard_map/all_to_all | solution.py:535
  (50 shorter events, 8.1 us)
Async XLA Ops:
  3.0 40.7 %all-to-all-start = ((bf16[4,256,512]{2,1,0:T(8,128)(2,1)}), bf16[4,256,512]{2,1,0:T(8,128)(2,1)S(1)}, u32[]{:S(2)}, u32[]{:S(2)}) async-start(bf16[4,256,512]{2,1,0:T(8,128)(2,1)} %pack_rows.1), calls=%async_computation | async-start | bytes 2097152 | tf_op jit(solution)/shard_map/all_to_all | solution.py:500
  7.5 39.3 %copy-start.13 = (s32[64]{0:T(128)S(1)}, s32[64]{0:T(128)}, u32[]{:S(2)}) copy-start(s32[64]{0:T(128)} %param.9) | copy-start | bytes 772
  43.7 28.5 %copy-start = (bf16[4,256,512]{2,1,0:T(8,128)(2,1)}, bf16[4,256,512]{2,1,0:T(8,128)(2,1)S(1)}, u32[]{:S(2)}) copy-start(bf16[4,256,512]{2,1,0:T(8,128)(2,1)S(1)} %all-to-all-done.qd_ref) | copy-start | bytes 3145732
  43.7 28.4 %copy-start.1 = (bf16[512,256]{1,0:T(8,128)(2,1)}, bf16[512,256]{1,0:T(8,128)(2,1)S(1)}, u32[]{:S(2)}) copy-start(bf16[512,256]{1,0:T(8,128)(2,1)S(1)} %get-tuple-element.61.quad_0) | copy-start | bytes 786436
  43.7 9.5 %collective-permute-start.1 = (bf16[512,256]{1,0:T(8,128)(2,1)S(1)}, bf16[512,256]{1,0:T(8,128)(2,1)S(1)}, u32[]{:S(2)}, u32[]{:S(2)}) collective-permute-start(bf16[512,256]{1,0:T(8,128)(2,1)S(1)} %get-tuple-element.60), channel_id=1, source_target_pairs={{0,384},{128,256},{256,128},{384,0},{1,385},{129,257},{257,129},{3... | collective-permute-start | bytes 786440 | tf_op jit(solution)/shard_map/ppermute | solution.py:507
  47.0 13.8 %collective-permute-start = (bf16[512,256]{1,0:T(8,128)(2,1)S(1)}, bf16[512,256]{1,0:T(8,128)(2,1)S(1)}, u32[]{:S(2)}, u32[]{:S(2)}) collective-permute-start(bf16[512,256]{1,0:T(8,128)(2,1)S(1)} %get-tuple-element.61.quad_0), channel_id=1, source_target_pairs={{0,128},{128,0},{256,384},{384,256},{1,129},{129,1},{257,385},{385... | collective-permute-start | bytes 786440 | tf_op jit(solution)/shard_map/ppermute | solution.py:508
  53.2 18.9 %copy-start.5 = (bf16[512,256]{1,0:T(8,128)(2,1)}, bf16[512,256]{1,0:T(8,128)(2,1)S(1)}, u32[]{:S(2)}) copy-start(bf16[512,256]{1,0:T(8,128)(2,1)S(1)} %collective-permute-done.1.quad_3) | copy-start | bytes 786436
  53.2 9.5 %collective-permute-start.2 = (bf16[512,256]{1,0:T(8,128)(2,1)S(1)}, bf16[512,256]{1,0:T(8,128)(2,1)S(1)}, u32[]{:S(2)}, u32[]{:S(2)}) collective-permute-start(bf16[512,256]{1,0:T(8,128)(2,1)S(1)} %collective-permute-done.1.quad_3), channel_id=1, source_target_pairs={{0,128},{128,0},{256,384},{384,256},{1,129},{129,1},{257,385},{385... | collective-permute-start | bytes 786440 | tf_op jit(solution)/shard_map/ppermute | solution.py:509
  55.3 16.8 %collective-permute-start.3 = (bf16[512,256]{1,0:T(8,128)(2,1)S(1)}, bf16[512,256]{1,0:T(8,128)(2,1)S(1)}, u32[]{:S(2)}, u32[]{:S(2)}) collective-permute-start(bf16[512,256]{1,0:T(8,128)(2,1)S(1)} %get-tuple-element.61.quad_0), channel_id=1, source_target_pairs={{0,1},{1,2},{2,3},{3,4},{4,5},{5,6},{6,7},{7,8},{8,9},{9,10},{10,1... | collective-permute-start | bytes 786440 | tf_op jit(solution)/shard_map/ppermute | solution.py:511
  57.3 14.9 %collective-permute-start.6 = (bf16[512,256]{1,0:T(8,128)(2,1)S(1)}, bf16[512,256]{1,0:T(8,128)(2,1)S(1)}, u32[]{:S(2)}, u32[]{:S(2)}) collective-permute-start(bf16[512,256]{1,0:T(8,128)(2,1)S(1)} %collective-permute-done.1.quad_3), channel_id=1, source_target_pairs={{0,1},{1,2},{2,3},{3,4},{4,5},{5,6},{6,7},{7,8},{8,9},{9,10},{10,1... | collective-permute-start | bytes 786440 | tf_op jit(solution)/shard_map/ppermute | solution.py:511
  60.8 11.4 %copy-start.6 = (bf16[512,256]{1,0:T(8,128)(2,1)}, bf16[512,256]{1,0:T(8,128)(2,1)S(1)}, u32[]{:S(2)}) copy-start(bf16[512,256]{1,0:T(8,128)(2,1)S(1)} %collective-permute-done.quad_1) | copy-start | bytes 786436
  60.8 11.4 %collective-permute-start.4 = (bf16[512,256]{1,0:T(8,128)(2,1)S(1)}, bf16[512,256]{1,0:T(8,128)(2,1)S(1)}, u32[]{:S(2)}, u32[]{:S(2)}) collective-permute-start(bf16[512,256]{1,0:T(8,128)(2,1)S(1)} %collective-permute-done.quad_1), channel_id=1, source_target_pairs={{0,1},{1,2},{2,3},{3,4},{4,5},{5,6},{6,7},{7,8},{8,9},{9,10},{10,1... | collective-permute-start | bytes 786440 | tf_op jit(solution)/shard_map/ppermute | solution.py:511
  62.7 9.4 %copy-start.7 = (bf16[512,256]{1,0:T(8,128)(2,1)}, bf16[512,256]{1,0:T(8,128)(2,1)S(1)}, u32[]{:S(2)}) copy-start(bf16[512,256]{1,0:T(8,128)(2,1)S(1)} %collective-permute-done.2.quad_2) | copy-start | bytes 786436
  62.7 9.5 %collective-permute-start.5 = (bf16[512,256]{1,0:T(8,128)(2,1)S(1)}, bf16[512,256]{1,0:T(8,128)(2,1)S(1)}, u32[]{:S(2)}, u32[]{:S(2)}) collective-permute-start(bf16[512,256]{1,0:T(8,128)(2,1)S(1)} %collective-permute-done.2.quad_2), channel_id=1, source_target_pairs={{0,1},{1,2},{2,3},{3,4},{4,5},{5,6},{6,7},{7,8},{8,9},{9,10},{10,1... | collective-permute-start | bytes 786440 | tf_op jit(solution)/shard_map/ppermute | solution.py:511
  66.0 6.2 %copy-start.4 = (s32[10]{0:T(128)}, s32[10]{0:T(128)S(1)}, u32[]{:S(2)}) copy-start(s32[10]{0:T(128)S(1)} %pad_add_fusion.scalars) | copy-start | bytes 124
  66.0 6.2 %copy-start.3 = (s32[4,4,128]{2,1,0:T(4,128)}, s32[4,4,128]{2,1,0:T(4,128)S(1)}, u32[]{:S(2)}) copy-start(s32[4,4,128]{2,1,0:T(4,128)S(1)} %tile.8) | copy-start | bytes 24580
  78.7 18.9 %collective-permute-start.7 = (bf16[2048,256]{1,0:T(8,128)(2,1)S(1)}, bf16[2048,256]{1,0:T(8,128)(2,1)S(1)}, u32[]{:S(2)}, u32[]{:S(2)}) collective-permute-start(bf16[2048,256]{1,0:T(8,128)(2,1)S(1)} %get-tuple-element.44), channel_id=1, source_target_pairs={{1,0},{2,1},{3,2},{4,3},{5,4},{6,5},{7,6},{8,7},{9,8},{10,9},{11,1... | collective-permute-start | bytes 3145736 | tf_op jit(solution)/shard_map/ppermute | solution.py:526
  119.0 7.9 %copy-start.11 = (bf16[256,512]{1,0:T(8,128)(2,1)S(1)}, bf16[256,512]{1,0:T(8,128)(2,1)}, u32[]{:S(2)}) copy-start(bf16[256,512]{1,0:T(8,128)(2,1)} %get-tuple-element.51) | copy-start | bytes 786436
  119.0 11.9 %copy-start.10 = (bf16[256,512]{1,0:T(8,128)(2,1)S(1)}, bf16[256,512]{1,0:T(8,128)(2,1)}, u32[]{:S(2)}) copy-start(bf16[256,512]{1,0:T(8,128)(2,1)} %get-tuple-element.52) | copy-start | bytes 786436
  119.0 24.8 %copy-start.2 = (bf16[256,512]{1,0:T(8,128)(2,1)S(1)}, bf16[256,512]{1,0:T(8,128)(2,1)}, u32[]{:S(2)}) copy-start(bf16[256,512]{1,0:T(8,128)(2,1)} %get-tuple-element.49.refs_0_) | copy-start | bytes 786436
  120.0 34.4 %all-to-all-start.2 = ((bf16[4,2,128,256]{3,2,1,0:T(8,128)(2,1)}), bf16[4,2,128,256]{3,2,1,0:T(8,128)(2,1)S(1)}, u32[]{:S(2)}, u32[]{:S(2)}) async-start(bf16[4,2,128,256]{3,2,1,0:T(8,128)(2,1)} %pair_sum.1), calls=%async_computation.2 | async-start | bytes 1048576 | tf_op jit(solution)/shard_map/all_to_all | solution.py:535
  124.5 16.8 %collective-permute-start.8 = (bf16[256,512]{1,0:T(8,128)(2,1)S(1)}, bf16[256,512]{1,0:T(8,128)(2,1)S(1)}, u32[]{:S(2)}, u32[]{:S(2)}) collective-permute-start(bf16[256,512]{1,0:T(8,128)(2,1)S(1)} %copy-done.12), channel_id=1, source_target_pairs={{0,128},{128,256},{256,384},{384,0},{1,129},{129,257},{257,385},{3... | collective-permute-start | bytes 786440 | tf_op jit(solution)/shard_map/ppermute | solution.py:537
  127.0 14.3 %collective-permute-start.9 = (bf16[256,512]{1,0:T(8,128)(2,1)S(1)}, bf16[256,512]{1,0:T(8,128)(2,1)S(1)}, u32[]{:S(2)}, u32[]{:S(2)}) collective-permute-start(bf16[256,512]{1,0:T(8,128)(2,1)S(1)} %copy-done.11), channel_id=1, source_target_pairs={{0,256},{128,384},{256,0},{384,128},{1,257},{129,385},{257,1},{385... | collective-permute-start | bytes 786440 | tf_op jit(solution)/shard_map/ppermute | solution.py:537
  131.0 12.8 %collective-permute-start.10 = (bf16[256,512]{1,0:T(8,128)(2,1)S(1)}, bf16[256,512]{1,0:T(8,128)(2,1)S(1)}, u32[]{:S(2)}, u32[]{:S(2)}) collective-permute-start(bf16[256,512]{1,0:T(8,128)(2,1)S(1)} %copy-done.10), channel_id=1, source_target_pairs={{0,384},{128,0},{256,128},{384,256},{1,385},{129,1},{257,129},{385... | collective-permute-start | bytes 786440 | tf_op jit(solution)/shard_map/ppermute | solution.py:537
  (3 other events, 7.3 us)
